TPU v7x, 32 devices: a whole 2x2x4 slice. The times are simulated.
32 devices in a mesh: gx: 8 (over z, y), gy: 4 (over x, core).
Axes of the slice: x: 2, y: 2, z: 4, core: 2. Of those that a mesh axis runs over, the one named last changes fastest.
Arguments:
- layer_in: bfloat16 [2048, 1536], P('gx', 'gy'), may hold values from -40 to 40
- first_gain: float32 [1536], P('gy'), may hold values from 0.5 to 1.5
- query_weight: bfloat16 [1536, 1536], P('gx', 'gy'), may hold values from -0.21875 to 0.21875
- key_matrix: bfloat16 [1536, 768], P('gx', 'gy'), may hold values from -0.21875 to 0.21875
- value_matrix: bfloat16 [1536, 768], P('gx', 'gy'), may hold values from -0.15625 to 0.15625
- out_weight: bfloat16 [1536, 1536], P('gy', 'gx'), may hold values from -0.875 to 0.875
- second_gain: float32 [1536], P('gy'), may hold values from 0.5 to 1.5
- gate_weight: bfloat16 [1536, 4096], P('gx', 'gy'), may hold values from -0.15625 to 0.15625
- up_weight: bfloat16 [1536, 4096], P('gx', 'gy'), may hold values from -0.15625 to 0.15625
- down_weight: bfloat16 [4096, 1536], P('gy', 'gx'), may hold values from -0.1875 to 0.1875
- out_grad: bfloat16 [2048, 1536], P('gx', 'gy'), may hold values from -6 to 6
Outputs:
- layer_out: bfloat16 [2048, 1536], P('gx', 'gy')
- in_grad: float32 [2048, 1536], P('gx', 'gy')
- first_gain_grad: float32 [1536], P('gy')
- query_grad: float32 [1536, 1536], P('gx', 'gy')
- key_grad: float32 [1536, 768], P('gx', 'gy')
- value_grad: float32 [1536, 768], P('gx', 'gy')
- out_proj_grad: float32 [1536, 1536], P('gy', 'gx')
- second_gain_grad: float32 [1536], P('gy')
- gate_grad: float32 [1536, 4096], P('gx', 'gy')
- up_grad: float32 [1536, 4096], P('gx', 'gy')
- down_grad: float32 [4096, 1536], P('gy', 'gx')
All inputs are finite; a program needn't handle non-finite values.
Results may differ from a plain program's by a relative error of at most 0.024.
Values may be sent and summed in bfloat16 or wider, within the bound.
No kernel may reach another device: no remote copies, remote signals or barrier semaphores. Data moves between devices by JAX's collectives and lax.ppermute only.
A program may use at most 128 MiB of HBM per device.

v0:
```python
import jax
import jax.numpy as jnp
from jax import lax
from jax.experimental import pallas as pl
from jax.experimental.pallas import tpu as pltpu
from jax.sharding import PartitionSpec as P

HEAD_DIM = 96
PROMPT_DEV = 4
CONT_DEV = 4
GROUP = (PROMPT_DEV + CONT_DEV) // 2
PROMPTS = PROMPT_DEV // 2

eps = 1e-05
neg_big = -1e30
rope_base = 100000.0
score_scale = HEAD_DIM ** (-0.5)
f32 = jnp.float32
bf16 = jnp.bfloat16


def dims(left, right, left_axis, right_axis):
    return lax.dot_general(
        left, right, (((left_axis,), (right_axis,)), ((), ())), preferred_element_type=f32
    )


class Place:
    def __init__(self):
        self.nx = lax.axis_size("gx")
        self.ny = lax.axis_size("gy")
        assert self.ny == 4 and self.nx % (PROMPT_DEV + CONT_DEV) == 0
        self.n = self.nx // 2
        self.gx = lax.axis_index("gx")
        self.gy = lax.axis_index("gy")
        self.z, self.y = self.gx // 2, self.gx % 2
        self.x, self.c = self.gy // 2, self.gy % 2
        self.z_in = self.z % GROUP
        offset = 2 * self.z_in + jnp.arange(2, dtype=jnp.int32)
        self.offset = offset
        self.lined = self.n == self.ny
        blocks = jnp.arange(self.ny, dtype=jnp.int32)
        first = jnp.stack([self.z, self.y, self.x, self.c, self.z_in]).astype(jnp.int32)
        self.table = jnp.concatenate(
            [first, jnp.minimum(offset, PROMPT_DEV), blocks ^ self.z if self.lined else blocks]
        )

    def swap_gx(self, value, bit):
        return lax.ppermute(value, "gx", [(i, i ^ bit) for i in range(self.nx)])

    def swap_y(self, value):
        return self.swap_gx(value, 1)

    def swap_x(self, value):
        return lax.ppermute(value, "gy", [(i, i ^ 2) for i in range(self.ny)])

    def swap_c(self, value):
        return lax.ppermute(value, "gy", [(i, i ^ 1) for i in range(self.ny)])

    def send_z(self, value, moves):
        pairs = [(2 * s + y, 2 * t + y) for s, t in moves for y in range(2)]
        return lax.ppermute(value, "gx", pairs)

    def by_y(self):
        return [[2 * z + y for z in range(self.n)] for y in range(2)]


def pair(flag, mine, other):
    return jnp.where(flag == 0, mine, other), jnp.where(flag == 0, other, mine)


def part_of(flag, whole, axis):
    low, high = jnp.split(whole, 2, axis)
    return jnp.where(flag == 0, low, high), jnp.where(flag == 0, high, low)


def after(value, *earlier):
    return lax.optimization_barrier((value,) + earlier)[0]


NEAR = [(0, 1), (1, 0), (2, 3), (3, 2)]
SECOND = [(0, 2), (1, 3), (2, 0), (3, 1)]
MIDDLE = [(1, 2), (2, 1)]
INWARD = [(0, 1), (3, 2)]
OUTWARD = [(1, 0), (2, 3)]


def gather_pieces(place, piece, late_middle=False):
    second = place.send_z(piece, SECOND)
    near = place.send_z(piece, NEAR)
    middle = place.send_z(after(piece, second) if late_middle else piece, MIDDLE)
    return [piece, near, second, middle, place.send_z(second, OUTWARD)]


def gather_whole(place, piece):
    every = lax.all_gather(piece, "gx", axis_index_groups=place.by_y())
    inner = place.n // place.ny
    if inner == 1:
        return every
    rows, cols = piece.shape
    every = every.reshape(place.ny, inner, rows, cols)
    return jnp.swapaxes(every, 1, 2).reshape(place.ny, rows, inner * cols)


def scatter_whole(place, parts):
    inner = place.n // place.ny
    if inner > 1:
        count, rows, cols = parts.shape
        parts = jnp.swapaxes(parts.reshape(count, rows, inner, cols // inner), 1, 2)
        parts = parts.reshape(place.n, rows, cols // inner)
    return lax.psum_scatter(parts, "gx", axis_index_groups=place.by_y())


def start_scatter(place, parts):
    if not place.lined:
        return [scatter_whole(place, jnp.stack(parts))]
    own, near, second, third = parts
    far = place.send_z(third, INWARD)
    middle = place.send_z(third, MIDDLE)
    return [own, second, far, place.send_z(near, NEAR), middle]


def second_scatter(place, started, *earlier):
    if not place.lined:
        return None
    second = after(started[1], *earlier)
    return place.send_z((second.astype(f32) + started[2].astype(f32)).astype(bf16), SECOND)


def end_scatter(place, started, second, *earlier):
    if not place.lined:
        return started[0].astype(f32)
    own, near, middle = after(started[0], *earlier), started[3], started[4]
    return own.astype(f32) + near.astype(f32) + middle.astype(f32) + second.astype(f32)


def reduce_core(place, keep, sends):
    return [keep[i] + place.swap_c(send).astype(f32) for i, send in enumerate(sends)]


def all_sum(place, keep, sends, before_first=(), before_second=()):
    first, second = reduce_core(place, keep, sends)
    low = (first.astype(bf16), second.astype(bf16))
    low = lax.optimization_barrier(low + tuple(before_first))
    first, second = (
        first + place.swap_x(low[0]).astype(f32),
        second + place.swap_y(low[1]).astype(f32),
    )
    low = (first.astype(bf16), second.astype(bf16))
    low = lax.optimization_barrier(low + tuple(before_second))
    own = [
        (first + place.swap_y(low[0]).astype(f32)).astype(bf16),
        (second + place.swap_x(low[1]).astype(f32)).astype(bf16),
    ]
    return own + [place.swap_c(part) for part in own]


def own_sum(place, keep, sends):
    first, second = reduce_core(place, keep, sends)
    mine, other = jnp.where(place.x == 0, first, second), jnp.where(place.x == 0, second, first)
    mine = mine + place.swap_x(other.astype(bf16)).astype(f32)
    mine, other = part_of(place.y, mine, 0)
    return mine + place.swap_y(other.astype(bf16)).astype(f32)


def own_block(place, blocks):
    rows = blocks.shape[1] // 2
    return lax.dynamic_slice(
        blocks, (place.gy, place.y * rows, 0), (1, rows, blocks.shape[2])
    )[0]


Z, Y, X, C, Z_IN, COUNT = range(6)
ORDER = COUNT + 2


def call(body, outs, table, operands, pieces=(), scratch=(), earlier=(), limit=24):
    lengths = [len(p) for p in pieces]
    flat = [a for p in pieces for a in p] + list(earlier)
    vmem = pl.BlockSpec(memory_space=pltpu.VMEM)

    def kernel(table_ref, *refs):
        plain, rest = refs[: len(operands)], refs[len(operands) :]
        lists = []
        for length in lengths:
            lists.append(rest[:length])
            rest = rest[length:]
        rest = rest[len(earlier) :]
        body(table_ref, *plain, *lists, *rest)

    return pl.pallas_call(
        kernel,
        out_shape=[jax.ShapeDtypeStruct(shape, dtype) for shape, dtype in outs],
        in_specs=[pl.BlockSpec(memory_space=pltpu.SMEM)]
        + [vmem] * len(operands)
        + [pl.BlockSpec(memory_space=pl.ANY)] * len(flat),
        out_specs=[vmem] * len(outs),
        scratch_shapes=list(scratch),
        compiler_params=pltpu.CompilerParams(vmem_limit_bytes=limit << 20),
    )(table, *operands, *flat)


def start_pieces(table, pieces, whole, sems, rows=slice(None)):
    count = whole.shape[0]
    block = [table[ORDER + k] for k in range(count)]

    def copy(piece, k):
        source = piece.at[rows] if rows != slice(None) else piece
        return pltpu.make_async_copy(source, whole.at[block[k]], sems.at[k])

    def wait(k):
        pltpu.make_async_copy(whole.at[0], whole.at[0], sems.at[k]).wait()

    if len(pieces) == 1:
        for k in range(count):
            copy(pieces[0].at[block[k]], k).start()
        return wait
    z = table[Z]
    own, near, second, middle, end = pieces
    for k, piece in enumerate((own, near, second)):
        copy(piece, k).start()
    inside = jnp.logical_or(z == 1, z == 2)

    @pl.when(inside)
    def _():
        copy(middle, 3).start()

    @pl.when(jnp.logical_not(inside))
    def _():
        copy(end, 3).start()

    return wait


def keep_and_send(table, block_of, keep, sends):
    core = table[C]
    for i, send in enumerate(sends):
        keep[i] = block_of(2 * i + core)
        send[...] = block_of(2 * i + 1 - core).astype(bf16)


def place_rows(table, pieces, whole):
    x, y, c = table[X], table[Y], table[C]
    tokens = whole.shape[1] // 2
    for dc in range(2):
        for dx in range(2):
            block = 2 * (x + dx - 2 * x * dx) + c + dc - 2 * c * dc
            for dy in range(2):
                at = pl.ds(pl.multiple_of(tokens * (y + dy - 2 * y * dy), tokens), tokens)
                array, start = pieces[4 * dc + 2 * dy + dx]
                whole[block, at, :] = array[start : start + tokens]


def stacked_pieces(near, far, stride, start=0):
    return [(a, start + i * stride) for a in (near, far) for i in range(4)]


def norm_rows(raw, gain, normed):
    def square(b, total):
        values = raw[b].astype(f32)
        return total + jnp.sum(values * values, axis=1, keepdims=True)

    count = raw.shape[0]
    total = lax.fori_loop(0, count, square, jnp.zeros((raw.shape[1], 1), f32))
    scale = lax.rsqrt(total / (count * raw.shape[2]) + eps)

    def norm(b, _):
        normed[b] = (raw[b].astype(f32) * scale * gain[b]).astype(bf16)
        return 0

    lax.fori_loop(0, count, norm, 0)
    return scale


def rows_body(table, near, far, *refs):
    gains = refs[:4]
    raw, grad, normed, inverse, gain_first, gain_second = refs[4:]
    tokens = raw.shape[1]
    place_rows(table, stacked_pieces(near, far, tokens), raw)
    place_rows(table, stacked_pieces(near, far, tokens, tokens // 2), grad)
    x, c = table[X], table[C]
    for dc in range(2):
        for dx in range(2):
            block = 2 * (x + dx - 2 * x * dx) + c + dc - 2 * c * dc
            gain = gains[2 * dc + dx][...]
            gain_first[block] = gain[0:1]
            gain_second[block] = gain[1:2]
    inverse[...] = norm_rows(raw, gain_first, normed)


def prompt_body(table, near, far, gain, normed, slot):
    tokens = slot.shape[1]
    for i in range(PROMPTS):
        at = 4 * i * (tokens // 2)
        place_rows(table, stacked_pieces(near, far, tokens // 2, at), slot)
        norm_rows(slot, gain, normed.at[:, i * tokens : (i + 1) * tokens])


def turn(values, cosine, sine):
    half = values.shape[0] // 2
    first, second = values[:half], values[half:]
    return jnp.concatenate(
        [first * cosine - second * sine, second * cosine + first * sine], axis=0
    )


def qkv_body(
    table,
    normed,
    prompt,
    cosine,
    sine,
    far_cosine,
    far_sine,
    pieces,
    query,
    own,
    far,
    weights,
    acc,
    far_acc,
    sems,
):
    wait = start_pieces(table, pieces, weights, sems)
    count = acc.shape[0]
    far_count = far.shape[0]
    for k in range(weights.shape[0]):
        wait(k)
    acc[...] = jnp.zeros_like(acc)
    far_acc[...] = jnp.zeros_like(far_acc)

    def one(b, _):
        acc[...] += dims(weights[b, :count], normed[b], 1, 1)
        far_acc[...] += dims(weights[b, count - far_count : count], prompt[b], 1, 1)
        return 0

    lax.fori_loop(0, normed.shape[0], one, 0)
    head = HEAD_DIM
    heads = query.shape[0] // head
    cos, sin = cosine[...], sine[...]
    for h in range(heads):
        at = slice(h * head, (h + 1) * head)
        query[at] = turn(acc[at], cos, sin).astype(bf16)
    at = slice(heads * head, (heads + 1) * head)
    own[:head] = turn(acc[at], cos, sin).astype(bf16)
    own[head:] = acc[(heads + 1) * head :].astype(bf16)
    far[:head] = turn(far_acc[:head], far_cosine[...], far_sine[...]).astype(bf16)
    far[head:] = far_acc[head:].astype(bf16)


def attend_body(
    table,
    query,
    own,
    far,
    weights,
    attended,
    attended_low,
    log_total,
    keep,
    first_send,
    second_send,
):
    tokens = own.shape[1]
    head = HEAD_DIM
    block = tokens // 2
    key_far, value_far = far[:head].T, far[head:]
    key_own = own[:head].T
    total = far.shape[1]
    near_row = lax.broadcasted_iota(jnp.int32, (block, block), 0)
    near_col = lax.broadcasted_iota(jnp.int32, (block, block), 1)
    causal = near_row <= near_col
    row = lax.broadcasted_iota(jnp.int32, (total, block), 0)
    for part in range(2):
        cols = slice(part * block, (part + 1) * block)
        key_near, value_near = key_own[cols], own[head:, cols]
        seen = row < table[COUNT + part] * block

        def one(h, _):
            at = pl.ds(pl.multiple_of(h * head, head), head)
            rows = query[at, cols]
            score_far = jnp.where(seen, dims(key_far, rows, 1, 0) * score_scale, neg_big)
            score_near = jnp.where(causal, dims(key_near, rows, 1, 0) * score_scale, neg_big)
            top = jnp.maximum(
                jnp.max(score_far, axis=0, keepdims=True), jnp.max(score_near, axis=0, keepdims=True)
            )
            weight_far = jnp.exp(score_far - top)
            weight_near = jnp.exp(score_near - top)
            weight = jnp.sum(weight_far, axis=0, keepdims=True) + jnp.sum(
                weight_near, axis=0, keepdims=True
            )
            out = dims(value_far, weight_far.astype(bf16), 1, 0) + dims(
                value_near, weight_near.astype(bf16), 1, 0
            )
            attended[at, cols] = out / weight
            log_total[h, :, cols] = top + jnp.log(weight)
            return 0

        lax.fori_loop(0, query.shape[0] // head, one, 0)
    values = attended[...]
    attended_low[...] = values.astype(bf16)
    flipped = values.T.astype(bf16)
    first = weights.shape[1] - query.shape[0]
    keep_and_send(
        table,
        lambda b: dims(flipped, weights[b, first:], 1, 0),
        keep,
        (first_send, second_send),
    )


def hidden_body(
    table, raw, own_first, own_second, other_first, other_second, gain, hidden, normed, inverse
):
    core = table[C]
    summed, other = (own_first, own_second), (other_first, other_second)
    for i in range(2):
        b = 2 * i + core
        hidden[b] = raw[b].astype(f32) + summed[i][...].astype(f32)
        b = 2 * i + 1 - core
        hidden[b] = raw[b].astype(f32) + other[i][...].astype(f32)

    def square(b, total):
        values = hidden[b]
        return total + jnp.sum(values * values, axis=1, keepdims=True)

    count = raw.shape[0]
    total = lax.fori_loop(0, count, square, jnp.zeros((raw.shape[1], 1), f32))
    scale = lax.rsqrt(total / (count * raw.shape[2]) + eps)
    inverse[...] = scale

    def norm(b, _):
        normed[b] = (hidden[b] * scale * gain[b]).astype(bf16)
        return 0

    lax.fori_loop(0, count, norm, 0)


def forward_body(
    table,
    normed,
    grad,
    pieces,
    active,
    change,
    keep,
    first_send,
    second_send,
    weights,
    acc,
    gate_slope,
    up_slope,
    sems,
):
    wait = start_pieces(table, pieces, weights, sems)
    count, tokens = normed.shape[:2]
    width = acc.shape[1]
    half = width // 2
    acc[...] = jnp.zeros_like(acc)

    def one(k, _):
        b = table[ORDER + k]
        wait(k)
        acc[...] += dims(normed[b], weights[b, :width], 1, 1)
        return 0

    lax.fori_loop(0, count, one, 0)
    rows = tokens // 4

    def part(i, _):
        at = pl.ds(pl.multiple_of(i * rows, rows), rows)
        gate, up = acc[at, :half], acc[at, half:]
        sigmoid = jax.nn.sigmoid(gate)
        active[at] = (gate * sigmoid * up).astype(bf16)
        gate_slope[at] = up * sigmoid * (1.0 + gate * (1.0 - sigmoid))
        up_slope[at] = gate * sigmoid
        return 0

    lax.fori_loop(0, 4, part, 0)

    def back(b, total):
        return total + dims(grad[b], weights[b, width:], 1, 1)

    slope = lax.fori_loop(0, count, back, jnp.zeros((tokens, half), f32))
    change[:, :half] = (slope * gate_slope[...]).astype(bf16)
    change[:, half:] = (slope * up_slope[...]).astype(bf16)
    values = change[...]
    keep_and_send(
        table,
        lambda b: dims(values, weights[b, :width], 1, 0),
        keep,
        (first_send, second_send),
    )


def forward_parts_body(table, active, grad, normed, change, *refs):
    parts, flipped = refs[:-1], refs[-1]
    width = change.shape[1]
    flipped[:width] = change[...].T
    flipped[width:] = active[...].T
    rows = width // 4

    def fill(first, count, source):
        def one(i, _):
            at = pl.ds(pl.multiple_of((first + i) * rows, rows), rows)
            for k, part in enumerate(parts):
                part[at] = dims(flipped[at], source[table[ORDER + k]], 1, 0).astype(bf16)
            return 0

        lax.fori_loop(0, count, one, 0)

    fill(0, 4, normed)
    fill(4, flipped.shape[0] // rows - 4, grad)


def down_body(table, active, pieces, keep, first_send, second_send, weights, sems):
    rows = weights.shape[1]
    wait = start_pieces(table, pieces, weights, sems, slice(2 * rows, 3 * rows))
    for k in range(weights.shape[0]):
        wait(k)
    values = active[...]
    keep_and_send(
        table, lambda b: dims(values, weights[b], 1, 0), keep, (first_send, second_send)
    )


def attend_back_body(
    table,
    hidden,
    inverse,
    own_first,
    own_second,
    other_first,
    other_second,
    grad,
    gain,
    weights,
    query,
    own,
    far,
    attended,
    log_total,
    cosine,
    sine,
    far_cosine,
    far_sine,
    through,
    pull,
    query_low,
    own_low,
    far_low,
    own_back,
    *rest,
):
    sends, inner_first = rest[: GROUP - 1], rest[GROUP - 1]
    far_back, change, branch = rest[GROUP:]
    core = table[C]
    count, tokens, model = hidden.shape
    for i, (mine, theirs) in enumerate(((own_first, other_first), (own_second, other_second))):
        change[2 * i + core] = mine[...].astype(f32) * gain[2 * i + core]
        change[2 * i + 1 - core] = theirs[...].astype(f32) * gain[2 * i + 1 - core]

    def product(b, total):
        return total + jnp.sum(change[b] * hidden[b], axis=1, keepdims=True)

    inner = lax.fori_loop(0, count, product, jnp.zeros((tokens, 1), f32))
    scale = inverse[...]
    back = scale * scale * scale * inner / (count * model)
    pull[...] = back

    def rows(b, total):
        values = grad[b].astype(f32) + scale * change[b] - hidden[b] * back
        low = values.astype(bf16)
        through[b] = low
        return total + dims(low, weights[b, first:], 1, 1)

    heads_cols = query.shape[0]
    first = weights.shape[1] - heads_cols
    total_rows = lax.fori_loop(0, count, rows, jnp.zeros((tokens, heads_cols), f32))
    branch[...] = total_rows.T.astype(bf16)

    head = HEAD_DIM
    block = tokens // 2
    key_far_t = far[:head]
    key_far, value_far = key_far_t.T, far[head:].T
    key_own, value_own = own[:head].T, own[head:].T
    total = far.shape[1]
    near_row = lax.broadcasted_iota(jnp.int32, (block, block), 0)
    near_col = lax.broadcasted_iota(jnp.int32, (block, block), 1)
    causal = near_row <= near_col
    row = lax.broadcasted_iota(jnp.int32, (total, block), 0)
    far_back[...] = jnp.zeros_like(far_back)
    own_back[...] = jnp.zeros_like(own_back)
    inner_first[...] = jnp.zeros_like(inner_first)
    for part in range(2):
        cols = slice(part * block, (part + 1) * block)
        key_near, value_near = key_own[cols], value_own[cols]
        key_near_t = own[:head, cols]
        seen = row < table[COUNT + part] * block

        def one_head(h, _):
            at = pl.ds(pl.multiple_of(h * head, head), head)
            rows_q, rows_grad = query[at, cols], branch[at, cols]
            delta = jnp.sum(
                rows_grad.astype(f32) * attended[at, cols], axis=0, keepdims=True
            )
            logs = log_total[h, :, cols]

            def one(key, value, allowed):
                score = dims(key, rows_q, 1, 0) * score_scale
                prob = jnp.where(allowed, jnp.exp(score - logs), 0.0)
                moved = (prob * (dims(value, rows_grad, 1, 0) - delta)).astype(bf16)
                return prob.astype(bf16), moved

            prob_far, moved_far = one(key_far, value_far, seen)
            prob_near, moved_near = one(key_near, value_near, causal)
            query_back = (
                dims(key_far_t, moved_far, 1, 0) + dims(key_near_t, moved_near, 1, 0)
            ) * score_scale
            inner_first[:, cols] += jnp.sum(
                query_back * rows_q.astype(f32), axis=0, keepdims=True
            )
            query_low[at, cols] = turn(query_back, cosine[:, cols], -sine[:, cols]).astype(bf16)
            far_back[:head] += dims(rows_q, moved_far, 1, 1) * score_scale
            far_back[head:] += dims(rows_grad, prob_far, 1, 1)
            own_back[:head, cols] += dims(rows_q, moved_near, 1, 1) * score_scale
            own_back[head:, cols] += dims(rows_grad, prob_near, 1, 1)
            return 0

        lax.fori_loop(0, heads_cols // head, one_head, 0)
    own_low[:head] = turn(own_back[:head], cosine[...], -sine[...]).astype(bf16)
    own_low[head:] = own_back[head:].astype(bf16)
    far_low[:head] = turn(far_back[:head], far_cosine[...], -far_sine[...]).astype(bf16)
    far_low[head:] = far_back[head:].astype(bf16)
    for slot in range(PROMPTS):

        @pl.when(table[Z_IN] == slot)
        def _():
            own_back[...] += far_back[:, slot * tokens : (slot + 1) * tokens]

    for k in range(1, GROUP):
        sends[k - 1][...] = far_back[:, :tokens].astype(bf16)
        for slot in range(1, PROMPTS):

            @pl.when(table[Z_IN] == slot + k)
            def _():
                sends[k - 1][...] = far_back[:, slot * tokens : (slot + 1) * tokens].astype(bf16)


def attend_parts_body(
    table, query_low, own_low, far_low, normed, prompt, attended_low, through, *parts
):
    first = query_low.shape[0]
    second = first + own_low.shape[0]
    for k, part in enumerate(parts):
        b = table[ORDER + k]
        part[:first] = dims(query_low[...], normed[b], 1, 0).astype(bf16)
        part[first:second] = (
            dims(own_low[...], normed[b], 1, 0) + dims(far_low[...], prompt[b], 1, 0)
        ).astype(bf16)
        part[second:] = dims(attended_low[...], through[b], 1, 0).astype(bf16)


def qkv_back_body(table, own_back, *refs):
    moved, refs = refs[: GROUP - 1], refs[GROUP - 1 :]
    query_low, weights, cosine, sine, own, inner = refs[:6]
    keep, first_send, second_send, inner_first = refs[6:]
    head = HEAD_DIM
    total = own_back[...]
    for part in moved:
        total = total + part[...].astype(f32)
    inner_first[...] = inner[...] + jnp.sum(total * own[...].astype(f32), axis=0, keepdims=True)
    key = turn(total[:head], cosine[...], -sine[...])
    low = jnp.concatenate([key, total[head:]], axis=0)
    flipped = jnp.concatenate([query_low[...].T, low.T.astype(bf16)], axis=1)
    width = flipped.shape[1]
    keep_and_send(
        table,
        lambda b: dims(flipped, weights[b, :width], 1, 0),
        keep,
        (first_send, second_send),
    )


def halves_of(table, whole):
    half = whole.shape[0] // 2
    low, high = whole[:half], whole[half:]
    flag = table[Y] == 0
    return jnp.where(flag, low, high), jnp.where(flag, high, low)


def split_body(table, *refs):
    count = len(refs) - 2
    mine_ref, other_ref = refs[-2:]
    at = 0
    for i, ref in enumerate(refs[:count]):
        whole = ref[...]
        if i < count - 1:
            whole = whole.T
        mine, other = halves_of(table, whole)
        rows = mine.shape[0]
        mine_ref[at : at + rows] = mine
        other_ref[at : at + rows] = other
        at += rows


def join_body(table, mine, got, *outs):
    flag = table[Y] == 0
    at = 0
    for i, out in enumerate(outs):
        turned = i < len(outs) - 1
        rows = out.shape[1 if turned else 0] // 2
        parts = mine[at : at + rows].astype(f32), got[at : at + rows].astype(f32)
        at += rows
        low, high = jnp.where(flag, parts[0], parts[1]), jnp.where(flag, parts[1], parts[0])
        if turned:
            out[:, :rows] = low.T
            out[:, rows:] = high.T
        else:
            out[:rows] = low
            out[rows:] = high


def rope_tables(positions, half):
    freq = rope_base ** (-(2.0 * jnp.arange(half, dtype=f32)) / (2.0 * half))
    angle = freq[:, None] * positions.astype(f32)[None, :]
    return (jnp.cos(angle), jnp.sin(angle))


def shards(
    layer_in,
    first_gain,
    query_weight,
    key_matrix,
    value_matrix,
    out_weight,
    second_gain,
    gate_weight,
    up_weight,
    down_weight,
    out_grad,
):
    place = Place()
    n, ny, y, z_in, table = place.n, place.ny, place.y, place.z_in, place.table
    lined = place.lined
    block, width = layer_in.shape
    tokens = 2 * block
    model_width = width * ny
    hidden_dev = gate_weight.shape[1] // 2
    query_rows = query_weight.shape[1] // 2
    kv_rows = key_matrix.shape[1]
    qkv_cols = query_rows + kv_rows
    full = (ny, tokens, width)
    wide = [((2,) + full[1:], f32), (full[1:], bf16), (full[1:], bf16)]

    def halves(*matrices):
        rows = sum(max(m.shape) for m in matrices) // 2
        cols = min(matrices[0].shape)
        return call(split_body, [((rows, cols), bf16)] * 2, table, matrices)

    def whole_piece(mine, got):
        return jnp.concatenate(pair(y, mine, got), axis=1)

    mine, other = halves(query_weight, key_matrix, value_matrix, out_weight)
    early_in = after(layer_in, other)
    attend_got = place.swap_y(other)
    attend_piece = whole_piece(mine, attend_got)
    mine, other = halves(gate_weight, up_weight, down_weight)
    forward_piece = whole_piece(mine, place.swap_y(after(other, attend_got)))
    if lined:
        attend_pieces = gather_pieces(place, attend_piece)
        forward_pieces = gather_pieces(place, after(forward_piece, *attend_pieces[1:]), True)
    else:
        attend_pieces = [gather_whole(place, attend_piece)]
        forward_pieces = [gather_whole(place, forward_piece)]
    attend_shape = (ny, qkv_cols + query_rows, width)
    forward_shape = (ny, 3 * hidden_dev, width)
    sems = pltpu.SemaphoreType.DMA((ny,))

    def over_cores(four):
        near = jnp.concatenate(four, axis=0)
        return [near, place.swap_c(near)]

    def spread(value):
        by_x = place.swap_x(value)
        return over_cores([value, by_x, place.swap_y(value), place.swap_y(by_x)])

    gains = jnp.stack([first_gain, second_gain])
    two = [gains, place.swap_x(gains)]
    gains = two + [place.swap_c(g) for g in two]
    raw, grad, normed_in, inverse_in, gain_in, gain_mid = call(
        rows_body,
        [(full, bf16)] * 3 + [((tokens, 1), f32)] + [((ny, 1, width), f32)] * 2,
        table,
        spread(after(jnp.concatenate([layer_in, out_grad], axis=0), attend_got)) + gains,
    )

    attend_hop = attend_pieces[len(attend_pieces) // 2]
    moved = [
        place.send_z(
            early_in,
            [(s, s + k) for s in range(n) if s % GROUP < PROMPTS and s % GROUP + k < GROUP],
        )
        for k in range(1, GROUP)
    ]
    slots = [layer_in] * PROMPTS
    for i in range(PROMPTS):
        for k in range(1, GROUP):
            slots[i] = jnp.where(z_in == i + k, moved[k - 1], slots[i])
    pieces = []
    for i, slot in enumerate(slots):
        slot = after(slot, attend_got)
        if i % 2 == 0:
            by_x = place.swap_x(slot)
            late, late_x = lax.optimization_barrier((slot, by_x, attend_hop))[:2]
            pieces += [slot, by_x, place.swap_y(late), place.swap_y(late_x)]
        else:
            by_y = place.swap_y(slot)
            late, late_y = lax.optimization_barrier((slot, by_y, attend_hop))[:2]
            pieces += [slot, place.swap_x(late), by_y, place.swap_x(late_y)]
    (prompt,) = call(
        prompt_body,
        [((ny, PROMPTS * tokens, width), bf16)],
        table,
        over_cores(pieces) + [gain_in],
        scratch=[pltpu.VMEM(full, bf16)],
    )

    within = jnp.arange(block, dtype=jnp.int32)
    positions = jnp.minimum(place.offset, PROMPT_DEV)[:, None] * block + within[None, :]
    cosine, sine = rope_tables(positions.reshape(-1), HEAD_DIM // 2)
    far_cosine, far_sine = rope_tables(
        jnp.arange(PROMPTS * tokens, dtype=jnp.int32), HEAD_DIM // 2
    )
    tables = [cosine, sine, far_cosine, far_sine]
    query, own, far, attend_weights = call(
        qkv_body,
        [
            ((query_rows, tokens), bf16),
            ((kv_rows, tokens), bf16),
            ((kv_rows, PROMPTS * tokens), bf16),
            (attend_shape, bf16),
        ],
        table,
        [normed_in, prompt] + tables,
        [attend_pieces],
        [
            pltpu.VMEM((qkv_cols, tokens), f32),
            pltpu.VMEM((kv_rows, PROMPTS * tokens), f32),
            sems,
        ],
    )
    attended, attended_low, log_total, keep, *sends = call(
        attend_body,
        [
            ((query_rows, tokens), f32),
            ((query_rows, tokens), bf16),
            ((query_rows // HEAD_DIM, 1, tokens), f32),
        ]
        + wide,
        table,
        [query, own, far, attend_weights],
    )
    summed = all_sum(place, keep, sends, [forward_pieces[len(forward_pieces) // 2]])

    hidden, normed_mid, inverse_mid = call(
        hidden_body,
        [(full, f32), (full, bf16), ((tokens, 1), f32)],
        table,
        [raw] + summed + [gain_mid],
    )
    active, change, keep, *sends = call(
        forward_body,
        [((tokens, hidden_dev), bf16), ((tokens, 2 * hidden_dev), bf16)] + wide,
        table,
        [normed_mid, grad],
        [forward_pieces],
        [pltpu.VMEM(forward_shape, bf16), pltpu.VMEM((tokens, 2 * hidden_dev), f32)]
        + [pltpu.VMEM((tokens, hidden_dev), f32)] * 2
        + [sems],
    )
    forward_parts = call(
        forward_parts_body,
        [(forward_shape[1:], bf16)] * ny,
        table,
        [active, grad, normed_mid, change],
        scratch=[pltpu.VMEM(forward_shape[1:2] + (tokens,), bf16)],
    )
    forward_started = start_scatter(place, forward_parts)
    summed = all_sum(place, keep, sends, before_second=forward_parts[:1])
    forward_second = second_scatter(place, forward_started, summed[-1])
    hidden_own = own_block(place, hidden)
    through, pull, query_low, own_low, far_low, own_back, *returns, inner_first = call(
        attend_back_body,
        [
            (full, bf16),
            ((tokens, 1), f32),
            ((query_rows, tokens), bf16),
            ((kv_rows, tokens), bf16),
            ((kv_rows, PROMPTS * tokens), bf16),
            ((kv_rows, tokens), f32),
        ]
        + [((kv_rows, tokens), bf16)] * (GROUP - 1)
        + [((1, tokens), f32)],
        table,
        [hidden, inverse_mid]
        + summed
        + [
            grad,
            gain_mid,
            attend_weights,
            query,
            own,
            far,
            attended,
            log_total,
        ]
        + tables,
        earlier=forward_started[2:3] + forward_started[4:],
        scratch=[
            pltpu.VMEM((kv_rows, PROMPTS * tokens), f32),
            pltpu.VMEM(full, f32),
            pltpu.VMEM((query_rows, tokens), bf16),
        ],
    )
    keep, *sends = call(
        down_body,
        wide,
        table,
        [active],
        [forward_pieces],
        [pltpu.VMEM((ny, hidden_dev, width), bf16), sems],
        earlier=[through],
    )
    layer_out = (hidden_own + own_sum(place, keep, sends)).astype(bf16)
    inverse_own, _ = part_of(y, inverse_mid, 0)
    pull_own, _ = part_of(y, pull, 0)
    mid_own = jnp.where(place.x == 0, summed[0], summed[1])
    mid_own = part_of(y, mid_own, 0)[0].astype(f32)
    through_own = (
        out_grad.astype(f32)
        + inverse_own * mid_own * second_gain[None, :]
        - hidden_own * pull_own
    )
    second_term = jnp.sum(mid_own * hidden_own * inverse_own, axis=0)

    moved = [
        place.send_z(
            returns[k - 1],
            [(s, s - k) for s in range(n) if 0 <= s % GROUP - k < PROMPTS],
        )
        for k in range(1, GROUP)
    ]
    attend_parts = call(
        attend_parts_body,
        [(attend_shape[1:], bf16)] * ny,
        table,
        [query_low, own_low, far_low, normed_in, prompt, attended_low, through],
    )
    keep, *sends, inner = call(
        qkv_back_body,
        wide + [((1, tokens), f32)],
        table,
        [own_back] + moved + [query_low, attend_weights, cosine, sine, own, inner_first],
        earlier=forward_started[3:4] + ([forward_second] if lined else []),
    )
    attend_started = start_scatter(place, attend_parts)
    if lined:
        attend_second = second_scatter(place, attend_started, forward_second)
    else:
        attend_second = None
    forward_grad = end_scatter(place, forward_started, forward_second, sends[-1])
    attend_grad = end_scatter(place, attend_started, attend_second, sends[-1])
    inner = inner + place.swap_c(inner)
    inner = inner + place.swap_x(inner)
    inner = inner + place.swap_y(inner)
    first_own = own_sum(place, keep, sends)
    input_own = layer_in.astype(f32)
    inverse_own, _ = part_of(y, inverse_in, 0)
    scaled = first_own * first_gain[None, :]
    inner = part_of(y, inner.reshape(tokens, 1), 0)[0]
    in_grad = (
        through_own + inverse_own * scaled - input_own * (inverse_own**2 * inner / model_width)
    )
    first_term = jnp.sum(first_own * input_own * inverse_own, axis=0)
    terms = jnp.stack([first_term, second_term])
    bit = 1
    while bit < place.nx:
        terms = terms + place.swap_gx(terms, bit)
        bit *= 2

    def joined(summed_part, outs):
        mine, other = part_of(y, summed_part, 1)
        got = place.swap_y(other.astype(bf16))
        return call(
            join_body,
            [(m.shape, f32) for m in outs],
            table,
            [mine, got],
        )

    gate_grad, up_grad, down_grad = joined(forward_grad, (gate_weight, up_weight, down_weight))
    query_out, key_out, value_out, out_out = joined(
        attend_grad, (query_weight, key_matrix, value_matrix, out_weight)
    )
    return (
        layer_out,
        in_grad,
        terms[0],
        query_out,
        key_out,
        value_out,
        out_out,
        terms[1],
        gate_grad,
        up_grad,
        down_grad,
    )


def solution(mesh):
    rows, cols, gain = P("gx", "gy"), P("gy", "gx"), P("gy")
    return jax.shard_map(
        shards,
        mesh=mesh,
        in_specs=(rows, gain, rows, rows, rows, cols, gain, rows, rows, cols, rows),
        out_specs=(rows, rows, gain, rows, rows, rows, cols, gain, rows, rows, cols),
        check_vma=False,
    )
```

profile of v0, /device:TPU:0, one launch (start us, length us, event | category | flops | bytes accessed | tf_op | source)
XLA Modules:
  0.0 438.9 jit_solution(12326357200438033062)
XLA Ops:
  9.1 4.2 collective-permute-start.10
  13.2 3.4 collective-permute-start.8
  33.5 7.4 %collective-permute-done.11 = bf16[256,384]{1,0:T(8,128)(2,1)} collective-permute-done((bf16[256,384]{1,0:T(8,128)(2,1)S(1)}, bf16[256,384]{1,0:T(8,128)(2,1)}, u32[]{:S(2)}, u32[]{:S(2)}) %collective-permute-start.11) | collective-permute-done | bytes 196640 | tf_op jit(solution)/shard_map/ppermute | solution.py:55
  43.9 3.5 collective-permute-done.12.refs_8_
  51.6 6.3 %collective-permute-done.15 = bf16[256,384]{1,0:T(8,128)(2,1)S(1)} collective-permute-done((bf16[256,384]{1,0:T(8,128)(2,1)S(1)}, bf16[256,384]{1,0:T(8,128)(2,1)S(1)}, u32[]{:S(2)}, u32[]{:S(2)}) %collective-permute-start.15) | collective-permute-done | bytes 196640 | tf_op jit(solution)/shard_map/ppermute | solution.py:49
  58.4 12.1 %collective-permute-done.13 = bf16[256,384]{1,0:T(8,128)(2,1)S(1)} collective-permute-done((bf16[256,384]{1,0:T(8,128)(2,1)S(1)}, bf16[256,384]{1,0:T(8,128)(2,1)S(1)}, u32[]{:S(2)}, u32[]{:S(2)}) %collective-permute-start.13) | collective-permute-done | bytes 196640 | tf_op jit(solution)/shard_map/ppermute | solution.py:49
  72.9 3.3 collective-permute-done.17
  78.4 13.4 %collective-permute-start.19 = (bf16[576,384]{1,0:T(8,128)(2,1)}, bf16[576,384]{1,0:T(8,128)(2,1)}, u32[]{:S(2)}, u32[]{:S(2)}) collective-permute-start(bf16[576,384]{1,0:T(8,128)(2,1)} %pad_maximum_fusion.1.refs_6_), channel_id=1, source_target_pairs={{0,8},{4,12},{8,0},{12,4},{16,24},{20,28},{24,16},{28,20},{1,9},{5... | collective-permute-start | bytes 1327112 | tf_op jit(solution)/shard_map/ppermute | solution.py:62
  98.7 4.4 collective-permute-done.19.refs_7_
  104.6 7.4 %collective-permute-done.21.refs_10_ = bf16[576,384]{1,0:T(8,128)(2,1)} collective-permute-done((bf16[576,384]{1,0:T(8,128)(2,1)}, bf16[576,384]{1,0:T(8,128)(2,1)}, u32[]{:S(2)}, u32[]{:S(2)}) %collective-permute-start.21) | collective-permute-done | bytes 442400 | tf_op jit(solution)/shard_map/ppermute | solution.py:62
  119.4 4.9 %shard_map.196.refs_1_.refs_4_ = bf16[4,1024,384]{2,1,0:T(8,128)(2,1)S(1)} custom-call(s32[11]{0:T(128)S(1)} %concatenate.18.table_ref, bf16[2048,384]{1,0:T(8,128)(2,1)S(1)} %copy-done.26, bf16[2048,384]{1,0:T(8,128)(2,1)} %collective-permute-done.18.refs_1_, f32[4,1,384]{2,1,0:T(1,128)S(1)} %get-tuple-element.106.refs_2_), custom_call_target="tpu_custom_call" | custom-call | tf_op jit(solution)/shard_map/pallas_call | solution.py:191
  124.4 4.8 %shard_map.197 = (bf16[192,512]{1,0:T(8,128)(2,1)S(1)}, bf16[192,512]{1,0:T(8,128)(2,1)S(1)}, bf16[192,1024]{1,0:T(8,128)(2,1)S(1)}, bf16[4,576,384]{2,1,0:T(8,128)(2,1)S(1)}) custom-call(s32[11]{0:T(128)S(1)} %concatenate.18.table_ref, bf16[4,512,384]{2,1,0:T(8,128)(2,1)S(1)} %get-tuple-element.97.refs_0_.refs_3_, ...), custom_call_target="tpu_custom_call" | custom-call | tf_op jit(solution)/shard_map/pallas_call | solution.py:191
  129.2 5.1 %shard_map.198 = (f32[192,512]{1,0:T(8,128)S(1)}, bf16[192,512]{1,0:T(8,128)(2,1)S(1)}, f32[2,1,512]{2,1,0:T(1,128)S(1)}, f32[2,512,384]{2,1,0:T(8,128)S(1)}, bf...) custom-call(s32[11]{0:T(128)S(1)} %concatenate.18.table_ref, ...), custom_call_target="tpu_custom_call" | custom-call | tf_op jit(solution)/shard_map/pallas_call | solution.py:191
  137.0 28.6 %collective-permute-done.25.refs_4_.refs_3_ = bf16[1536,384]{1,0:T(8,128)(2,1)S(1)} collective-permute-done((bf16[1536,384]{1,0:T(8,128)(2,1)S(1)}, bf16[1536,384]{1,0:T(8,128)(2,1)S(1)}, u32[]{:S(2)}, u32[]{:S(2)}) %collective-permute-start.25) | collective-permute-done | bytes 1179680 | tf_op jit(solution)/shard_map/ppermute | solution.py:62
  170.2 4.9 %collective-permute-done.26 = bf16[512,384]{1,0:T(8,128)(2,1)S(1)} collective-permute-done((bf16[512,384]{1,0:T(8,128)(2,1)S(1)}, bf16[512,384]{1,0:T(8,128)(2,1)S(1)}, u32[]{:S(2)}, u32[]{:S(2)}) %collective-permute-start.26) | collective-permute-done | bytes 393248 | tf_op jit(solution)/shard_map/ppermute | solution.py:55
  177.8 7.4 %collective-permute-done.28 = bf16[512,384]{1,0:T(8,128)(2,1)S(1)} collective-permute-done((bf16[512,384]{1,0:T(8,128)(2,1)S(1)}, bf16[512,384]{1,0:T(8,128)(2,1)S(1)}, u32[]{:S(2)}, u32[]{:S(2)}) %collective-permute-start.28) | collective-permute-done | bytes 393248 | tf_op jit(solution)/shard_map/ppermute | solution.py:49
  191.6 4.8 %collective-permute-done.32.refs_3_.refs_2_ = bf16[1536,384]{1,0:T(8,128)(2,1)S(1)} collective-permute-done((bf16[1536,384]{1,0:T(8,128)(2,1)S(1)}, bf16[1536,384]{1,0:T(8,128)(2,1)S(1)}, u32[]{:S(2)}, u32[]{:S(2)}) %collective-permute-start.32) | collective-permute-done | bytes 1179680 | tf_op jit(solution)/shard_map/ppermute | solution.py:62
  196.5 22.4 %collective-permute-done.34.refs_6_.refs_5_ = bf16[1536,384]{1,0:T(8,128)(2,1)S(1)} collective-permute-done((bf16[1536,384]{1,0:T(8,128)(2,1)S(1)}, bf16[1536,384]{1,0:T(8,128)(2,1)S(1)}, u32[]{:S(2)}, u32[]{:S(2)}) %collective-permute-start.34) | collective-permute-done | bytes 1179680 | tf_op jit(solution)/shard_map/ppermute | solution.py:62
  218.8 9.8 %shard_map.201 = (bf16[512,512]{1,0:T(8,128)(2,1)S(1)}, bf16[512,1024]{1,0:T(8,128)(2,1)S(1)}, f32[2,512,384]{2,1,0:T(8,128)S(1)}, bf16[512,384]{1,0:T(8,128)(2,1)S(1)}, bf16[512,384]{1,0:T(8,128)(2,1)S(1)}) custom-call(s32[11]{0:T(128)S(1)} %concatenate.18.table_ref, bf16[4,512,384]{2,1,0:T(8,128)(2,1)S(1)} %get-tuple-element.124.refs_0_.refs_2_, ...), custom_call_target="tpu_custom_call" | custom-call | tf_op jit(solution)/shard_map/pallas_call | solution.py:191
  233.4 6.4 %shard_map.202 = (bf16[1536,384]{1,0:T(8,128)(2,1)S(1)}, bf16[1536,384]{1,0:T(8,128)(2,1)}, bf16[1536,384]{1,0:T(8,128)(2,1)S(1)}, bf16[1536,384]{1,0:T(8,128)(2,1)}) custom-call(s32[11]{0:T(128)S(1)} %concatenate.18.table_ref, bf16[512,512]{1,0:T(8,128)(2,1)S(1)} %get-tuple-element.127.refs_0_, bf16[4,512,384]{2,1,0:T(8,128)(2,1)S(1)} %get-tuple-element.125.refs_1_.refs_6_, ...), custom_call_target="tpu_custom_call" | custom-call | tf_op jit(solution)/shard_map/pallas_call | solution.py:191
  247.3 8.7 %collective-permute-done.39 = bf16[512,384]{1,0:T(8,128)(2,1)} collective-permute-done((bf16[512,384]{1,0:T(8,128)(2,1)}, bf16[512,384]{1,0:T(8,128)(2,1)}, u32[]{:S(2)}, u32[]{:S(2)}) %collective-permute-start.39) | collective-permute-done | bytes 393248 | tf_op jit(solution)/shard_map/ppermute | solution.py:49
  256.2 3.2 broadcast_select_fusion.2
  259.9 6.7 %collective-permute-done.43.refs_18_ = bf16[1536,384]{1,0:T(8,128)(2,1)} collective-permute-done((bf16[1536,384]{1,0:T(8,128)(2,1)}, bf16[1536,384]{1,0:T(8,128)(2,1)}, u32[]{:S(2)}, u32[]{:S(2)}) %collective-permute-start.43) | collective-permute-done | bytes 1179680 | tf_op jit(solution)/shard_map/ppermute | solution.py:62
  268.6 18.5 %shard_map.203 = (bf16[4,512,384]{2,1,0:T(8,128)(2,1)S(1)}, f32[512,1]{1,0:T(8,128)S(1)}, bf16[192,512]{1,0:T(8,128)(2,1)S(1)}, bf16[192,512]{1,0:T(8,128)(2,1)S...) custom-call(s32[11]{0:T(128)S(1)} %concatenate.18.table_ref, ...), custom_call_target="tpu_custom_call" | custom-call | tf_op jit(solution)/shard_map/pallas_call | solution.py:191
  290.5 5.6 %collective-permute-start.52 = (bf16[1536,384]{1,0:T(8,128)(2,1)}, bf16[1536,384]{1,0:T(8,128)(2,1)}, u32[]{:S(2)}, u32[]{:S(2)}) collective-permute-start(bf16[1536,384]{1,0:T(8,128)(2,1)} %get-tuple-element.153), channel_id=1, source_target_pairs={{0,8},{4,12},{8,0},{12,4},{16,24},{20,28},{24,16},{28,20},{1,9},{5... | collective-permute-start | bytes 3538952 | tf_op jit(solution)/shard_map/ppermute | solution.py:62
  304.1 4.1 collective-permute-done.47
  313.6 3.5 shard_map.206
  321.0 22.0 %collective-permute-done.52.refs_10_ = bf16[1536,384]{1,0:T(8,128)(2,1)} collective-permute-done((bf16[1536,384]{1,0:T(8,128)(2,1)}, bf16[1536,384]{1,0:T(8,128)(2,1)}, u32[]{:S(2)}, u32[]{:S(2)}) %collective-permute-start.52) | collective-permute-done | bytes 1179680 | tf_op jit(solution)/shard_map/ppermute | solution.py:62
  348.0 24.7 %collective-permute-done.50.refs_2_ = bf16[192,512]{1,0:T(8,128)(2,1)S(1)} collective-permute-done((bf16[192,512]{1,0:T(8,128)(2,1)}, bf16[192,512]{1,0:T(8,128)(2,1)S(1)}, u32[]{:S(2)}, u32[]{:S(2)}) %collective-permute-start.50) | collective-permute-done | bytes 196640 | tf_op jit(solution)/shard_map/ppermute | solution.py:62
  390.0 11.3 %collective-permute-done.60 = f32[1,512]{1,0:T(1,128)S(1)} collective-permute-done((f32[1,512]{1,0:T(1,128)S(1)}, f32[1,512]{1,0:T(1,128)S(1)}, u32[]{:S(2)}, u32[]{:S(2)}) %collective-permute-start.60) | collective-permute-done | bytes 2080 | tf_op jit(solution)/shard_map/ppermute | solution.py:49
  406.7 3.8 collective-permute-done.57
  414.6 8.5 %collective-permute-done.67 = bf16[576,384]{1,0:T(8,128)(2,1)} collective-permute-done((bf16[576,384]{1,0:T(8,128)(2,1)}, bf16[576,384]{1,0:T(8,128)(2,1)}, u32[]{:S(2)}, u32[]{:S(2)}) %collective-permute-start.67) | collective-permute-done | bytes 442400 | tf_op jit(solution)/shard_map/ppermute | solution.py:62
  (392 shorter events, 151.4 us)
Async XLA Ops:
  6.1 18.0 %collective-permute-start = (bf16[576,192]{1,0:T(8,128)(2,1)}, bf16[576,192]{1,0:T(8,128)(2,1)}, u32[]{:S(2)}, u32[]{:S(2)}) collective-permute-start(bf16[576,192]{1,0:T(8,128)(2,1)} %get-tuple-element.94), channel_id=1, source_target_pairs={{0,4},{4,0},{8,12},{12,8},{16,20},{20,16},{24,28},{28,24},{1,5},{5... | collective-permute-start | bytes 663560 | tf_op jit(solution)/shard_map/ppermute | solution.py:49
  9.1 18.4 %collective-permute-start.10 = (bf16[256,384]{1,0:T(8,128)(2,1)}, bf16[256,384]{1,0:T(8,128)(2,1)}, u32[]{:S(2)}, u32[]{:S(2)}) collective-permute-start(bf16[256,384]{1,0:T(8,128)(2,1)} %param.11), channel_id=1, source_target_pairs={{0,8},{4,12},{8,16},{12,20},{1,9},{5,13},{9,17},{13,21},{2,10},{6,... | collective-permute-start | bytes 589832 | tf_op jit(solution)/shard_map/ppermute | solution.py:62
  26.0 21.4 %collective-permute-start.12 = (bf16[576,384]{1,0:T(8,128)(2,1)}, bf16[576,384]{1,0:T(8,128)(2,1)}, u32[]{:S(2)}, u32[]{:S(2)}) collective-permute-start(bf16[576,384]{1,0:T(8,128)(2,1)} %pad_maximum_fusion.1.refs_6_), channel_id=1, source_target_pairs={{0,16},{4,20},{8,24},{12,28},{16,0},{20,4},{24,8},{28,12},{1,17},{... | collective-permute-start | bytes 1327112 | tf_op jit(solution)/shard_map/ppermute | solution.py:62
  26.0 16.3 %collective-permute-start.1 = (bf16[512,384]{1,0:T(8,128)(2,1)}, bf16[512,384]{1,0:T(8,128)(2,1)}, u32[]{:S(2)}, u32[]{:S(2)}) collective-permute-start(bf16[512,384]{1,0:T(8,128)(2,1)} %pad_maximum_fusion.2), channel_id=1, source_target_pairs={{0,2},{1,3},{2,0},{3,1},{4,6},{5,7},{6,4},{7,5},{8,10},{9,11},{10,... | collective-permute-start | bytes 1179656 | tf_op jit(solution)/shard_map/ppermute | solution.py:55
  28.7 20.2 %collective-permute-start.2 = (bf16[512,384]{1,0:T(8,128)(2,1)}, bf16[512,384]{1,0:T(8,128)(2,1)}, u32[]{:S(2)}, u32[]{:S(2)}) collective-permute-start(bf16[512,384]{1,0:T(8,128)(2,1)} %pad_maximum_fusion.2), channel_id=1, source_target_pairs={{0,4},{4,0},{8,12},{12,8},{16,20},{20,16},{24,28},{28,24},{1,5},{5... | collective-permute-start | bytes 1179656 | tf_op jit(solution)/shard_map/ppermute | solution.py:49
  30.9 62.3 %collective-permute-start.24 = (bf16[1536,192]{0,1:T(8,128)(2,1)}, bf16[1536,192]{0,1:T(8,128)(2,1)}, u32[]{:S(2)}, u32[]{:S(2)}) collective-permute-start(bf16[1536,192]{0,1:T(8,128)(2,1)} %copy.43), channel_id=1, source_target_pairs={{0,4},{4,0},{8,12},{12,8},{16,20},{20,16},{24,28},{28,24},{1,5},{5... | collective-permute-start | bytes 1769480 | tf_op jit(solution)/shard_map/ppermute | solution.py:49
  40.8 17.1 %collective-permute-start.15 = (bf16[256,384]{1,0:T(8,128)(2,1)S(1)}, bf16[256,384]{1,0:T(8,128)(2,1)S(1)}, u32[]{:S(2)}, u32[]{:S(2)}) collective-permute-start(bf16[256,384]{1,0:T(8,128)(2,1)S(1)} %get-tuple-element.104), channel_id=1, source_target_pairs={{0,4},{4,0},{8,12},{12,8},{16,20},{20,16},{24,28},{28,24},{1,5},{5... | collective-permute-start | bytes 589832 | tf_op jit(solution)/shard_map/ppermute | solution.py:49
  42.3 34.0 %collective-permute-start.3 = (bf16[512,384]{1,0:T(8,128)(2,1)}, bf16[512,384]{1,0:T(8,128)(2,1)S(1)}, u32[]{:S(2)}, u32[]{:S(2)}) collective-permute-start(bf16[512,384]{1,0:T(8,128)(2,1)} %collective-permute-done.1), channel_id=1, source_target_pairs={{0,4},{4,0},{8,12},{12,8},{16,20},{20,16},{24,28},{28,24},{1,5},{5... | collective-permute-start | bytes 1179656 | tf_op jit(solution)/shard_map/ppermute | solution.py:49
  47.4 23.2 %collective-permute-start.13 = (bf16[256,384]{1,0:T(8,128)(2,1)S(1)}, bf16[256,384]{1,0:T(8,128)(2,1)S(1)}, u32[]{:S(2)}, u32[]{:S(2)}) collective-permute-start(bf16[256,384]{1,0:T(8,128)(2,1)S(1)} %get-tuple-element.101), channel_id=1, source_target_pairs={{0,4},{4,0},{8,12},{12,8},{16,20},{20,16},{24,28},{28,24},{1,5},{5... | collective-permute-start | bytes 589832 | tf_op jit(solution)/shard_map/ppermute | solution.py:49
  48.9 23.8 %collective-permute-start.14 = (bf16[256,384]{1,0:T(8,128)(2,1)}, bf16[256,384]{1,0:T(8,128)(2,1)S(1)}, u32[]{:S(2)}, u32[]{:S(2)}) collective-permute-start(bf16[256,384]{1,0:T(8,128)(2,1)} %collective-permute-done.11), channel_id=1, source_target_pairs={{0,4},{4,0},{8,12},{12,8},{16,20},{20,16},{24,28},{28,24},{1,5},{5... | collective-permute-start | bytes 589832 | tf_op jit(solution)/shard_map/ppermute | solution.py:49
  76.2 43.1 %collective-permute-start.18 = (bf16[2048,384]{1,0:T(8,128)(2,1)S(1)}, bf16[2048,384]{1,0:T(8,128)(2,1)}, u32[]{:S(2)}, u32[]{:S(2)}) collective-permute-start(bf16[2048,384]{1,0:T(8,128)(2,1)S(1)} %constant_dynamic-update-slice_fusion.4.refs_0_), channel_id=1, source_target_pairs={{0,1},{1,0},{2,3},{3,2},{4,5},{5,4},{6,7},{7,6},{8,9},{9,8},{10,11... | collective-permute-start | bytes 4718600 | tf_op jit(solution)/shard_map/ppermute | solution.py:58
  76.4 39.5 %collective-permute-start.4 = (bf16[2048,384]{1,0:T(8,128)(2,1)S(1)}, bf16[2048,384]{1,0:T(8,128)(2,1)}, u32[]{:S(2)}, u32[]{:S(2)}) collective-permute-start(bf16[2048,384]{1,0:T(8,128)(2,1)S(1)} %constant_dynamic-update-slice_fusion.refs_0_), channel_id=1, source_target_pairs={{0,1},{1,0},{2,3},{3,2},{4,5},{5,4},{6,7},{7,6},{8,9},{9,8},{10,11... | collective-permute-start | bytes 4718600 | tf_op jit(solution)/shard_map/ppermute | solution.py:58
  78.4 24.7 %collective-permute-start.19 = (bf16[576,384]{1,0:T(8,128)(2,1)}, bf16[576,384]{1,0:T(8,128)(2,1)}, u32[]{:S(2)}, u32[]{:S(2)}) collective-permute-start(bf16[576,384]{1,0:T(8,128)(2,1)} %pad_maximum_fusion.1.refs_6_), channel_id=1, source_target_pairs={{0,8},{4,12},{8,0},{12,4},{16,24},{20,28},{24,16},{28,20},{1,9},{5... | collective-permute-start | bytes 1327112 | tf_op jit(solution)/shard_map/ppermute | solution.py:62
  93.3 18.7 %collective-permute-start.21 = (bf16[576,384]{1,0:T(8,128)(2,1)}, bf16[576,384]{1,0:T(8,128)(2,1)}, u32[]{:S(2)}, u32[]{:S(2)}) collective-permute-start(bf16[576,384]{1,0:T(8,128)(2,1)} %collective-permute-done.12.refs_8_), channel_id=1, source_target_pairs={{8,0},{12,4},{16,24},{20,28},{9,1},{13,5},{17,25},{21,29},{10,2},{... | collective-permute-start | bytes 1327112 | tf_op jit(solution)/shard_map/ppermute | solution.py:62
  112.0 53.6 %collective-permute-start.25 = (bf16[1536,384]{1,0:T(8,128)(2,1)S(1)}, bf16[1536,384]{1,0:T(8,128)(2,1)S(1)}, u32[]{:S(2)}, u32[]{:S(2)}) collective-permute-start(bf16[1536,384]{1,0:T(8,128)(2,1)S(1)} %pad_maximum_fusion.refs_2_.refs_1_), channel_id=1, source_target_pairs={{0,16},{4,20},{8,24},{12,28},{16,0},{20,4},{24,8},{28,12},{1,17},{... | collective-permute-start | bytes 3538952 | tf_op jit(solution)/shard_map/ppermute | solution.py:62
  167.5 28.9 %collective-permute-start.32 = (bf16[1536,384]{1,0:T(8,128)(2,1)S(1)}, bf16[1536,384]{1,0:T(8,128)(2,1)S(1)}, u32[]{:S(2)}, u32[]{:S(2)}) collective-permute-start(bf16[1536,384]{1,0:T(8,128)(2,1)S(1)} %pad_maximum_fusion.refs_2_.refs_1_), channel_id=1, source_target_pairs={{0,8},{4,12},{8,0},{12,4},{16,24},{20,28},{24,16},{28,20},{1,9},{5... | collective-permute-start | bytes 3538952 | tf_op jit(solution)/shard_map/ppermute | solution.py:62
  167.9 28.5 %collective-permute-start.33 = (bf16[1536,384]{1,0:T(8,128)(2,1)S(1)}, bf16[1536,384]{1,0:T(8,128)(2,1)S(1)}, u32[]{:S(2)}, u32[]{:S(2)}) collective-permute-start(bf16[1536,384]{1,0:T(8,128)(2,1)S(1)} %pad_maximum_fusion.refs_2_.refs_1_), channel_id=1, source_target_pairs={{8,16},{12,20},{16,8},{20,12},{9,17},{13,21},{17,9},{21,13},{10,18... | collective-permute-start | bytes 3538952 | tf_op jit(solution)/shard_map/ppermute | solution.py:62
  168.7 50.1 %collective-permute-start.34 = (bf16[1536,384]{1,0:T(8,128)(2,1)S(1)}, bf16[1536,384]{1,0:T(8,128)(2,1)S(1)}, u32[]{:S(2)}, u32[]{:S(2)}) collective-permute-start(bf16[1536,384]{1,0:T(8,128)(2,1)S(1)} %collective-permute-done.25.refs_4_.refs_3_), channel_id=1, source_target_pairs={{8,0},{12,4},{16,24},{20,28},{9,1},{13,5},{17,25},{21,29},{10,2},{... | collective-permute-start | bytes 3538952 | tf_op jit(solution)/shard_map/ppermute | solution.py:62
  239.8 26.8 %collective-permute-start.43 = (bf16[1536,384]{1,0:T(8,128)(2,1)}, bf16[1536,384]{1,0:T(8,128)(2,1)}, u32[]{:S(2)}, u32[]{:S(2)}) collective-permute-start(bf16[1536,384]{1,0:T(8,128)(2,1)} %get-tuple-element.140), channel_id=1, source_target_pairs={{0,8},{4,12},{24,16},{28,20},{1,9},{5,13},{25,17},{29,21},{2,10},{... | collective-permute-start | bytes 3538952 | tf_op jit(solution)/shard_map/ppermute | solution.py:62
  242.3 24.3 %collective-permute-start.44 = (bf16[1536,384]{1,0:T(8,128)(2,1)}, bf16[1536,384]{1,0:T(8,128)(2,1)}, u32[]{:S(2)}, u32[]{:S(2)}) collective-permute-start(bf16[1536,384]{1,0:T(8,128)(2,1)} %get-tuple-element.140), channel_id=1, source_target_pairs={{8,16},{12,20},{16,8},{20,12},{9,17},{13,21},{17,9},{21,13},{10,18... | collective-permute-start | bytes 3538952 | tf_op jit(solution)/shard_map/ppermute | solution.py:62
  290.5 52.5 %collective-permute-start.52 = (bf16[1536,384]{1,0:T(8,128)(2,1)}, bf16[1536,384]{1,0:T(8,128)(2,1)}, u32[]{:S(2)}, u32[]{:S(2)}) collective-permute-start(bf16[1536,384]{1,0:T(8,128)(2,1)} %get-tuple-element.153), channel_id=1, source_target_pairs={{0,8},{4,12},{8,0},{12,4},{16,24},{20,28},{24,16},{28,20},{1,9},{5... | collective-permute-start | bytes 3538952 | tf_op jit(solution)/shard_map/ppermute | solution.py:62
  301.2 71.5 %collective-permute-start.53 = (bf16[1536,384]{1,0:T(8,128)(2,1)}, bf16[1536,384]{1,0:T(8,128)(2,1)}, u32[]{:S(2)}, u32[]{:S(2)}) collective-permute-start(bf16[1536,384]{1,0:T(8,128)(2,1)} %add_convert_fusion), channel_id=1, source_target_pairs={{0,16},{4,20},{8,24},{12,28},{16,0},{20,4},{24,8},{28,12},{1,17},{... | collective-permute-start | bytes 3538952 | tf_op jit(solution)/shard_map/ppermute | solution.py:62
  310.8 35.7 %collective-permute-start.49 = (bf16[192,512]{1,0:T(8,128)(2,1)}, bf16[192,512]{1,0:T(8,128)(2,1)S(1)}, u32[]{:S(2)}, u32[]{:S(2)}) collective-permute-start(bf16[192,512]{1,0:T(8,128)(2,1)} %get-tuple-element.148), channel_id=1, source_target_pairs={{8,0},{12,4},{16,8},{20,12},{9,1},{13,5},{17,9},{21,13},{10,2},{14... | collective-permute-start | bytes 589832 | tf_op jit(solution)/shard_map/ppermute | solution.py:62
  312.1 60.6 %collective-permute-start.50 = (bf16[192,512]{1,0:T(8,128)(2,1)}, bf16[192,512]{1,0:T(8,128)(2,1)S(1)}, u32[]{:S(2)}, u32[]{:S(2)}) collective-permute-start(bf16[192,512]{1,0:T(8,128)(2,1)} %get-tuple-element.149), channel_id=1, source_target_pairs={{16,0},{20,4},{24,8},{28,12},{17,1},{21,5},{25,9},{29,13},{18,2},{... | collective-permute-start | bytes 589832 | tf_op jit(solution)/shard_map/ppermute | solution.py:62
  317.8 54.9 %collective-permute-start.51 = (bf16[192,512]{1,0:T(8,128)(2,1)S(1)}, bf16[192,512]{1,0:T(8,128)(2,1)S(1)}, u32[]{:S(2)}, u32[]{:S(2)}) collective-permute-start(bf16[192,512]{1,0:T(8,128)(2,1)S(1)} %copy-done.75), channel_id=1, source_target_pairs={{24,0},{28,4},{25,1},{29,5},{26,2},{30,6},{27,3},{31,7}} | collective-permute-start | bytes 589832 | tf_op jit(solution)/shard_map/ppermute | solution.py:62
  343.0 43.3 %collective-permute-start.66 = (bf16[576,384]{1,0:T(8,128)(2,1)}, bf16[576,384]{1,0:T(8,128)(2,1)}, u32[]{:S(2)}, u32[]{:S(2)}) collective-permute-start(bf16[576,384]{1,0:T(8,128)(2,1)} %get-tuple-element.166), channel_id=1, source_target_pairs={{0,8},{4,12},{24,16},{28,20},{1,9},{5,13},{25,17},{29,21},{2,10},{... | collective-permute-start | bytes 1327112 | tf_op jit(solution)/shard_map/ppermute | solution.py:62
  346.6 68.0 %collective-permute-start.65 = (bf16[576,384]{1,0:T(8,128)(2,1)}, bf16[576,384]{1,0:T(8,128)(2,1)}, u32[]{:S(2)}, u32[]{:S(2)}) collective-permute-start(bf16[576,384]{1,0:T(8,128)(2,1)} %get-tuple-element.166), channel_id=1, source_target_pairs={{8,16},{12,20},{16,8},{20,12},{9,17},{13,21},{17,9},{21,13},{10,18... | collective-permute-start | bytes 1327112 | tf_op jit(solution)/shard_map/ppermute | solution.py:62
  378.5 36.1 %collective-permute-start.64 = (bf16[576,384]{1,0:T(8,128)(2,1)}, bf16[576,384]{1,0:T(8,128)(2,1)}, u32[]{:S(2)}, u32[]{:S(2)}) collective-permute-start(bf16[576,384]{1,0:T(8,128)(2,1)} %get-tuple-element.165), channel_id=1, source_target_pairs={{0,8},{4,12},{8,0},{12,4},{16,24},{20,28},{24,16},{28,20},{1,9},{5... | collective-permute-start | bytes 1327112 | tf_op jit(solution)/shard_map/ppermute | solution.py:62
  380.9 20.8 %collective-permute-start.56 = (bf16[512,384]{1,0:T(8,128)(2,1)}, bf16[512,384]{1,0:T(8,128)(2,1)}, u32[]{:S(2)}, u32[]{:S(2)}) collective-permute-start(bf16[512,384]{1,0:T(8,128)(2,1)} %select_convert_fusion.1), channel_id=1, source_target_pairs={{0,2},{1,3},{2,0},{3,1},{4,6},{5,7},{6,4},{7,5},{8,10},{9,11},{10,... | collective-permute-start | bytes 1179656 | tf_op jit(solution)/shard_map/ppermute | solution.py:55
  385.8 42.8 %collective-permute-start.69 = (bf16[1536,192]{0,1:T(8,128)(2,1)}, bf16[1536,192]{0,1:T(8,128)(2,1)}, u32[]{:S(2)}, u32[]{:S(2)}) collective-permute-start(bf16[1536,192]{0,1:T(8,128)(2,1)} %copy.47), channel_id=1, source_target_pairs={{0,4},{4,0},{8,12},{12,8},{16,20},{20,16},{24,28},{28,24},{1,5},{5... | collective-permute-start | bytes 1769480 | tf_op jit(solution)/shard_map/ppermute | solution.py:49
  386.4 14.9 %collective-permute-start.60 = (f32[1,512]{1,0:T(1,128)S(1)}, f32[1,512]{1,0:T(1,128)S(1)}, u32[]{:S(2)}, u32[]{:S(2)}) collective-permute-start(f32[1,512]{1,0:T(1,128)S(1)} %add.193), channel_id=1, source_target_pairs={{0,4},{4,0},{8,12},{12,8},{16,20},{20,16},{24,28},{28,24},{1,5},{5... | collective-permute-start | bytes 6152 | tf_op jit(solution)/shard_map/ppermute | solution.py:49
  401.3 21.8 %collective-permute-start.67 = (bf16[576,384]{1,0:T(8,128)(2,1)}, bf16[576,384]{1,0:T(8,128)(2,1)}, u32[]{:S(2)}, u32[]{:S(2)}) collective-permute-start(bf16[576,384]{1,0:T(8,128)(2,1)} %add_convert_fusion.1), channel_id=1, source_target_pairs={{0,16},{4,20},{8,24},{12,28},{16,0},{20,4},{24,8},{28,12},{1,17},{... | collective-permute-start | bytes 1327112 | tf_op jit(solution)/shard_map/ppermute | solution.py:62
  (134 other events, 1885.4 us)
where the time goes:
time: 444 us; the launch traced here: 439 us
  waiting for transfers between devices  216 us (49%)
  starting transfers between devices  85 us (19%)
  Pallas kernels  68.5 us (15%)
  other arithmetic  37.6 us (8%)
  local copies, waits for them, and re-layouts  29.7 us (7%)
    ppermute x22, waiting for transfers between devices, send_z(): return lax.ppermute(value, 'gx', pairs)  134 us
    pallas_call x15, Pallas kernels, call(): pl.pallas_call(kernel, out_shape=[jax.ShapeDtypeStruct(shape, dtype) for...  68.5 us
    ppermute x19, waiting for transfers between devices, swap_gx(): return lax.ppermute(value, 'gx', [(i, i ^ bit) for i in range(self.nx)])  55.3 us
    ppermute x22, starting transfers between devices, send_z(): return lax.ppermute(value, 'gx', pairs)  51.7 us
    ppermute x12, waiting for transfers between devices, swap_x(): return lax.ppermute(value, 'gy', [(i, i ^ 2) for i in range(self.ny)])  20.1 us
    unnamed x207, local copies, waits for them, and re-layouts  19.9 us
    ppermute x19, starting transfers between devices, swap_gx(): return lax.ppermute(value, 'gx', [(i, i ^ bit) for i in range(self.nx)])  16.9 us
    ppermute x12, starting transfers between devices, swap_x(): return lax.ppermute(value, 'gy', [(i, i ^ 2) for i in range(self.ny)])  12.3 us
  transfers between devices with their start and end apart: 70, of which 33 were waited for; matrix products, arithmetic and copies ran while one was open for 13% of the time, Pallas kernels for 8%

commit v1 on v0

--- a/solution.py
+++ b/solution.py
@@ -241,18 +241,17 @@
 
 def place_rows(table, pieces, whole):
     x, y, c = table[X], table[Y], table[C]
-    tokens = whole.shape[1] // 2
+    tokens = pieces[0].shape[0]
     for dc in range(2):
         for dx in range(2):
             block = 2 * (x + dx - 2 * x * dx) + c + dc - 2 * c * dc
             for dy in range(2):
                 at = pl.ds(pl.multiple_of(tokens * (y + dy - 2 * y * dy), tokens), tokens)
-                array, start = pieces[4 * dc + 2 * dy + dx]
-                whole[block, at, :] = array[start : start + tokens]
-
-
-def stacked_pieces(near, far, stride, start=0):
-    return [(a, start + i * stride) for a in (near, far) for i in range(4)]
+                whole[block, at, :] = pieces[4 * dc + 2 * dy + dx][...]
+
+
+def grad_body(table, *refs):
+    place_rows(table, refs[:8], refs[8])
 
 
 def norm_rows(raw, gain, normed):
@@ -272,12 +271,10 @@
     return scale
 
 
-def rows_body(table, near, far, *refs):
-    gains = refs[:4]
-    raw, grad, normed, inverse, gain_first, gain_second = refs[4:]
-    tokens = raw.shape[1]
-    place_rows(table, stacked_pieces(near, far, tokens), raw)
-    place_rows(table, stacked_pieces(near, far, tokens, tokens // 2), grad)
+def rows_body(table, *refs):
+    gains = refs[8:12]
+    raw, normed, inverse, gain_first, gain_second = refs[12:]
+    place_rows(table, refs[:8], raw)
     x, c = table[X], table[C]
     for dc in range(2):
         for dx in range(2):
@@ -288,14 +285,6 @@
     inverse[...] = norm_rows(raw, gain_first, normed)
 
 
-def prompt_body(table, near, far, gain, normed, slot):
-    tokens = slot.shape[1]
-    for i in range(PROMPTS):
-        at = 4 * i * (tokens // 2)
-        place_rows(table, stacked_pieces(near, far, tokens // 2, at), slot)
-        norm_rows(slot, gain, normed.at[:, i * tokens : (i + 1) * tokens])
-
-
 def turn(values, cosine, sine):
     half = values.shape[0] // 2
     first, second = values[:half], values[half:]
@@ -305,33 +294,16 @@
 
 
 def qkv_body(
-    table,
-    normed,
-    prompt,
-    cosine,
-    sine,
-    far_cosine,
-    far_sine,
-    pieces,
-    query,
-    own,
-    far,
-    weights,
-    acc,
-    far_acc,
-    sems,
+    table, normed, cosine, sine, pieces, query, own, weights, acc, sems
 ):
     wait = start_pieces(table, pieces, weights, sems)
     count = acc.shape[0]
-    far_count = far.shape[0]
-    for k in range(weights.shape[0]):
+    acc[...] = jnp.zeros_like(acc)
+
+    def one(k, _):
+        b = table[ORDER + k]
         wait(k)
-    acc[...] = jnp.zeros_like(acc)
-    far_acc[...] = jnp.zeros_like(far_acc)
-
-    def one(b, _):
         acc[...] += dims(weights[b, :count], normed[b], 1, 1)
-        far_acc[...] += dims(weights[b, count - far_count : count], prompt[b], 1, 1)
         return 0
 
     lax.fori_loop(0, normed.shape[0], one, 0)
@@ -344,24 +316,22 @@
     at = slice(heads * head, (heads + 1) * head)
     own[:head] = turn(acc[at], cos, sin).astype(bf16)
     own[head:] = acc[(heads + 1) * head :].astype(bf16)
-    far[:head] = turn(far_acc[:head], far_cosine[...], far_sine[...]).astype(bf16)
-    far[head:] = far_acc[head:].astype(bf16)
-
-
-def attend_body(
-    table,
-    query,
-    own,
-    far,
-    weights,
-    attended,
-    attended_low,
-    log_total,
-    keep,
-    first_send,
-    second_send,
-):
+
+
+def attend_body(table, query, own, *refs):
+    moved, refs = refs[: GROUP - 1], refs[GROUP - 1 :]
+    weights, attended, attended_low, log_total, far, keep, first_send, second_send = refs
     tokens = own.shape[1]
+    for place in range(GROUP):
+
+        @pl.when(table[Z_IN] == place)
+        def _():
+            for slot in range(PROMPTS):
+                k = place - slot
+                far[:, slot * tokens : (slot + 1) * tokens] = (
+                    moved[k - 1][...] if k > 0 else own[...]
+                )
+
     head = HEAD_DIM
     block = tokens // 2
     key_far, value_far = far[:head].T, far[head:]
@@ -542,13 +512,9 @@
     log_total,
     cosine,
     sine,
-    far_cosine,
-    far_sine,
     through,
     pull,
     query_low,
-    own_low,
-    far_low,
     own_back,
     *rest,
 ):
@@ -628,10 +594,6 @@
             return 0
 
         lax.fori_loop(0, heads_cols // head, one_head, 0)
-    own_low[:head] = turn(own_back[:head], cosine[...], -sine[...]).astype(bf16)
-    own_low[head:] = own_back[head:].astype(bf16)
-    far_low[:head] = turn(far_back[:head], far_cosine[...], -far_sine[...]).astype(bf16)
-    far_low[head:] = far_back[head:].astype(bf16)
     for slot in range(PROMPTS):
 
         @pl.when(table[Z_IN] == slot)
@@ -647,24 +609,20 @@
                 sends[k - 1][...] = far_back[:, slot * tokens : (slot + 1) * tokens].astype(bf16)
 
 
-def attend_parts_body(
-    table, query_low, own_low, far_low, normed, prompt, attended_low, through, *parts
-):
+def attend_parts_body(table, query_low, own_low, normed, attended_low, through, *parts):
     first = query_low.shape[0]
     second = first + own_low.shape[0]
     for k, part in enumerate(parts):
         b = table[ORDER + k]
         part[:first] = dims(query_low[...], normed[b], 1, 0).astype(bf16)
-        part[first:second] = (
-            dims(own_low[...], normed[b], 1, 0) + dims(far_low[...], prompt[b], 1, 0)
-        ).astype(bf16)
+        part[first:second] = dims(own_low[...], normed[b], 1, 0).astype(bf16)
         part[second:] = dims(attended_low[...], through[b], 1, 0).astype(bf16)
 
 
 def qkv_back_body(table, own_back, *refs):
     moved, refs = refs[: GROUP - 1], refs[GROUP - 1 :]
     query_low, weights, cosine, sine, own, inner = refs[:6]
-    keep, first_send, second_send, inner_first = refs[6:]
+    keep, first_send, second_send, inner_first, own_low = refs[6:]
     head = HEAD_DIM
     total = own_back[...]
     for part in moved:
@@ -672,6 +630,7 @@
     inner_first[...] = inner[...] + jnp.sum(total * own[...].astype(f32), axis=0, keepdims=True)
     key = turn(total[:head], cosine[...], -sine[...])
     low = jnp.concatenate([key, total[head:]], axis=0)
+    own_low[...] = low.astype(bf16)
     flipped = jnp.concatenate([query_low[...].T, low.T.astype(bf16)], axis=1)
     width = flipped.shape[1]
     keep_and_send(
@@ -689,13 +648,18 @@
     return jnp.where(flag, low, high), jnp.where(flag, high, low)
 
 
-def split_body(table, *refs):
-    count = len(refs) - 2
-    mine_ref, other_ref = refs[-2:]
+def split_body(table, matrices, mine_ref, other_ref, *scratch):
+    copies = [
+        pltpu.make_async_copy(source, held, scratch[-1].at[i])
+        for i, (source, held) in enumerate(zip(matrices, scratch))
+    ]
+    for copy in copies:
+        copy.start()
     at = 0
-    for i, ref in enumerate(refs[:count]):
-        whole = ref[...]
-        if i < count - 1:
+    for i, copy in enumerate(copies):
+        copy.wait()
+        whole = scratch[i][...]
+        if i < len(copies) - 1:
             whole = whole.T
         mine, other = halves_of(table, whole)
         rows = mine.shape[0]
@@ -756,17 +720,30 @@
     def halves(*matrices):
         rows = sum(max(m.shape) for m in matrices) // 2
         cols = min(matrices[0].shape)
-        return call(split_body, [((rows, cols), bf16)] * 2, table, matrices)
+        return call(
+            split_body,
+            [((rows, cols), bf16)] * 2,
+            table,
+            [],
+            [matrices],
+            [pltpu.VMEM(m.shape, bf16) for m in matrices]
+            + [pltpu.SemaphoreType.DMA((len(matrices),))],
+        )
 
     def whole_piece(mine, got):
         return jnp.concatenate(pair(y, mine, got), axis=1)
 
+    def spread(value):
+        by_x = place.swap_x(value)
+        four = [value, by_x, place.swap_y(value), place.swap_y(by_x)]
+        return four + [place.swap_c(r) for r in four]
+
     mine, other = halves(query_weight, key_matrix, value_matrix, out_weight)
-    early_in = after(layer_in, other)
     attend_got = place.swap_y(other)
     attend_piece = whole_piece(mine, attend_got)
+    input_rows = spread(after(layer_in, other))
     mine, other = halves(gate_weight, up_weight, down_weight)
-    forward_piece = whole_piece(mine, place.swap_y(after(other, attend_got)))
+    forward_piece = whole_piece(mine, place.swap_y(after(other, attend_got, input_rows[3])))
     if lined:
         attend_pieces = gather_pieces(place, attend_piece)
         forward_pieces = gather_pieces(place, after(forward_piece, *attend_pieces[1:]), True)
@@ -777,89 +754,46 @@
     forward_shape = (ny, 3 * hidden_dev, width)
     sems = pltpu.SemaphoreType.DMA((ny,))
 
-    def over_cores(four):
-        near = jnp.concatenate(four, axis=0)
-        return [near, place.swap_c(near)]
-
-    def spread(value):
-        by_x = place.swap_x(value)
-        return over_cores([value, by_x, place.swap_y(value), place.swap_y(by_x)])
-
     gains = jnp.stack([first_gain, second_gain])
     two = [gains, place.swap_x(gains)]
     gains = two + [place.swap_c(g) for g in two]
-    raw, grad, normed_in, inverse_in, gain_in, gain_mid = call(
+    raw, normed_in, inverse_in, gain_in, gain_mid = call(
         rows_body,
-        [(full, bf16)] * 3 + [((tokens, 1), f32)] + [((ny, 1, width), f32)] * 2,
-        table,
-        spread(after(jnp.concatenate([layer_in, out_grad], axis=0), attend_got)) + gains,
-    )
-
-    attend_hop = attend_pieces[len(attend_pieces) // 2]
+        [(full, bf16)] * 2 + [((tokens, 1), f32)] + [((ny, 1, width), f32)] * 2,
+        table,
+        input_rows + gains,
+    )
+
+    within = jnp.arange(block, dtype=jnp.int32)
+    positions = jnp.minimum(place.offset, PROMPT_DEV)[:, None] * block + within[None, :]
+    cosine, sine = rope_tables(positions.reshape(-1), HEAD_DIM // 2)
+    query, own, attend_weights = call(
+        qkv_body,
+        [((query_rows, tokens), bf16), ((kv_rows, tokens), bf16), (attend_shape, bf16)],
+        table,
+        [normed_in, cosine, sine],
+        [attend_pieces],
+        [pltpu.VMEM((qkv_cols, tokens), f32), sems],
+    )
     moved = [
         place.send_z(
-            early_in,
+            own,
             [(s, s + k) for s in range(n) if s % GROUP < PROMPTS and s % GROUP + k < GROUP],
         )
         for k in range(1, GROUP)
     ]
-    slots = [layer_in] * PROMPTS
-    for i in range(PROMPTS):
-        for k in range(1, GROUP):
-            slots[i] = jnp.where(z_in == i + k, moved[k - 1], slots[i])
-    pieces = []
-    for i, slot in enumerate(slots):
-        slot = after(slot, attend_got)
-        if i % 2 == 0:
-            by_x = place.swap_x(slot)
-            late, late_x = lax.optimization_barrier((slot, by_x, attend_hop))[:2]
-            pieces += [slot, by_x, place.swap_y(late), place.swap_y(late_x)]
-        else:
-            by_y = place.swap_y(slot)
-            late, late_y = lax.optimization_barrier((slot, by_y, attend_hop))[:2]
-            pieces += [slot, place.swap_x(late), by_y, place.swap_x(late_y)]
-    (prompt,) = call(
-        prompt_body,
-        [((ny, PROMPTS * tokens, width), bf16)],
-        table,
-        over_cores(pieces) + [gain_in],
-        scratch=[pltpu.VMEM(full, bf16)],
-    )
-
-    within = jnp.arange(block, dtype=jnp.int32)
-    positions = jnp.minimum(place.offset, PROMPT_DEV)[:, None] * block + within[None, :]
-    cosine, sine = rope_tables(positions.reshape(-1), HEAD_DIM // 2)
-    far_cosine, far_sine = rope_tables(
-        jnp.arange(PROMPTS * tokens, dtype=jnp.int32), HEAD_DIM // 2
-    )
-    tables = [cosine, sine, far_cosine, far_sine]
-    query, own, far, attend_weights = call(
-        qkv_body,
-        [
-            ((query_rows, tokens), bf16),
-            ((kv_rows, tokens), bf16),
-            ((kv_rows, PROMPTS * tokens), bf16),
-            (attend_shape, bf16),
-        ],
-        table,
-        [normed_in, prompt] + tables,
-        [attend_pieces],
-        [
-            pltpu.VMEM((qkv_cols, tokens), f32),
-            pltpu.VMEM((kv_rows, PROMPTS * tokens), f32),
-            sems,
-        ],
-    )
-    attended, attended_low, log_total, keep, *sends = call(
+    (grad,) = call(grad_body, [(full, bf16)], table, spread(after(out_grad, query)))
+    attended, attended_low, log_total, far, keep, *sends = call(
         attend_body,
         [
             ((query_rows, tokens), f32),
             ((query_rows, tokens), bf16),
             ((query_rows // HEAD_DIM, 1, tokens), f32),
+            ((kv_rows, PROMPTS * tokens), bf16),
         ]
         + wide,
         table,
-        [query, own, far, attend_weights],
+        [query, own] + moved + [attend_weights],
     )
     summed = all_sum(place, keep, sends, [forward_pieces[len(forward_pieces) // 2]])
 
@@ -890,14 +824,12 @@
     summed = all_sum(place, keep, sends, before_second=forward_parts[:1])
     forward_second = second_scatter(place, forward_started, summed[-1])
     hidden_own = own_block(place, hidden)
-    through, pull, query_low, own_low, far_low, own_back, *returns, inner_first = call(
+    through, pull, query_low, own_back, *returns, inner_first = call(
         attend_back_body,
         [
             (full, bf16),
             ((tokens, 1), f32),
             ((query_rows, tokens), bf16),
-            ((kv_rows, tokens), bf16),
-            ((kv_rows, PROMPTS * tokens), bf16),
             ((kv_rows, tokens), f32),
         ]
         + [((kv_rows, tokens), bf16)] * (GROUP - 1)
@@ -914,8 +846,9 @@
             far,
             attended,
             log_total,
-        ]
-        + tables,
+            cosine,
+            sine,
+        ],
         earlier=forward_started[2:3] + forward_started[4:],
         scratch=[
             pltpu.VMEM((kv_rows, PROMPTS * tokens), f32),
@@ -923,16 +856,6 @@
             pltpu.VMEM((query_rows, tokens), bf16),
         ],
     )
-    keep, *sends = call(
-        down_body,
-        wide,
-        table,
-        [active],
-        [forward_pieces],
-        [pltpu.VMEM((ny, hidden_dev, width), bf16), sems],
-        earlier=[through],
-    )
-    layer_out = (hidden_own + own_sum(place, keep, sends)).astype(bf16)
     inverse_own, _ = part_of(y, inverse_mid, 0)
     pull_own, _ = part_of(y, pull, 0)
     mid_own = jnp.where(place.x == 0, summed[0], summed[1])
@@ -951,26 +874,26 @@
         )
         for k in range(1, GROUP)
     ]
+    keep, *sends, inner, own_low = call(
+        qkv_back_body,
+        wide + [((1, tokens), f32), ((kv_rows, tokens), bf16)],
+        table,
+        [own_back] + moved + [query_low, attend_weights, cosine, sine, own, inner_first],
+        earlier=forward_started[3:4] + ([forward_second] if lined else []),
+    )
     attend_parts = call(
         attend_parts_body,
         [(attend_shape[1:], bf16)] * ny,
         table,
-        [query_low, own_low, far_low, normed_in, prompt, attended_low, through],
-    )
-    keep, *sends, inner = call(
-        qkv_back_body,
-        wide + [((1, tokens), f32)],
-        table,
-        [own_back] + moved + [query_low, attend_weights, cosine, sine, own, inner_first],
-        earlier=forward_started[3:4] + ([forward_second] if lined else []),
+        [query_low, own_low, normed_in, attended_low, through],
     )
     attend_started = start_scatter(place, attend_parts)
     if lined:
         attend_second = second_scatter(place, attend_started, forward_second)
     else:
         attend_second = None
-    forward_grad = end_scatter(place, forward_started, forward_second, sends[-1])
-    attend_grad = end_scatter(place, attend_started, attend_second, sends[-1])
+    forward_grad = end_scatter(place, forward_started, forward_second, own_low)
+    attend_grad = end_scatter(place, attend_started, attend_second, own_low)
     inner = inner + place.swap_c(inner)
     inner = inner + place.swap_x(inner)
     inner = inner + place.swap_y(inner)
@@ -988,6 +911,17 @@
     while bit < place.nx:
         terms = terms + place.swap_gx(terms, bit)
         bit *= 2
+
+    keep, *sends = call(
+        down_body,
+        wide,
+        table,
+        [active],
+        [forward_pieces],
+        [pltpu.VMEM((ny, hidden_dev, width), bf16), sems],
+        earlier=[own_low],
+    )
+    layer_out = (hidden_own + own_sum(place, keep, sends)).astype(bf16)
 
     def joined(summed_part, outs):
         mine, other = part_of(y, summed_part, 1)

time: 444 us -> 438 us (0.986)
  local copies, waits for them, and re-layouts: 29.7 us -> 44.8 us
  Pallas kernels: 68.5 us -> 55.4 us
  waiting for transfers between devices: 216 us -> 204 us
  starting transfers between devices: 85 us -> 96.9 us
    ppermute x19 -> x18, waiting for transfers between devices: 55.3 us -> 38 us  [swap_gx(): return lax.ppermute(value, 'gx', [(i, i ^ bit) for i in range(self.nx)])]
    unnamed x207 -> x165, local copies, waits for them, and re-layouts: 19.9 us -> 35.1 us
    ppermute x22, starting transfers between devices: 51.7 us -> 65.8 us  [send_z(): return lax.ppermute(value, 'gx', pairs)]
    pallas_call x15, Pallas kernels: 68.5 us -> 55.4 us  [call(): pl.pallas_call(kernel, out_shape=[jax.ShapeDtypeStruct(shape, dtype) for...]
    ppermute x22, waiting for transfers between devices: 134 us -> 142 us  [send_z(): return lax.ppermute(value, 'gx', pairs)]
    ppermute x12 -> x10, waiting for transfers between devices: 20.1 us -> 15.8 us  [swap_x(): return lax.ppermute(value, 'gy', [(i, i ^ 2) for i in range(self.ny)])]
    ppermute x19 -> x18, starting transfers between devices: 16.9 us -> 15.5 us  [swap_gx(): return lax.ppermute(value, 'gx', [(i, i ^ bit) for i in range(self.nx)])]
    ppermute x12 -> x10, starting transfers between devices: 12.3 us -> 11.7 us  [swap_x(): return lax.ppermute(value, 'gy', [(i, i ^ 2) for i in range(self.ny)])]
  transfers between devices with their start and end apart: 70 -> 73, of which waited for: 33 -> 39; matrix products, arithmetic and copies ran while one was open for 13% -> 11% of each run, Pallas kernels for 8% -> 9%
where the time goes in v1:
time: 438 us; the launch traced here: 437 us
  waiting for transfers between devices  204 us (47%)
  starting transfers between devices  96.9 us (22%)
  Pallas kernels  55.4 us (13%)
  local copies, waits for them, and re-layouts  44.8 us (10%)
  other arithmetic  33.5 us (8%)
    ppermute x22, waiting for transfers between devices, send_z(): return lax.ppermute(value, 'gx', pairs)  142 us
    ppermute x22, starting transfers between devices, send_z(): return lax.ppermute(value, 'gx', pairs)  65.8 us
    pallas_call x15, Pallas kernels, call(): pl.pallas_call(kernel, out_shape=[jax.ShapeDtypeStruct(shape, dtype) for...  55.4 us
    ppermute x18, waiting for transfers between devices, swap_gx(): return lax.ppermute(value, 'gx', [(i, i ^ bit) for i in range(self.nx)])  38 us
    unnamed x165, local copies, waits for them, and re-layouts  35.1 us
    ppermute x10, waiting for transfers between devices, swap_x(): return lax.ppermute(value, 'gy', [(i, i ^ 2) for i in range(self.ny)])  15.8 us
    ppermute x18, starting transfers between devices, swap_gx(): return lax.ppermute(value, 'gx', [(i, i ^ bit) for i in range(self.nx)])  15.5 us
    ppermute x10, starting transfers between devices, swap_x(): return lax.ppermute(value, 'gy', [(i, i ^ 2) for i in range(self.ny)])  11.7 us
  transfers between devices with their start and end apart: 73, of which 39 were waited for; matrix products, arithmetic and copies ran while one was open for 11% of the time, Pallas kernels for 9%

profile of v1, /device:TPU:0, one launch (start us, length us, event | category | flops | bytes accessed | tf_op | source)
XLA Modules:
  0.0 436.5 jit_solution(8769420177636584031)
XLA Ops:
  7.0 3.0 collective-permute-start
  11.5 3.6 collective-permute-done.refs_1_
  21.1 3.3 collective-permute-done.2.refs_3_
  32.2 14.8 %collective-permute-done.12.refs_5_ = bf16[576,384]{1,0:T(8,128)(2,1)S(1)} collective-permute-done((bf16[576,384]{1,0:T(8,128)(2,1)S(1)}, bf16[576,384]{1,0:T(8,128)(2,1)S(1)}, u32[]{:S(2)}, u32[]{:S(2)}) %collective-permute-start.12) | collective-permute-done | bytes 442400 | tf_op jit(solution)/shard_map/ppermute | solution.py:62
  54.8 6.3 %collective-permute-done.14.refs_7_ = bf16[576,384]{1,0:T(8,128)(2,1)S(1)} collective-permute-done((bf16[576,384]{1,0:T(8,128)(2,1)S(1)}, bf16[576,384]{1,0:T(8,128)(2,1)S(1)}, u32[]{:S(2)}, u32[]{:S(2)}) %collective-permute-start.14) | collective-permute-done | bytes 442400 | tf_op jit(solution)/shard_map/ppermute | solution.py:62
  70.7 3.3 shard_map.196
  74.0 4.4 %collective-permute-start.15 = (bf16[192,512]{1,0:T(8,128)(2,1)S(1)}, bf16[192,512]{1,0:T(8,128)(2,1)S(1)}, u32[]{:S(2)}, u32[]{:S(2)}) collective-permute-start(bf16[192,512]{1,0:T(8,128)(2,1)S(1)} %get-tuple-element.91.refs_1_.refs_10_.refs_8_), channel_id=1, source_target_pairs={{0,8},{4,12},{8,16},{12,20},{1,9},{5,13},{9,17},{13,21},{2,10},{6,... | collective-permute-start | bytes 589832 | tf_op jit(solution)/shard_map/ppermute | solution.py:62
  81.1 13.5 %collective-permute-done.15.refs_2_ = bf16[192,512]{1,0:T(8,128)(2,1)S(1)} collective-permute-done((bf16[192,512]{1,0:T(8,128)(2,1)S(1)}, bf16[192,512]{1,0:T(8,128)(2,1)S(1)}, u32[]{:S(2)}, u32[]{:S(2)}) %collective-permute-start.15) | collective-permute-done | bytes 196640 | tf_op jit(solution)/shard_map/ppermute | solution.py:62
  94.5 4.3 collective-permute-done.16.refs_3_
  101.4 5.2 %shard_map.197 = (f32[192,512]{1,0:T(8,128)S(1)}, bf16[192,512]{1,0:T(8,128)(2,1)S(1)}, f32[2,1,512]{2,1,0:T(1,128)S(1)}, bf16[192,1024]{1,0:T(8,128)(2,1)S(1)},...) custom-call(s32[11]{0:T(128)S(1)} %concatenate.9.table_ref, ...), custom_call_target="tpu_custom_call" | custom-call | tf_op jit(solution)/shard_map/pallas_call | solution.py:191
  109.2 5.5 %collective-permute-done.21.refs_4_.refs_3_ = bf16[1536,384]{1,0:T(8,128)(2,1)S(1)} collective-permute-done((bf16[1536,384]{1,0:T(8,128)(2,1)S(1)}, bf16[1536,384]{1,0:T(8,128)(2,1)S(1)}, u32[]{:S(2)}, u32[]{:S(2)}) %collective-permute-start.21) | collective-permute-done | bytes 1179680 | tf_op jit(solution)/shard_map/ppermute | solution.py:62
  118.7 9.0 %collective-permute-done.28.refs_1_ = bf16[256,384]{1,0:T(8,128)(2,1)S(1)} collective-permute-done((bf16[256,384]{1,0:T(8,128)(2,1)S(1)}, bf16[256,384]{1,0:T(8,128)(2,1)S(1)}, u32[]{:S(2)}, u32[]{:S(2)}) %collective-permute-start.28) | collective-permute-done | bytes 196640 | tf_op jit(solution)/shard_map/ppermute | solution.py:55
  127.8 27.7 %collective-permute-start.35 = (bf16[1536,384]{1,0:T(8,128)(2,1)S(1)}, bf16[1536,384]{1,0:T(8,128)(2,1)S(1)}, u32[]{:S(2)}, u32[]{:S(2)}) collective-permute-start(bf16[1536,384]{1,0:T(8,128)(2,1)S(1)} %pad_maximum_fusion.refs_2_.refs_1_), channel_id=1, source_target_pairs={{0,8},{4,12},{8,0},{12,4},{16,24},{20,28},{24,16},{28,20},{1,9},{5... | collective-permute-start | bytes 3538952 | tf_op jit(solution)/shard_map/ppermute | solution.py:62
  158.3 3.0 collective-permute-done.30.refs_3_
  162.6 7.8 %collective-permute-done.24 = bf16[512,384]{1,0:T(8,128)(2,1)S(1)} collective-permute-done((bf16[512,384]{1,0:T(8,128)(2,1)S(1)}, bf16[512,384]{1,0:T(8,128)(2,1)S(1)}, u32[]{:S(2)}, u32[]{:S(2)}) %collective-permute-start.24) | collective-permute-done | bytes 393248 | tf_op jit(solution)/shard_map/ppermute | solution.py:49
  176.9 5.5 %collective-permute-done.35.refs_3_.refs_2_ = bf16[1536,384]{1,0:T(8,128)(2,1)S(1)} collective-permute-done((bf16[1536,384]{1,0:T(8,128)(2,1)S(1)}, bf16[1536,384]{1,0:T(8,128)(2,1)S(1)}, u32[]{:S(2)}, u32[]{:S(2)}) %collective-permute-start.35) | collective-permute-done | bytes 1179680 | tf_op jit(solution)/shard_map/ppermute | solution.py:62
  182.4 23.8 %collective-permute-done.37.refs_6_.refs_5_ = bf16[1536,384]{1,0:T(8,128)(2,1)S(1)} collective-permute-done((bf16[1536,384]{1,0:T(8,128)(2,1)S(1)}, bf16[1536,384]{1,0:T(8,128)(2,1)S(1)}, u32[]{:S(2)}, u32[]{:S(2)}) %collective-permute-start.37) | collective-permute-done | bytes 1179680 | tf_op jit(solution)/shard_map/ppermute | solution.py:62
  206.2 10.0 %shard_map.201 = (bf16[512,512]{1,0:T(8,128)(2,1)S(1)}, bf16[512,1024]{1,0:T(8,128)(2,1)S(1)}, f32[2,512,384]{2,1,0:T(8,128)S(1)}, bf16[512,384]{1,0:T(8,128)(2,1)S(1)}, bf16[512,384]{1,0:T(8,128)(2,1)S(1)}) custom-call(s32[11]{0:T(128)S(1)} %concatenate.9.table_ref, bf16[4,512,384]{2,1,0:T(8,128)(2,1)S(1)} %get-tuple-element.106.refs_0_.refs_2_, ...), custom_call_target="tpu_custom_call" | custom-call | tf_op jit(solution)/shard_map/pallas_call | solution.py:191
  220.2 6.4 %shard_map.202 = (bf16[1536,384]{1,0:T(8,128)(2,1)S(1)}, bf16[1536,384]{1,0:T(8,128)(2,1)}, bf16[1536,384]{1,0:T(8,128)(2,1)S(1)}, bf16[1536,384]{1,0:T(8,128)(2,1)}) custom-call(s32[11]{0:T(128)S(1)} %concatenate.9.table_ref, bf16[512,512]{1,0:T(8,128)(2,1)S(1)} %get-tuple-element.109.refs_0_, bf16[4,512,384]{2,1,0:T(8,128)(2,1)S(1)} %shard_map.200.refs_1_.refs_6_, ...), custom_call_target="tpu_custom_call" | custom-call | tf_op jit(solution)/shard_map/pallas_call | solution.py:191
  233.5 8.6 %collective-permute-done.42 = bf16[512,384]{1,0:T(8,128)(2,1)} collective-permute-done((bf16[512,384]{1,0:T(8,128)(2,1)}, bf16[512,384]{1,0:T(8,128)(2,1)}, u32[]{:S(2)}, u32[]{:S(2)}) %collective-permute-start.42) | collective-permute-done | bytes 393248 | tf_op jit(solution)/shard_map/ppermute | solution.py:49
  242.4 3.3 broadcast_select_fusion.2
  247.4 3.4 collective-permute-start.51
  251.6 3.1 collective-permute-done.46.refs_16_
  257.3 5.6 %collective-permute-start.52 = (bf16[1536,384]{1,0:T(8,128)(2,1)}, bf16[1536,384]{1,0:T(8,128)(2,1)}, u32[]{:S(2)}, u32[]{:S(2)}) collective-permute-start(bf16[1536,384]{1,0:T(8,128)(2,1)} %add_convert_fusion), channel_id=1, source_target_pairs={{0,16},{4,20},{8,24},{12,28},{16,0},{20,4},{24,8},{28,12},{1,17},{... | collective-permute-start | bytes 3538952 | tf_op jit(solution)/shard_map/ppermute | solution.py:62
  274.5 8.8 %shard_map.203 = (bf16[4,512,384]{2,1,0:T(8,128)(2,1)S(1)}, f32[512,1]{1,0:T(8,128)S(1)}, bf16[192,512]{1,0:T(8,128)(2,1)S(1)}, f32[192,512]{1,0:T(8,128)S(1)}, ...) custom-call(s32[11]{0:T(128)S(1)} %concatenate.9.table_ref, ...), custom_call_target="tpu_custom_call" | custom-call | tf_op jit(solution)/shard_map/pallas_call | solution.py:191
  288.8 15.2 %collective-permute-done.48.refs_1_ = bf16[192,512]{1,0:T(8,128)(2,1)S(1)} collective-permute-done((bf16[192,512]{1,0:T(8,128)(2,1)S(1)}, bf16[192,512]{1,0:T(8,128)(2,1)S(1)}, u32[]{:S(2)}, u32[]{:S(2)}) %collective-permute-start.48) | collective-permute-done | bytes 196640 | tf_op jit(solution)/shard_map/ppermute | solution.py:62
  304.1 40.4 %collective-permute-done.49.refs_2_ = bf16[192,512]{1,0:T(8,128)(2,1)S(1)} collective-permute-done((bf16[192,512]{1,0:T(8,128)(2,1)S(1)}, bf16[192,512]{1,0:T(8,128)(2,1)S(1)}, u32[]{:S(2)}, u32[]{:S(2)}) %collective-permute-start.49) | collective-permute-done | bytes 196640 | tf_op jit(solution)/shard_map/ppermute | solution.py:62
  347.3 3.1 convert_add_fusion
  371.3 3.3 shard_map.205
  389.6 7.1 %collective-permute-done.72 = bf16[1536,192]{0,1:T(8,128)(2,1)} collective-permute-done((bf16[1536,192]{0,1:T(8,128)(2,1)}, bf16[1536,192]{0,1:T(8,128)(2,1)}, u32[]{:S(2)}, u32[]{:S(2)}) %collective-permute-start.72) | collective-permute-done | bytes 589856 | tf_op jit(solution)/shard_map/ppermute | solution.py:49
  410.8 6.8 %collective-permute-done.70 = bf16[576,384]{1,0:T(8,128)(2,1)} collective-permute-done((bf16[576,384]{1,0:T(8,128)(2,1)}, bf16[576,384]{1,0:T(8,128)(2,1)}, u32[]{:S(2)}, u32[]{:S(2)}) %collective-permute-start.70) | collective-permute-done | bytes 442400 | tf_op jit(solution)/shard_map/ppermute | solution.py:62
  422.1 2.9 collective-permute-done.64
  (350 shorter events, 162.8 us)
Async XLA Ops:
  16.8 47.1 %collective-permute-start.1 = (bf16[256,384]{1,0:T(8,128)(2,1)}, bf16[256,384]{1,0:T(8,128)(2,1)}, u32[]{:S(2)}, u32[]{:S(2)}) collective-permute-start(bf16[256,384]{1,0:T(8,128)(2,1)} %refs_0_.3), channel_id=1, source_target_pairs={{0,4},{4,0},{8,12},{12,8},{16,20},{20,16},{24,28},{28,24},{1,5},{5... | collective-permute-start | bytes 589832 | tf_op jit(solution)/shard_map/ppermute | solution.py:49
  24.7 23.0 %collective-permute-start.20 = (bf16[1536,192]{0,1:T(8,128)(2,1)S(1)}, bf16[1536,192]{0,1:T(8,128)(2,1)}, u32[]{:S(2)}, u32[]{:S(2)}) collective-permute-start(bf16[1536,192]{0,1:T(8,128)(2,1)S(1)} %copy.43), channel_id=1, source_target_pairs={{0,4},{4,0},{8,12},{12,8},{16,20},{20,16},{24,28},{28,24},{1,5},{5... | collective-permute-start | bytes 1769480 | tf_op jit(solution)/shard_map/ppermute | solution.py:49
  27.4 19.5 %collective-permute-start.12 = (bf16[576,384]{1,0:T(8,128)(2,1)S(1)}, bf16[576,384]{1,0:T(8,128)(2,1)S(1)}, u32[]{:S(2)}, u32[]{:S(2)}) collective-permute-start(bf16[576,384]{1,0:T(8,128)(2,1)S(1)} %pad_maximum_fusion.1.refs_3_), channel_id=1, source_target_pairs={{0,16},{4,20},{8,24},{12,28},{16,0},{20,4},{24,8},{28,12},{1,17},{... | collective-permute-start | bytes 1327112 | tf_op jit(solution)/shard_map/ppermute | solution.py:62
  30.1 22.8 %collective-permute-start.7 = (f32[2,384]{1,0:T(2,128)S(1)}, f32[2,384]{1,0:T(2,128)S(1)}, u32[]{:S(2)}, u32[]{:S(2)}) collective-permute-start(f32[2,384]{1,0:T(2,128)S(1)} %pad_maximum_fusion.2.refs_8_), channel_id=1, source_target_pairs={{0,2},{1,3},{2,0},{3,1},{4,6},{5,7},{6,4},{7,5},{8,10},{9,11},{10,... | collective-permute-start | bytes 9224 | tf_op jit(solution)/shard_map/ppermute | solution.py:55
  30.6 22.8 %collective-permute-start.11 = (bf16[576,384]{1,0:T(8,128)(2,1)S(1)}, bf16[576,384]{1,0:T(8,128)(2,1)S(1)}, u32[]{:S(2)}, u32[]{:S(2)}) collective-permute-start(bf16[576,384]{1,0:T(8,128)(2,1)S(1)} %pad_maximum_fusion.1.refs_3_), channel_id=1, source_target_pairs={{0,8},{4,12},{8,0},{12,4},{16,24},{20,28},{24,16},{28,20},{1,9},{5... | collective-permute-start | bytes 1327112 | tf_op jit(solution)/shard_map/ppermute | solution.py:62
  61.8 52.8 %collective-permute-start.21 = (bf16[1536,384]{1,0:T(8,128)(2,1)S(1)}, bf16[1536,384]{1,0:T(8,128)(2,1)S(1)}, u32[]{:S(2)}, u32[]{:S(2)}) collective-permute-start(bf16[1536,384]{1,0:T(8,128)(2,1)S(1)} %pad_maximum_fusion.refs_2_.refs_1_), channel_id=1, source_target_pairs={{0,16},{4,20},{8,24},{12,28},{16,0},{20,4},{24,8},{28,12},{1,17},{... | collective-permute-start | bytes 3538952 | tf_op jit(solution)/shard_map/ppermute | solution.py:62
  74.0 20.5 %collective-permute-start.15 = (bf16[192,512]{1,0:T(8,128)(2,1)S(1)}, bf16[192,512]{1,0:T(8,128)(2,1)S(1)}, u32[]{:S(2)}, u32[]{:S(2)}) collective-permute-start(bf16[192,512]{1,0:T(8,128)(2,1)S(1)} %get-tuple-element.91.refs_1_.refs_10_.refs_8_), channel_id=1, source_target_pairs={{0,8},{4,12},{8,16},{12,20},{1,9},{5,13},{9,17},{13,21},{2,10},{6,... | collective-permute-start | bytes 589832 | tf_op jit(solution)/shard_map/ppermute | solution.py:62
  78.4 20.4 %collective-permute-start.16 = (bf16[192,512]{1,0:T(8,128)(2,1)S(1)}, bf16[192,512]{1,0:T(8,128)(2,1)S(1)}, u32[]{:S(2)}, u32[]{:S(2)}) collective-permute-start(bf16[192,512]{1,0:T(8,128)(2,1)S(1)} %get-tuple-element.91.refs_1_.refs_10_.refs_8_), channel_id=1, source_target_pairs={{0,16},{4,20},{8,24},{12,28},{1,17},{5,21},{9,25},{13,29},{2,18},{... | collective-permute-start | bytes 589832 | tf_op jit(solution)/shard_map/ppermute | solution.py:62
  79.8 21.6 %collective-permute-start.17 = (bf16[192,512]{1,0:T(8,128)(2,1)S(1)}, bf16[192,512]{1,0:T(8,128)(2,1)S(1)}, u32[]{:S(2)}, u32[]{:S(2)}) collective-permute-start(bf16[192,512]{1,0:T(8,128)(2,1)S(1)} %get-tuple-element.91.refs_1_.refs_10_.refs_8_), channel_id=1, source_target_pairs={{0,24},{4,28},{1,25},{5,29},{2,26},{6,30},{3,27},{7,31}} | collective-permute-start | bytes 589832 | tf_op jit(solution)/shard_map/ppermute | solution.py:62
  114.7 41.3 %collective-permute-start.22 = (bf16[512,384]{1,0:T(8,128)(2,1)S(1)}, bf16[512,384]{1,0:T(8,128)(2,1)S(1)}, u32[]{:S(2)}, u32[]{:S(2)}) collective-permute-start(bf16[512,384]{1,0:T(8,128)(2,1)S(1)} %get-tuple-element.100), channel_id=1, source_target_pairs={{0,2},{1,3},{2,0},{3,1},{4,6},{5,7},{6,4},{7,5},{8,10},{9,11},{10,... | collective-permute-start | bytes 1179656 | tf_op jit(solution)/shard_map/ppermute | solution.py:55
  115.5 41.3 %collective-permute-start.23 = (bf16[512,384]{1,0:T(8,128)(2,1)S(1)}, bf16[512,384]{1,0:T(8,128)(2,1)S(1)}, u32[]{:S(2)}, u32[]{:S(2)}) collective-permute-start(bf16[512,384]{1,0:T(8,128)(2,1)S(1)} %get-tuple-element.101), channel_id=1, source_target_pairs={{0,4},{4,0},{8,12},{12,8},{16,20},{20,16},{24,28},{28,24},{1,5},{5... | collective-permute-start | bytes 1179656 | tf_op jit(solution)/shard_map/ppermute | solution.py:49
  117.2 38.3 %collective-permute-start.29 = (bf16[256,384]{1,0:T(8,128)(2,1)S(1)}, bf16[256,384]{1,0:T(8,128)(2,1)S(1)}, u32[]{:S(2)}, u32[]{:S(2)}) collective-permute-start(bf16[256,384]{1,0:T(8,128)(2,1)S(1)} %copy-done.42), channel_id=1, source_target_pairs={{0,4},{4,0},{8,12},{12,8},{16,20},{20,16},{24,28},{28,24},{1,5},{5... | collective-permute-start | bytes 589832 | tf_op jit(solution)/shard_map/ppermute | solution.py:49
  118.7 37.2 %collective-permute-start.31 = (bf16[256,384]{1,0:T(8,128)(2,1)S(1)}, bf16[256,384]{1,0:T(8,128)(2,1)S(1)}, u32[]{:S(2)}, u32[]{:S(2)}) collective-permute-start(bf16[256,384]{1,0:T(8,128)(2,1)S(1)} %copy-done.42), channel_id=1, source_target_pairs={{0,1},{1,0},{2,3},{3,2},{4,5},{5,4},{6,7},{7,6},{8,9},{9,8},{10,11... | collective-permute-start | bytes 589832 | tf_op jit(solution)/shard_map/ppermute | solution.py:58
  127.8 54.6 %collective-permute-start.35 = (bf16[1536,384]{1,0:T(8,128)(2,1)S(1)}, bf16[1536,384]{1,0:T(8,128)(2,1)S(1)}, u32[]{:S(2)}, u32[]{:S(2)}) collective-permute-start(bf16[1536,384]{1,0:T(8,128)(2,1)S(1)} %pad_maximum_fusion.refs_2_.refs_1_), channel_id=1, source_target_pairs={{0,8},{4,12},{8,0},{12,4},{16,24},{20,28},{24,16},{28,20},{1,9},{5... | collective-permute-start | bytes 3538952 | tf_op jit(solution)/shard_map/ppermute | solution.py:62
  156.0 26.4 %collective-permute-start.36 = (bf16[1536,384]{1,0:T(8,128)(2,1)S(1)}, bf16[1536,384]{1,0:T(8,128)(2,1)S(1)}, u32[]{:S(2)}, u32[]{:S(2)}) collective-permute-start(bf16[1536,384]{1,0:T(8,128)(2,1)S(1)} %pad_maximum_fusion.refs_2_.refs_1_), channel_id=1, source_target_pairs={{8,16},{12,20},{16,8},{20,12},{9,17},{13,21},{17,9},{21,13},{10,18... | collective-permute-start | bytes 3538952 | tf_op jit(solution)/shard_map/ppermute | solution.py:62
  156.7 49.4 %collective-permute-start.37 = (bf16[1536,384]{1,0:T(8,128)(2,1)S(1)}, bf16[1536,384]{1,0:T(8,128)(2,1)S(1)}, u32[]{:S(2)}, u32[]{:S(2)}) collective-permute-start(bf16[1536,384]{1,0:T(8,128)(2,1)S(1)} %collective-permute-done.21.refs_4_.refs_3_), channel_id=1, source_target_pairs={{8,0},{12,4},{16,24},{20,28},{9,1},{13,5},{17,25},{21,29},{10,2},{... | collective-permute-start | bytes 3538952 | tf_op jit(solution)/shard_map/ppermute | solution.py:62
  226.6 28.1 %collective-permute-start.46 = (bf16[1536,384]{1,0:T(8,128)(2,1)}, bf16[1536,384]{1,0:T(8,128)(2,1)}, u32[]{:S(2)}, u32[]{:S(2)}) collective-permute-start(bf16[1536,384]{1,0:T(8,128)(2,1)} %get-tuple-element.123), channel_id=1, source_target_pairs={{0,8},{4,12},{24,16},{28,20},{1,9},{5,13},{25,17},{29,21},{2,10},{... | collective-permute-start | bytes 3538952 | tf_op jit(solution)/shard_map/ppermute | solution.py:62
  247.4 41.4 %collective-permute-start.51 = (bf16[1536,384]{1,0:T(8,128)(2,1)}, bf16[1536,384]{1,0:T(8,128)(2,1)}, u32[]{:S(2)}, u32[]{:S(2)}) collective-permute-start(bf16[1536,384]{1,0:T(8,128)(2,1)} %get-tuple-element.130), channel_id=1, source_target_pairs={{0,8},{4,12},{8,0},{12,4},{16,24},{20,28},{24,16},{28,20},{1,9},{5... | collective-permute-start | bytes 3538952 | tf_op jit(solution)/shard_map/ppermute | solution.py:62
  257.3 87.2 %collective-permute-start.52 = (bf16[1536,384]{1,0:T(8,128)(2,1)}, bf16[1536,384]{1,0:T(8,128)(2,1)}, u32[]{:S(2)}, u32[]{:S(2)}) collective-permute-start(bf16[1536,384]{1,0:T(8,128)(2,1)} %add_convert_fusion), channel_id=1, source_target_pairs={{0,16},{4,20},{8,24},{12,28},{16,0},{20,4},{24,8},{28,12},{1,17},{... | collective-permute-start | bytes 3538952 | tf_op jit(solution)/shard_map/ppermute | solution.py:62
  284.5 19.6 %collective-permute-start.48 = (bf16[192,512]{1,0:T(8,128)(2,1)S(1)}, bf16[192,512]{1,0:T(8,128)(2,1)S(1)}, u32[]{:S(2)}, u32[]{:S(2)}) collective-permute-start(bf16[192,512]{1,0:T(8,128)(2,1)S(1)} %get-tuple-element.125), channel_id=1, source_target_pairs={{8,0},{12,4},{16,8},{20,12},{9,1},{13,5},{17,9},{21,13},{10,2},{14... | collective-permute-start | bytes 589832 | tf_op jit(solution)/shard_map/ppermute | solution.py:62
  285.8 58.7 %collective-permute-start.49 = (bf16[192,512]{1,0:T(8,128)(2,1)S(1)}, bf16[192,512]{1,0:T(8,128)(2,1)S(1)}, u32[]{:S(2)}, u32[]{:S(2)}) collective-permute-start(bf16[192,512]{1,0:T(8,128)(2,1)S(1)} %get-tuple-element.126), channel_id=1, source_target_pairs={{16,0},{20,4},{24,8},{28,12},{17,1},{21,5},{25,9},{29,13},{18,2},{... | collective-permute-start | bytes 589832 | tf_op jit(solution)/shard_map/ppermute | solution.py:62
  287.1 57.4 %collective-permute-start.50 = (bf16[192,512]{1,0:T(8,128)(2,1)S(1)}, bf16[192,512]{1,0:T(8,128)(2,1)S(1)}, u32[]{:S(2)}, u32[]{:S(2)}) collective-permute-start(bf16[192,512]{1,0:T(8,128)(2,1)S(1)} %get-tuple-element.127), channel_id=1, source_target_pairs={{24,0},{28,4},{25,1},{29,5},{26,2},{30,6},{27,3},{31,7}} | collective-permute-start | bytes 589832 | tf_op jit(solution)/shard_map/ppermute | solution.py:62
  352.2 27.5 %collective-permute-start.57 = (bf16[512,384]{1,0:T(8,128)(2,1)}, bf16[512,384]{1,0:T(8,128)(2,1)}, u32[]{:S(2)}, u32[]{:S(2)}) collective-permute-start(bf16[512,384]{1,0:T(8,128)(2,1)} %get-tuple-element.140), channel_id=1, source_target_pairs={{0,1},{1,0},{2,3},{3,2},{4,5},{5,4},{6,7},{7,6},{8,9},{9,8},{10,11... | collective-permute-start | bytes 1179656 | tf_op jit(solution)/shard_map/ppermute | solution.py:58
  352.3 28.8 %collective-permute-start.58 = (bf16[512,384]{1,0:T(8,128)(2,1)}, bf16[512,384]{1,0:T(8,128)(2,1)}, u32[]{:S(2)}, u32[]{:S(2)}) collective-permute-start(bf16[512,384]{1,0:T(8,128)(2,1)} %get-tuple-element.141), channel_id=1, source_target_pairs={{0,1},{1,0},{2,3},{3,2},{4,5},{5,4},{6,7},{7,6},{8,9},{9,8},{10,11... | collective-permute-start | bytes 1179656 | tf_op jit(solution)/shard_map/ppermute | solution.py:58
  354.1 21.7 %collective-permute-start.63 = (f32[1,512]{1,0:T(1,128)S(1)}, f32[1,512]{1,0:T(1,128)}, u32[]{:S(2)}, u32[]{:S(2)}) collective-permute-start(f32[1,512]{1,0:T(1,128)S(1)} %add.193), channel_id=1, source_target_pairs={{0,4},{4,0},{8,12},{12,8},{16,20},{20,16},{24,28},{28,24},{1,5},{5... | collective-permute-start | bytes 6152 | tf_op jit(solution)/shard_map/ppermute | solution.py:49
  365.6 21.3 %collective-permute-start.69 = (bf16[576,384]{1,0:T(8,128)(2,1)}, bf16[576,384]{1,0:T(8,128)(2,1)}, u32[]{:S(2)}, u32[]{:S(2)}) collective-permute-start(bf16[576,384]{1,0:T(8,128)(2,1)} %get-tuple-element.148), channel_id=1, source_target_pairs={{0,8},{4,12},{24,16},{28,20},{1,9},{5,13},{25,17},{29,21},{2,10},{... | collective-permute-start | bytes 1327112 | tf_op jit(solution)/shard_map/ppermute | solution.py:62
  379.7 31.1 %collective-permute-start.68 = (bf16[576,384]{1,0:T(8,128)(2,1)}, bf16[576,384]{1,0:T(8,128)(2,1)}, u32[]{:S(2)}, u32[]{:S(2)}) collective-permute-start(bf16[576,384]{1,0:T(8,128)(2,1)} %get-tuple-element.148), channel_id=1, source_target_pairs={{8,16},{12,20},{16,8},{20,12},{9,17},{13,21},{17,9},{21,13},{10,18... | collective-permute-start | bytes 1327112 | tf_op jit(solution)/shard_map/ppermute | solution.py:62
  383.7 27.1 %collective-permute-start.67 = (bf16[576,384]{1,0:T(8,128)(2,1)}, bf16[576,384]{1,0:T(8,128)(2,1)}, u32[]{:S(2)}, u32[]{:S(2)}) collective-permute-start(bf16[576,384]{1,0:T(8,128)(2,1)} %get-tuple-element.147), channel_id=1, source_target_pairs={{0,8},{4,12},{8,0},{12,4},{16,24},{20,28},{24,16},{28,20},{1,9},{5... | collective-permute-start | bytes 1327112 | tf_op jit(solution)/shard_map/ppermute | solution.py:62
  383.7 21.8 %collective-permute-start.59 = (bf16[512,384]{1,0:T(8,128)(2,1)}, bf16[512,384]{1,0:T(8,128)(2,1)}, u32[]{:S(2)}, u32[]{:S(2)}) collective-permute-start(bf16[512,384]{1,0:T(8,128)(2,1)} %select_convert_fusion.1), channel_id=1, source_target_pairs={{0,2},{1,3},{2,0},{3,1},{4,6},{5,7},{6,4},{7,5},{8,10},{9,11},{10,... | collective-permute-start | bytes 1179656 | tf_op jit(solution)/shard_map/ppermute | solution.py:55
  386.9 20.8 %collective-permute-start.55 = (bf16[512,384]{1,0:T(8,128)(2,1)}, bf16[512,384]{1,0:T(8,128)(2,1)}, u32[]{:S(2)}, u32[]{:S(2)}) collective-permute-start(bf16[512,384]{1,0:T(8,128)(2,1)} %select_convert_fusion.2), channel_id=1, source_target_pairs={{0,2},{1,3},{2,0},{3,1},{4,6},{5,7},{6,4},{7,5},{8,10},{9,11},{10,... | collective-permute-start | bytes 1179656 | tf_op jit(solution)/shard_map/ppermute | solution.py:55
  396.7 20.9 %collective-permute-start.70 = (bf16[576,384]{1,0:T(8,128)(2,1)}, bf16[576,384]{1,0:T(8,128)(2,1)}, u32[]{:S(2)}, u32[]{:S(2)}) collective-permute-start(bf16[576,384]{1,0:T(8,128)(2,1)} %add_convert_fusion.1), channel_id=1, source_target_pairs={{0,16},{4,20},{8,24},{12,28},{16,0},{20,4},{24,8},{28,12},{1,17},{... | collective-permute-start | bytes 1327112 | tf_op jit(solution)/shard_map/ppermute | solution.py:62
  409.2 20.3 %collective-permute-start.56 = (bf16[256,384]{1,0:T(8,128)(2,1)S(1)}, bf16[256,384]{1,0:T(8,128)(2,1)S(1)}, u32[]{:S(2)}, u32[]{:S(2)}) collective-permute-start(bf16[256,384]{1,0:T(8,128)(2,1)S(1)} %select_convert_fusion.5), channel_id=1, source_target_pairs={{0,4},{4,0},{8,12},{12,8},{16,20},{20,16},{24,28},{28,24},{1,5},{5... | collective-permute-start | bytes 589832 | tf_op jit(solution)/shard_map/ppermute | solution.py:49
  (121 other events, 1122.8 us)

commit v2 on v1

--- a/solution.py
+++ b/solution.py
@@ -1,3 +1,5 @@
+from functools import partial
+
 import jax
 import jax.numpy as jnp
 from jax import lax
@@ -120,47 +122,55 @@
     return [own, second, far, place.send_z(near, NEAR), middle]
 
 
-def second_scatter(place, started, *earlier):
+def second_scatter(place, started, part, count, *earlier):
     if not place.lined:
         return None
-    second = after(started[1], *earlier)
-    return place.send_z((second.astype(f32) + started[2].astype(f32)).astype(bf16), SECOND)
-
-
-def end_scatter(place, started, second, *earlier):
+    rows, cols = started[1].shape
+    at = slice(part * (rows // count), (part + 1) * (rows // count))
+    (summed,) = call(
+        partial(add_body, rows=at),
+        [((rows // count, cols), bf16)],
+        place.table,
+        [],
+        [started[1:3]],
+        [pltpu.VMEM((rows // count, cols), bf16)] * 2 + [pltpu.SemaphoreType.DMA((2,))],
+        earlier=[started[4]] + list(earlier),
+    )
+    return place.send_z(summed, SECOND)
+
+
+def end_scatter(place, started, seconds, *earlier):
     if not place.lined:
-        return started[0].astype(f32)
-    own, near, middle = after(started[0], *earlier), started[3], started[4]
-    return own.astype(f32) + near.astype(f32) + middle.astype(f32) + second.astype(f32)
-
-
-def reduce_core(place, keep, sends):
-    return [keep[i] + place.swap_c(send).astype(f32) for i, send in enumerate(sends)]
-
-
-def all_sum(place, keep, sends, before_first=(), before_second=()):
-    first, second = reduce_core(place, keep, sends)
-    low = (first.astype(bf16), second.astype(bf16))
+        return started
+    return [after(started[0], *earlier), started[3], started[4]] + list(seconds)
+
+
+def add(left, right):
+    return (left.astype(f32) + right.astype(f32)).astype(bf16)
+
+
+def reduce_core(place, keeps, sends):
+    return [add(keep, place.swap_c(send)) for keep, send in zip(keeps, sends)]
+
+
+def all_sum(place, keeps, sends, before_first=(), before_second=(), before_last=()):
+    low = tuple(reduce_core(place, keeps, sends))
     low = lax.optimization_barrier(low + tuple(before_first))
-    first, second = (
-        first + place.swap_x(low[0]).astype(f32),
-        second + place.swap_y(low[1]).astype(f32),
-    )
-    low = (first.astype(bf16), second.astype(bf16))
+    low = add(low[0], place.swap_x(low[0])), add(low[1], place.swap_y(low[1]))
     low = lax.optimization_barrier(low + tuple(before_second))
-    own = [
-        (first + place.swap_y(low[0]).astype(f32)).astype(bf16),
-        (second + place.swap_x(low[1]).astype(f32)).astype(bf16),
-    ]
+    own = (add(low[0], place.swap_y(low[0])), add(low[1], place.swap_x(low[1])))
+    if before_last:
+        own = lax.optimization_barrier(own + tuple(before_last))[:2]
+    own = list(own)
     return own + [place.swap_c(part) for part in own]
 
 
-def own_sum(place, keep, sends):
-    first, second = reduce_core(place, keep, sends)
+def own_sum(place, keeps, sends):
+    first, second = reduce_core(place, keeps, sends)
     mine, other = jnp.where(place.x == 0, first, second), jnp.where(place.x == 0, second, first)
-    mine = mine + place.swap_x(other.astype(bf16)).astype(f32)
+    mine = add(mine, place.swap_x(other))
     mine, other = part_of(place.y, mine, 0)
-    return mine + place.swap_y(other.astype(bf16)).astype(f32)
+    return mine.astype(f32) + place.swap_y(other).astype(f32)
 
 
 def own_block(place, blocks):
@@ -174,30 +184,48 @@
 ORDER = COUNT + 2
 
 
-def call(body, outs, table, operands, pieces=(), scratch=(), earlier=(), limit=24):
+def call(body, outs, table, operands, pieces=(), scratch=(), earlier=(), held=(), alias=0, limit=24):
     lengths = [len(p) for p in pieces]
     flat = [a for p in pieces for a in p] + list(earlier)
     vmem = pl.BlockSpec(memory_space=pltpu.VMEM)
+    copied = [pltpu.VMEM(a.shape, a.dtype) for a in held]
+    if held:
+        copied.append(pltpu.SemaphoreType.DMA((len(held),)))
 
     def kernel(table_ref, *refs):
         plain, rest = refs[: len(operands)], refs[len(operands) :]
+        sources, rest = rest[: len(held)], rest[len(held) :]
         lists = []
         for length in lengths:
             lists.append(rest[:length])
             rest = rest[length:]
         rest = rest[len(earlier) :]
-        body(table_ref, *plain, *lists, *rest)
+        targets = ()
+        if held:
+            rest, targets = rest[: -len(copied)], rest[-len(copied) :]
+            copies = [
+                pltpu.make_async_copy(source, target, targets[-1].at[i])
+                for i, (source, target) in enumerate(zip(sources, targets))
+            ]
+            for copy in copies:
+                copy.start()
+            for copy in copies:
+                copy.wait()
+        body(table_ref, *plain, *targets[:-1], *lists, *rest)
 
     return pl.pallas_call(
         kernel,
         out_shape=[jax.ShapeDtypeStruct(shape, dtype) for shape, dtype in outs],
         in_specs=[pl.BlockSpec(memory_space=pltpu.SMEM)]
-        + [vmem] * len(operands)
+        + [pl.BlockSpec(memory_space=pl.ANY)] * alias
+        + [vmem] * (len(operands) - alias)
+        + [pl.BlockSpec(memory_space=pltpu.HBM)] * len(held)
         + [pl.BlockSpec(memory_space=pl.ANY)] * len(flat),
-        out_specs=[vmem] * len(outs),
-        scratch_shapes=list(scratch),
+        out_specs=[pl.BlockSpec(memory_space=pl.ANY)] * alias + [vmem] * (len(outs) - alias),
+        scratch_shapes=list(scratch) + copied,
+        input_output_aliases={i + 1: i for i in range(alias)},
         compiler_params=pltpu.CompilerParams(vmem_limit_bytes=limit << 20),
-    )(table, *operands, *flat)
+    )(table, *operands, *held, *flat)
 
 
 def start_pieces(table, pieces, whole, sems, rows=slice(None)):
@@ -232,26 +260,24 @@
     return wait
 
 
-def keep_and_send(table, block_of, keep, sends):
+def keep_and_send(table, block_of, outs):
     core = table[C]
-    for i, send in enumerate(sends):
-        keep[i] = block_of(2 * i + core)
-        send[...] = block_of(2 * i + 1 - core).astype(bf16)
-
-
-def place_rows(table, pieces, whole):
+    for i in range(2):
+        outs[i][...] = block_of(2 * i + core).astype(bf16)
+        outs[2 + i][...] = block_of(2 * i + 1 - core).astype(bf16)
+
+
+def place_rows(table, pieces, raw, grad):
     x, y, c = table[X], table[Y], table[C]
-    tokens = pieces[0].shape[0]
+    tokens = raw.shape[1] // 2
     for dc in range(2):
         for dx in range(2):
             block = 2 * (x + dx - 2 * x * dx) + c + dc - 2 * c * dc
             for dy in range(2):
                 at = pl.ds(pl.multiple_of(tokens * (y + dy - 2 * y * dy), tokens), tokens)
-                whole[block, at, :] = pieces[4 * dc + 2 * dy + dx][...]
-
-
-def grad_body(table, *refs):
-    place_rows(table, refs[:8], refs[8])
+                piece = pieces[4 * dc + 2 * dy + dx]
+                raw[block, at, :] = piece[:tokens]
+                grad[block, at, :] = piece[tokens:]
 
 
 def norm_rows(raw, gain, normed):
@@ -273,8 +299,8 @@
 
 def rows_body(table, *refs):
     gains = refs[8:12]
-    raw, normed, inverse, gain_first, gain_second = refs[12:]
-    place_rows(table, refs[:8], raw)
+    raw, grad, normed, inverse, gain_first, gain_second = refs[12:]
+    place_rows(table, refs[:8], raw, grad)
     x, c = table[X], table[C]
     for dc in range(2):
         for dx in range(2):
@@ -320,7 +346,7 @@
 
 def attend_body(table, query, own, *refs):
     moved, refs = refs[: GROUP - 1], refs[GROUP - 1 :]
-    weights, attended, attended_low, log_total, far, keep, first_send, second_send = refs
+    (weights, attended, attended_low, log_total, far), outs = refs[:5], refs[5:]
     tokens = own.shape[1]
     for place in range(GROUP):
 
@@ -374,13 +400,12 @@
     keep_and_send(
         table,
         lambda b: dims(flipped, weights[b, first:], 1, 0),
-        keep,
-        (first_send, second_send),
+        outs,
     )
 
 
 def hidden_body(
-    table, raw, own_first, own_second, other_first, other_second, gain, hidden, normed, inverse
+    table, own_first, own_second, other_first, other_second, raw, gain, hidden, normed, inverse
 ):
     core = table[C]
     summed, other = (own_first, own_second), (other_first, other_second)
@@ -413,15 +438,9 @@
     pieces,
     active,
     change,
-    keep,
-    first_send,
-    second_send,
-    weights,
-    acc,
-    gate_slope,
-    up_slope,
-    sems,
+    *refs,
 ):
+    outs, (weights, acc, gate_slope, up_slope, sems) = refs[:4], refs[4:]
     wait = start_pieces(table, pieces, weights, sems)
     count, tokens = normed.shape[:2]
     width = acc.shape[1]
@@ -458,12 +477,11 @@
     keep_and_send(
         table,
         lambda b: dims(values, weights[b, :width], 1, 0),
-        keep,
-        (first_send, second_send),
-    )
-
-
-def forward_parts_body(table, active, grad, normed, change, *refs):
+        outs,
+    )
+
+
+def forward_parts_body(table, active, normed, change, grad, *refs):
     parts, flipped = refs[:-1], refs[-1]
     width = change.shape[1]
     flipped[:width] = change[...].T
@@ -483,25 +501,24 @@
     fill(4, flipped.shape[0] // rows - 4, grad)
 
 
-def down_body(table, active, pieces, keep, first_send, second_send, weights, sems):
+def down_body(table, active, pieces, *refs):
+    outs, (weights, sems) = refs[:4], refs[4:]
     rows = weights.shape[1]
     wait = start_pieces(table, pieces, weights, sems, slice(2 * rows, 3 * rows))
     for k in range(weights.shape[0]):
         wait(k)
     values = active[...]
-    keep_and_send(
-        table, lambda b: dims(values, weights[b], 1, 0), keep, (first_send, second_send)
-    )
+    keep_and_send(table, lambda b: dims(values, weights[b], 1, 0), outs)
 
 
 def attend_back_body(
     table,
-    hidden,
-    inverse,
     own_first,
     own_second,
     other_first,
     other_second,
+    hidden,
+    inverse,
     grad,
     gain,
     weights,
@@ -609,20 +626,20 @@
                 sends[k - 1][...] = far_back[:, slot * tokens : (slot + 1) * tokens].astype(bf16)
 
 
-def attend_parts_body(table, query_low, own_low, normed, attended_low, through, *parts):
-    first = query_low.shape[0]
-    second = first + own_low.shape[0]
+def attend_parts_body(table, query_low, through, normed, attended_low, *parts):
+    rows = query_low.shape[0]
     for k, part in enumerate(parts):
         b = table[ORDER + k]
-        part[:first] = dims(query_low[...], normed[b], 1, 0).astype(bf16)
-        part[first:second] = dims(own_low[...], normed[b], 1, 0).astype(bf16)
-        part[second:] = dims(attended_low[...], through[b], 1, 0).astype(bf16)
-
-
-def qkv_back_body(table, own_back, *refs):
-    moved, refs = refs[: GROUP - 1], refs[GROUP - 1 :]
-    query_low, weights, cosine, sine, own, inner = refs[:6]
-    keep, first_send, second_send, inner_first, own_low = refs[6:]
+        part[:rows] = dims(query_low[...], normed[b], 1, 0).astype(bf16)
+        part[-rows:] = dims(attended_low[...], through[b], 1, 0).astype(bf16)
+
+
+def qkv_back_body(table, *refs):
+    count = table.shape[0] - ORDER
+    own_back, moved, refs = refs[count], refs[count + 1 : count + GROUP], refs[count + GROUP :]
+    query_low, inner, weights, cosine, sine, own, normed = refs[:7]
+    parts, outs = refs[7 : 7 + count], refs[7 + count : 11 + count]
+    inner_first, own_low, changed, sems = refs[11 + count :]
     head = HEAD_DIM
     total = own_back[...]
     for part in moved:
@@ -631,14 +648,18 @@
     key = turn(total[:head], cosine[...], -sine[...])
     low = jnp.concatenate([key, total[head:]], axis=0)
     own_low[...] = low.astype(bf16)
+    first = query_low.shape[0]
+    copies = []
+    for k, part in enumerate(parts):
+        changed[k] = dims(own_low[...], normed[table[ORDER + k]], 1, 0).astype(bf16)
+        target = part.at[first : first + low.shape[0]]
+        copies.append(pltpu.make_async_copy(changed.at[k], target, sems.at[k]))
+        copies[k].start()
     flipped = jnp.concatenate([query_low[...].T, low.T.astype(bf16)], axis=1)
     width = flipped.shape[1]
-    keep_and_send(
-        table,
-        lambda b: dims(flipped, weights[b, :width], 1, 0),
-        keep,
-        (first_send, second_send),
-    )
+    keep_and_send(table, lambda b: dims(flipped, weights[b, :width], 1, 0), outs)
+    for copy in copies:
+        copy.wait()
 
 
 def halves_of(table, whole):
@@ -648,41 +669,72 @@
     return jnp.where(flag, low, high), jnp.where(flag, high, low)
 
 
-def split_body(table, matrices, mine_ref, other_ref, *scratch):
+def add_body(table, sources, out, first, second, sems, *, rows):
     copies = [
-        pltpu.make_async_copy(source, held, scratch[-1].at[i])
-        for i, (source, held) in enumerate(zip(matrices, scratch))
+        pltpu.make_async_copy(source.at[rows], held, sems.at[i])
+        for i, (source, held) in enumerate(zip(sources, (first, second)))
     ]
     for copy in copies:
         copy.start()
+    for copy in copies:
+        copy.wait()
+    out[...] = add(first[...], second[...])
+
+
+def pack(rows, packed):
+    half, cols = packed.shape[0], rows.shape[1]
+    packed[:, :cols] = rows[:half].astype(packed.dtype)
+    packed[:, cols:] = rows[half:].astype(packed.dtype)
+
+
+def split_body(table, *refs):
+    matrices, (mine_ref, other_ref) = refs[:-2], refs[-2:]
+    pairs = [halves_of(table, matrix[...].T) for matrix in matrices]
+    pack(jnp.concatenate([mine for mine, _ in pairs], axis=0), mine_ref)
+    pack(jnp.concatenate([other for _, other in pairs], axis=0), other_ref)
+
+
+def piece_body(table, mine_ref, got_ref, piece):
+    flag = table[Y] == 0
+    mine, got = mine_ref[...], got_ref[...]
+    low, high = jnp.where(flag, mine, got), jnp.where(flag, got, mine)
+    half, cols = mine.shape[0], mine.shape[1] // 2
+    for i in range(2):
+        piece[i * half : (i + 1) * half, :cols] = low[:, i * cols : (i + 1) * cols]
+        piece[i * half : (i + 1) * half, cols:] = high[:, i * cols : (i + 1) * cols]
+
+
+def sum_body(table, *refs):
+    parts, (mine_ref, other_ref) = refs[:-2], refs[-2:]
+    whole = [part for part in parts if part.shape == parts[0].shape]
+    total = whole[0][...].astype(f32)
+    for part in whole[1:]:
+        total = total + part[...].astype(f32)
+    rest = [part[...].astype(f32) for part in parts if part.shape != parts[0].shape]
+    if rest:
+        total = total + jnp.concatenate(rest, axis=0)
+    cols = total.shape[1] // 2
+    low, high = total[:, :cols], total[:, cols:]
+    flag = table[Y] == 0
+    pack(jnp.where(flag, low, high), mine_ref)
+    pack(jnp.where(flag, high, low), other_ref)
+
+
+def join_body(table, mine_ref, got_ref, *outs):
+    flag = table[Y] == 0
+    cols = mine_ref.shape[1] // 2
+
+    def unpacked(ref):
+        return jnp.concatenate([ref[:, :cols], ref[:, cols:]], axis=0).astype(f32)
+
+    mine, got = unpacked(mine_ref), unpacked(got_ref)
+    low, high = jnp.where(flag, mine, got), jnp.where(flag, got, mine)
     at = 0
-    for i, copy in enumerate(copies):
-        copy.wait()
-        whole = scratch[i][...]
-        if i < len(copies) - 1:
-            whole = whole.T
-        mine, other = halves_of(table, whole)
-        rows = mine.shape[0]
-        mine_ref[at : at + rows] = mine
-        other_ref[at : at + rows] = other
+    for out in outs:
+        rows = out.shape[1] // 2
+        out[:, :rows] = low[at : at + rows].T
+        out[:, rows:] = high[at : at + rows].T
         at += rows
-
-
-def join_body(table, mine, got, *outs):
-    flag = table[Y] == 0
-    at = 0
-    for i, out in enumerate(outs):
-        turned = i < len(outs) - 1
-        rows = out.shape[1 if turned else 0] // 2
-        parts = mine[at : at + rows].astype(f32), got[at : at + rows].astype(f32)
-        at += rows
-        low, high = jnp.where(flag, parts[0], parts[1]), jnp.where(flag, parts[1], parts[0])
-        if turned:
-            out[:, :rows] = low.T
-            out[:, rows:] = high.T
-        else:
-            out[:rows] = low
-            out[rows:] = high
 
 
 def rope_tables(positions, half):
@@ -715,35 +767,32 @@
     kv_rows = key_matrix.shape[1]
     qkv_cols = query_rows + kv_rows
     full = (ny, tokens, width)
-    wide = [((2,) + full[1:], f32), (full[1:], bf16), (full[1:], bf16)]
-
-    def halves(*matrices):
-        rows = sum(max(m.shape) for m in matrices) // 2
-        cols = min(matrices[0].shape)
-        return call(
-            split_body,
-            [((rows, cols), bf16)] * 2,
-            table,
-            [],
-            [matrices],
-            [pltpu.VMEM(m.shape, bf16) for m in matrices]
-            + [pltpu.SemaphoreType.DMA((len(matrices),))],
-        )
+    wide = [(full[1:], bf16)] * 4
+
+    def halves(*matrices, earlier=()):
+        rows = sum(m.shape[1] for m in matrices) // 2
+        packed = (rows // 2, 2 * matrices[0].shape[0])
+        return call(split_body, [(packed, bf16)] * 2, table, [], held=matrices, earlier=earlier)
 
     def whole_piece(mine, got):
-        return jnp.concatenate(pair(y, mine, got), axis=1)
-
-    def spread(value):
+        rows, cols = mine.shape
+        (piece,) = call(piece_body, [((2 * rows, cols), bf16)], table, [mine, got])
+        return piece
+
+    def spread(value, *before_y):
         by_x = place.swap_x(value)
-        four = [value, by_x, place.swap_y(value), place.swap_y(by_x)]
+        late, late_x = lax.optimization_barrier((value, by_x) + before_y)[:2]
+        four = [value, by_x, place.swap_y(late), place.swap_y(late_x)]
         return four + [place.swap_c(r) for r in four]
 
-    mine, other = halves(query_weight, key_matrix, value_matrix, out_weight)
+    mine, other = halves(query_weight, key_matrix, value_matrix, out_weight.T)
     attend_got = place.swap_y(other)
     attend_piece = whole_piece(mine, attend_got)
-    input_rows = spread(after(layer_in, other))
-    mine, other = halves(gate_weight, up_weight, down_weight)
-    forward_piece = whole_piece(mine, place.swap_y(after(other, attend_got, input_rows[3])))
+    mine, other = halves(gate_weight, up_weight, down_weight.T, earlier=[attend_got])
+    forward_got = place.swap_y(other)
+    forward_piece = whole_piece(mine, forward_got)
+    rows = jnp.concatenate([layer_in, out_grad], axis=0)
+    input_rows = spread(after(rows, attend_got), forward_got)
     if lined:
         attend_pieces = gather_pieces(place, attend_piece)
         forward_pieces = gather_pieces(place, after(forward_piece, *attend_pieces[1:]), True)
@@ -757,9 +806,9 @@
     gains = jnp.stack([first_gain, second_gain])
     two = [gains, place.swap_x(gains)]
     gains = two + [place.swap_c(g) for g in two]
-    raw, normed_in, inverse_in, gain_in, gain_mid = call(
+    raw, grad, normed_in, inverse_in, gain_in, gain_mid = call(
         rows_body,
-        [(full, bf16)] * 2 + [((tokens, 1), f32)] + [((ny, 1, width), f32)] * 2,
+        [(full, bf16)] * 3 + [((tokens, 1), f32)] + [((ny, 1, width), f32)] * 2,
         table,
         input_rows + gains,
     )
@@ -782,8 +831,7 @@
         )
         for k in range(1, GROUP)
     ]
-    (grad,) = call(grad_body, [(full, bf16)], table, spread(after(out_grad, query)))
-    attended, attended_low, log_total, far, keep, *sends = call(
+    attended, attended_low, log_total, far, *halves_out = call(
         attend_body,
         [
             ((query_rows, tokens), f32),
@@ -795,34 +843,45 @@
         table,
         [query, own] + moved + [attend_weights],
     )
-    summed = all_sum(place, keep, sends, [forward_pieces[len(forward_pieces) // 2]])
+    summed = all_sum(
+        place,
+        halves_out[:2],
+        halves_out[2:],
+        before_first=forward_pieces[1:3] if lined else forward_pieces,
+        before_last=forward_pieces[3:],
+    )
 
     hidden, normed_mid, inverse_mid = call(
         hidden_body,
         [(full, f32), (full, bf16), ((tokens, 1), f32)],
         table,
-        [raw] + summed + [gain_mid],
-    )
-    active, change, keep, *sends = call(
+        summed,
+        held=[raw, gain_mid],
+    )
+    active, change, *halves_out = call(
         forward_body,
         [((tokens, hidden_dev), bf16), ((tokens, 2 * hidden_dev), bf16)] + wide,
         table,
-        [normed_mid, grad],
+        [normed_mid],
         [forward_pieces],
         [pltpu.VMEM(forward_shape, bf16), pltpu.VMEM((tokens, 2 * hidden_dev), f32)]
         + [pltpu.VMEM((tokens, hidden_dev), f32)] * 2
         + [sems],
+        held=[grad],
     )
     forward_parts = call(
         forward_parts_body,
         [(forward_shape[1:], bf16)] * ny,
         table,
-        [active, grad, normed_mid, change],
+        [active, normed_mid, change],
+        held=[grad],
         scratch=[pltpu.VMEM(forward_shape[1:2] + (tokens,), bf16)],
     )
     forward_started = start_scatter(place, forward_parts)
-    summed = all_sum(place, keep, sends, before_second=forward_parts[:1])
-    forward_second = second_scatter(place, forward_started, summed[-1])
+    summed = all_sum(
+        place, halves_out[:2], halves_out[2:], before_second=forward_parts[:1]
+    )
+    forward_second = second_scatter(place, forward_started, 0, 2, summed[-1])
     hidden_own = own_block(place, hidden)
     through, pull, query_low, own_back, *returns, inner_first = call(
         attend_back_body,
@@ -835,9 +894,10 @@
         + [((kv_rows, tokens), bf16)] * (GROUP - 1)
         + [((1, tokens), f32)],
         table,
-        [hidden, inverse_mid]
-        + summed
-        + [
+        summed,
+        held=[
+            hidden,
+            inverse_mid,
             grad,
             gain_mid,
             attend_weights,
@@ -874,30 +934,38 @@
         )
         for k in range(1, GROUP)
     ]
-    keep, *sends, inner, own_low = call(
-        qkv_back_body,
-        wide + [((1, tokens), f32), ((kv_rows, tokens), bf16)],
-        table,
-        [own_back] + moved + [query_low, attend_weights, cosine, sine, own, inner_first],
-        earlier=forward_started[3:4] + ([forward_second] if lined else []),
-    )
     attend_parts = call(
         attend_parts_body,
         [(attend_shape[1:], bf16)] * ny,
         table,
-        [query_low, own_low, normed_in, attended_low, through],
-    )
+        [query_low, through],
+        held=[normed_in, attended_low],
+    )
+    results = call(
+        qkv_back_body,
+        [(attend_shape[1:], bf16)] * ny
+        + wide
+        + [((1, tokens), f32), ((kv_rows, tokens), bf16)],
+        table,
+        list(attend_parts) + [own_back] + moved + [query_low, inner_first],
+        held=[attend_weights, cosine, sine, own, normed_in],
+        scratch=[pltpu.VMEM((ny, kv_rows, width), bf16), sems],
+        earlier=forward_started[3:4] + ([forward_second] if lined else []),
+        alias=ny,
+    )
+    attend_parts, first_halves, (inner, own_low) = results[:ny], results[ny:-2], results[-2:]
     attend_started = start_scatter(place, attend_parts)
-    if lined:
-        attend_second = second_scatter(place, attend_started, forward_second)
-    else:
-        attend_second = None
-    forward_grad = end_scatter(place, forward_started, forward_second, own_low)
-    attend_grad = end_scatter(place, attend_started, attend_second, own_low)
+    forward_seconds = [
+        forward_second,
+        second_scatter(place, forward_started, 1, 2, summed[-1], moved[0]),
+    ]
+    attend_second = second_scatter(place, attend_started, 0, 1)
+    forward_grad = end_scatter(place, forward_started, forward_seconds, own_low)
+    attend_grad = end_scatter(place, attend_started, [attend_second], own_low)
     inner = inner + place.swap_c(inner)
     inner = inner + place.swap_x(inner)
     inner = inner + place.swap_y(inner)
-    first_own = own_sum(place, keep, sends)
+    first_own = own_sum(place, first_halves[:2], first_halves[2:])
     input_own = layer_in.astype(f32)
     inverse_own, _ = part_of(y, inverse_in, 0)
     scaled = first_own * first_gain[None, :]
@@ -912,30 +980,30 @@
         terms = terms + place.swap_gx(terms, bit)
         bit *= 2
 
-    keep, *sends = call(
+    down_halves = call(
         down_body,
         wide,
         table,
-        [active],
+        [],
         [forward_pieces],
         [pltpu.VMEM((ny, hidden_dev, width), bf16), sems],
         earlier=[own_low],
-    )
-    layer_out = (hidden_own + own_sum(place, keep, sends)).astype(bf16)
-
-    def joined(summed_part, outs):
-        mine, other = part_of(y, summed_part, 1)
-        got = place.swap_y(other.astype(bf16))
+        held=[active],
+    )
+    layer_out = (hidden_own + own_sum(place, down_halves[:2], down_halves[2:])).astype(bf16)
+
+    def joined(parts, outs):
+        rows, cols = parts[0].shape
+        packed = (rows // 2, cols)
+        mine, other = call(sum_body, [(packed, f32), (packed, bf16)], table, parts)
+        shapes = [(cols // 2, inner) for inner in outs]
         return call(
-            join_body,
-            [(m.shape, f32) for m in outs],
-            table,
-            [mine, got],
+            join_body, [(s, f32) for s in shapes], table, [mine, place.swap_y(other)]
         )
 
-    gate_grad, up_grad, down_grad = joined(forward_grad, (gate_weight, up_weight, down_weight))
+    gate_grad, up_grad, down_grad = joined(forward_grad, [2 * hidden_dev] * 3)
     query_out, key_out, value_out, out_out = joined(
-        attend_grad, (query_weight, key_matrix, value_matrix, out_weight)
+        attend_grad, [2 * query_rows, kv_rows, kv_rows, 2 * query_rows]
     )
     return (
         layer_out,
@@ -944,11 +1012,11 @@
         query_out,
         key_out,
         value_out,
-        out_out,
+        out_out.T,
         terms[1],
         gate_grad,
         up_grad,
-        down_grad,
+        down_grad.T,
     )
 
 

time: 438 us -> 365 us (0.83)
  waiting for transfers between devices: 204 us -> 178 us
  local copies, waits for them, and re-layouts: 44.8 us -> 20.6 us
  starting transfers between devices: 96.9 us -> 77.2 us
  other arithmetic: 33.5 us -> 15.2 us
  Pallas kernels: 55.4 us -> 71.1 us
    ppermute x22 -> x23, waiting for transfers between devices: 142 us -> 117 us  [send_z(): return lax.ppermute(value, 'gx', pairs)]
    ppermute x22 -> x23, starting transfers between devices: 65.8 us -> 42.9 us  [send_z(): return lax.ppermute(value, 'gx', pairs)]
    pallas_call x15 -> x21, Pallas kernels: 55.4 us -> 71.1 us  [call(): pl.pallas_call(kernel, out_shape=[jax.ShapeDtypeStruct(shape, dtype) for...]
    unnamed x165 -> x169, local copies, waits for them, and re-layouts: 35.1 us -> 19.8 us
    convert_element_type x14 -> x13, other arithmetic: 13.6 us -> 5.07 us  [the longest x12 3.29 us: add(): return (left.astype(f32) + right.astype(f32)).astype(bf16)]
    add x4 -> x0, other arithmetic: 7.48 us -> none  [the longest x2 4.57 us: end_scatter(): own.astype(f32) + near.astype(f32) + middle.astype(f32) + second.astype(f32)]
    ppermute x18 -> x16, starting transfers between devices: 15.5 us -> 20.5 us  [swap_gx(): return lax.ppermute(value, 'gx', [(i, i ^ bit) for i in range(self.nx)])]
    ppermute x18 -> x16, waiting for transfers between devices: 38 us -> 43 us  [swap_gx(): return lax.ppermute(value, 'gx', [(i, i ^ bit) for i in range(self.nx)])]
  transfers between devices with their start and end apart: 73 -> 67, of which waited for: 39 -> 31; matrix products, arithmetic and copies ran while one was open for 11% -> 4% of each run, Pallas kernels for 9% -> 13%
where the time goes in v2:
time: 365 us; the launch traced here: 364 us
  waiting for transfers between devices  178 us (49%)
  starting transfers between devices  77.2 us (21%)
  Pallas kernels  71.1 us (19%)
  local copies, waits for them, and re-layouts  20.6 us (6%)
  other arithmetic  15.2 us (4%)
    ppermute x23, waiting for transfers between devices, send_z(): return lax.ppermute(value, 'gx', pairs)  117 us
    pallas_call x21, Pallas kernels, call(): pl.pallas_call(kernel, out_shape=[jax.ShapeDtypeStruct(shape, dtype) for...  71.1 us
    ppermute x16, waiting for transfers between devices, swap_gx(): return lax.ppermute(value, 'gx', [(i, i ^ bit) for i in range(self.nx)])  43 us
    ppermute x23, starting transfers between devices, send_z(): return lax.ppermute(value, 'gx', pairs)  42.9 us
    ppermute x16, starting transfers between devices, swap_gx(): return lax.ppermute(value, 'gx', [(i, i ^ bit) for i in range(self.nx)])  20.5 us
    unnamed x169, local copies, waits for them, and re-layouts  19.8 us
    ppermute x9, waiting for transfers between devices, swap_x(): return lax.ppermute(value, 'gy', [(i, i ^ 2) for i in range(self.ny)])  11.5 us
    ppermute x9, starting transfers between devices, swap_x(): return lax.ppermute(value, 'gy', [(i, i ^ 2) for i in range(self.ny)])  9.82 us
  transfers between devices with their start and end apart: 67, of which 31 were waited for; matrix products, arithmetic and copies ran while one was open for 4% of the time, Pallas kernels for 13%

profile of v2, /device:TPU:0, one launch (start us, length us, event | category | flops | bytes accessed | tf_op | source)
XLA Modules:
  0.0 364.5 jit_solution(4828969825454398674)
XLA Ops:
  6.0 3.0 collective-permute-start
  9.0 5.4 %collective-permute-done.refs_3_.refs_1_ = bf16[288,384]{1,0:T(8,128)(2,1)S(1)} collective-permute-done((bf16[288,384]{1,0:T(8,128)(2,1)S(1)}, bf16[288,384]{1,0:T(8,128)(2,1)S(1)}, u32[]{:S(2)}, u32[]{:S(2)}) %collective-permute-start) | collective-permute-done | bytes 221216 | tf_op jit(solution)/shard_map/ppermute | solution.py:51
  23.5 2.7 collective-permute-start.13
  36.6 9.0 %collective-permute-done.13.refs_5_ = bf16[576,384]{1,0:T(8,128)(2,1)S(1)} collective-permute-done((bf16[576,384]{1,0:T(8,128)(2,1)S(1)}, bf16[576,384]{1,0:T(8,128)(2,1)S(1)}, u32[]{:S(2)}, u32[]{:S(2)}) %collective-permute-start.13) | collective-permute-done | bytes 442400 | tf_op jit(solution)/shard_map/ppermute | solution.py:64
  47.6 6.2 %collective-permute-done.4.refs_3_ = bf16[512,384]{1,0:T(8,128)(2,1)S(1)} collective-permute-done((bf16[512,384]{1,0:T(8,128)(2,1)S(1)}, bf16[512,384]{1,0:T(8,128)(2,1)S(1)}, u32[]{:S(2)}, u32[]{:S(2)}) %collective-permute-start.4) | collective-permute-done | bytes 393248 | tf_op jit(solution)/shard_map/ppermute | solution.py:51
  53.9 3.4 collective-permute-done.15.refs_7_
  66.5 3.3 shard_map.198
  74.4 42.5 %collective-permute-done.16.refs_2_ = bf16[192,512]{1,0:T(8,128)(2,1)S(1)} collective-permute-done((bf16[192,512]{1,0:T(8,128)(2,1)S(1)}, bf16[192,512]{1,0:T(8,128)(2,1)S(1)}, u32[]{:S(2)}, u32[]{:S(2)}) %collective-permute-start.16) | collective-permute-done | bytes 196640 | tf_op jit(solution)/shard_map/ppermute | solution.py:64
  116.9 4.3 %collective-permute-done.17.refs_3_ = bf16[192,512]{1,0:T(8,128)(2,1)S(1)} collective-permute-done((bf16[192,512]{1,0:T(8,128)(2,1)S(1)}, bf16[192,512]{1,0:T(8,128)(2,1)S(1)}, u32[]{:S(2)}, u32[]{:S(2)}) %collective-permute-start.17) | collective-permute-done | bytes 196640 | tf_op jit(solution)/shard_map/ppermute | solution.py:64
  121.2 3.7 %collective-permute-done.18.refs_4_ = bf16[192,512]{1,0:T(8,128)(2,1)S(1)} collective-permute-done((bf16[192,512]{1,0:T(8,128)(2,1)S(1)}, bf16[192,512]{1,0:T(8,128)(2,1)S(1)}, u32[]{:S(2)}, u32[]{:S(2)}) %collective-permute-start.18) | collective-permute-done | bytes 196640 | tf_op jit(solution)/shard_map/ppermute | solution.py:64
  124.9 5.2 %shard_map.199 = (f32[192,512]{1,0:T(8,128)S(1)}, bf16[192,512]{1,0:T(8,128)(2,1)S(1)}, f32[2,1,512]{2,1,0:T(1,128)S(1)}, bf16[192,1024]{1,0:T(8,128)(2,1)S(1)},...) custom-call(s32[11]{0:T(128)S(1)} %concatenate.6.table_ref, ...), custom_call_target="tpu_custom_call" | custom-call | tf_op jit(solution)/shard_map/pallas_call | solution.py:216
  135.8 8.1 %collective-permute-done.24 = bf16[512,384]{1,0:T(8,128)(2,1)S(1)} collective-permute-done((bf16[512,384]{1,0:T(8,128)(2,1)S(1)}, bf16[512,384]{1,0:T(8,128)(2,1)S(1)}, u32[]{:S(2)}, u32[]{:S(2)}) %collective-permute-start.24) | collective-permute-done | bytes 393248 | tf_op jit(solution)/shard_map/ppermute | solution.py:51
  146.3 8.2 %collective-permute-done.26 = bf16[512,384]{1,0:T(8,128)(2,1)S(1)} collective-permute-done((bf16[512,384]{1,0:T(8,128)(2,1)S(1)}, bf16[512,384]{1,0:T(8,128)(2,1)S(1)}, u32[]{:S(2)}, u32[]{:S(2)}) %collective-permute-start.26) | collective-permute-done | bytes 393248 | tf_op jit(solution)/shard_map/ppermute | solution.py:57
  154.8 13.5 %collective-permute-done.28.refs_6_.refs_5_ = bf16[1536,384]{1,0:T(8,128)(2,1)S(1)} collective-permute-done((bf16[1536,384]{1,0:T(8,128)(2,1)S(1)}, bf16[1536,384]{1,0:T(8,128)(2,1)S(1)}, u32[]{:S(2)}, u32[]{:S(2)}) %collective-permute-start.28) | collective-permute-done | bytes 1179680 | tf_op jit(solution)/shard_map/ppermute | solution.py:64
  174.3 10.2 %shard_map.202 = (bf16[512,512]{1,0:T(8,128)(2,1)S(1)}, bf16[512,1024]{1,0:T(8,128)(2,1)S(1)}, bf16[512,384]{1,0:T(8,128)(2,1)S(1)}, bf16[512,384]{1,0:T(8,128)(...) custom-call(s32[11]{0:T(128)S(1)} %concatenate.6.table_ref, ...), custom_call_target="tpu_custom_call" | custom-call | tf_op jit(solution)/shard_map/pallas_call | solution.py:216
  190.1 6.4 %shard_map.203 = (bf16[1536,384]{1,0:T(8,128)(2,1)S(1)}, bf16[1536,384]{1,0:T(8,128)(2,1)S(1)}, bf16[1536,384]{1,0:T(8,128)(2,1)S(1)}, bf16[1536,384]{1,0:T(8,128)(2,1)}) custom-call(s32[11]{0:T(128)S(1)} %concatenate.6.table_ref, bf16[512,512]{1,0:T(8,128)(2,1)S(1)} %get-tuple-element.126.refs_0_, ...), custom_call_target="tpu_custom_call" | custom-call | tf_op jit(solution)/shard_map/pallas_call | solution.py:216
  196.5 3.4 collective-permute-start.39
  204.5 7.9 %collective-permute-done.35 = bf16[512,384]{1,0:T(8,128)(2,1)} collective-permute-done((bf16[512,384]{1,0:T(8,128)(2,1)}, bf16[512,384]{1,0:T(8,128)(2,1)}, u32[]{:S(2)}, u32[]{:S(2)}) %collective-permute-start.35) | collective-permute-done | bytes 393248 | tf_op jit(solution)/shard_map/ppermute | solution.py:51
  215.3 10.4 %collective-permute-done.39.refs_16_.refs_1_ = bf16[1536,384]{1,0:T(8,128)(2,1)} collective-permute-done((bf16[1536,384]{1,0:T(8,128)(2,1)}, bf16[1536,384]{1,0:T(8,128)(2,1)}, u32[]{:S(2)}, u32[]{:S(2)}) %collective-permute-start.39) | collective-permute-done | bytes 1179680 | tf_op jit(solution)/shard_map/ppermute | solution.py:64
  227.7 4.1 %collective-permute-start.45 = (bf16[768,384]{1,0:T(8,128)(2,1)S(1)}, bf16[768,384]{1,0:T(8,128)(2,1)S(1)}, u32[]{:S(2)}, u32[]{:S(2)}) collective-permute-start(bf16[768,384]{1,0:T(8,128)(2,1)S(1)} %shard_map.206), channel_id=1, source_target_pairs={{0,16},{4,20},{8,24},{12,28},{16,0},{20,4},{24,8},{28,12},{1,17},{... | collective-permute-start | bytes 1769480 | tf_op jit(solution)/shard_map/ppermute | solution.py:64
  232.9 10.3 %shard_map.204 = (bf16[4,512,384]{2,1,0:T(8,128)(2,1)S(1)}, f32[512,1]{1,0:T(8,128)S(1)}, bf16[192,512]{1,0:T(8,128)(2,1)S(1)}, f32[192,512]{1,0:T(8,128)S(1)}, ...) custom-call(s32[11]{0:T(128)S(1)} %concatenate.6.table_ref, ...), custom_call_target="tpu_custom_call" | custom-call | tf_op jit(solution)/shard_map/pallas_call | solution.py:216
  247.3 2.7 shard_map.205
  253.1 21.8 %collective-permute-done.42.refs_6_ = bf16[192,512]{1,0:T(8,128)(2,1)S(1)} collective-permute-done((bf16[192,512]{1,0:T(8,128)(2,1)S(1)}, bf16[192,512]{1,0:T(8,128)(2,1)S(1)}, u32[]{:S(2)}, u32[]{:S(2)}) %collective-permute-start.42) | collective-permute-done | bytes 196640 | tf_op jit(solution)/shard_map/ppermute | solution.py:64
  275.0 5.5 %shard_map.207 = (bf16[576,384]{1,0:T(8,128)(2,1)S(1)}, bf16[576,384]{1,0:T(8,128)(2,1)}, bf16[576,384]{1,0:T(8,128)(2,1)S(1)}, bf16[576,384]{1,0:T(8,128)(2,1)}...) custom-call(s32[11]{0:T(128)S(1)} %concatenate.6.table_ref, ...), custom_call_target="tpu_custom_call", output_to_operand_aliasing={{0}: (1, {}), {1}: (2, {}), {2}: (3, {}), {3}: (4, {})} | custom-call | tf_op jit(solution)/shard_map/pallas_call | solution.py:216
  289.8 3.0 shard_map.212
  298.2 7.4 %collective-permute-start.62 = (bf16[576,384]{1,0:T(8,128)(2,1)}, bf16[576,384]{1,0:T(8,128)(2,1)}, u32[]{:S(2)}, u32[]{:S(2)}) collective-permute-start(bf16[576,384]{1,0:T(8,128)(2,1)} %get-tuple-element.171), channel_id=1, source_target_pairs={{0,8},{4,12},{24,16},{28,20},{1,9},{5,13},{25,17},{29,21},{2,10},{... | collective-permute-start | bytes 1327112 | tf_op jit(solution)/shard_map/ppermute | solution.py:64
  312.7 5.6 %collective-permute-done.65.refs_4_ = bf16[768,384]{1,0:T(8,128)(2,1)} collective-permute-done((bf16[768,384]{1,0:T(8,128)(2,1)}, bf16[768,384]{1,0:T(8,128)(2,1)}, u32[]{:S(2)}, u32[]{:S(2)}) %collective-permute-start.65) | collective-permute-done | bytes 589856 | tf_op jit(solution)/shard_map/ppermute | solution.py:64
  329.7 2.9 collective-permute-start.63
  332.6 10.9 %collective-permute-done.53 = bf16[256,384]{1,0:T(8,128)(2,1)S(1)} collective-permute-done((bf16[256,384]{1,0:T(8,128)(2,1)S(1)}, bf16[256,384]{1,0:T(8,128)(2,1)S(1)}, u32[]{:S(2)}, u32[]{:S(2)}) %collective-permute-start.53) | collective-permute-done | bytes 196640 | tf_op jit(solution)/shard_map/ppermute | solution.py:51
  346.6 2.8 collective-permute-done.57
  350.7 2.7 shard_map.214
  356.5 3.4 collective-permute-start.59
  (338 shorter events, 122.6 us)
Async XLA Ops:
  19.3 14.6 %collective-permute-start.2 = (bf16[768,384]{1,0:T(8,128)(2,1)S(1)}, bf16[768,384]{1,0:T(8,128)(2,1)S(1)}, u32[]{:S(2)}, u32[]{:S(2)}) collective-permute-start(bf16[768,384]{1,0:T(8,128)(2,1)S(1)} %get-tuple-element.100), channel_id=1, source_target_pairs={{0,4},{4,0},{8,12},{12,8},{16,20},{20,16},{24,28},{28,24},{1,5},{5... | collective-permute-start | bytes 1769480 | tf_op jit(solution)/shard_map/ppermute | solution.py:51
  23.5 22.1 %collective-permute-start.13 = (bf16[576,384]{1,0:T(8,128)(2,1)S(1)}, bf16[576,384]{1,0:T(8,128)(2,1)S(1)}, u32[]{:S(2)}, u32[]{:S(2)}) collective-permute-start(bf16[576,384]{1,0:T(8,128)(2,1)S(1)} %shard_map.197.refs_3_), channel_id=1, source_target_pairs={{0,16},{4,20},{8,24},{12,28},{16,0},{20,4},{24,8},{28,12},{1,17},{... | collective-permute-start | bytes 1327112 | tf_op jit(solution)/shard_map/ppermute | solution.py:64
  26.1 20.8 %collective-permute-start.12 = (bf16[576,384]{1,0:T(8,128)(2,1)S(1)}, bf16[576,384]{1,0:T(8,128)(2,1)S(1)}, u32[]{:S(2)}, u32[]{:S(2)}) collective-permute-start(bf16[576,384]{1,0:T(8,128)(2,1)S(1)} %shard_map.197.refs_3_), channel_id=1, source_target_pairs={{0,8},{4,12},{8,0},{12,4},{16,24},{20,28},{24,16},{28,20},{1,9},{5... | collective-permute-start | bytes 1327112 | tf_op jit(solution)/shard_map/ppermute | solution.py:64
  27.7 19.3 %collective-permute-start.14 = (bf16[576,384]{1,0:T(8,128)(2,1)S(1)}, bf16[576,384]{1,0:T(8,128)(2,1)S(1)}, u32[]{:S(2)}, u32[]{:S(2)}) collective-permute-start(bf16[576,384]{1,0:T(8,128)(2,1)S(1)} %shard_map.197.refs_3_), channel_id=1, source_target_pairs={{8,16},{12,20},{16,8},{20,12},{9,17},{13,21},{17,9},{21,13},{10,18... | collective-permute-start | bytes 1327112 | tf_op jit(solution)/shard_map/ppermute | solution.py:64
  35.3 18.5 %collective-permute-start.4 = (bf16[512,384]{1,0:T(8,128)(2,1)S(1)}, bf16[512,384]{1,0:T(8,128)(2,1)S(1)}, u32[]{:S(2)}, u32[]{:S(2)}) collective-permute-start(bf16[512,384]{1,0:T(8,128)(2,1)S(1)} %collective-permute-done.1.refs_1_), channel_id=1, source_target_pairs={{0,4},{4,0},{8,12},{12,8},{16,20},{20,16},{24,28},{28,24},{1,5},{5... | collective-permute-start | bytes 1179656 | tf_op jit(solution)/shard_map/ppermute | solution.py:51
  46.9 14.2 %collective-permute-start.5 = (bf16[512,384]{1,0:T(8,128)(2,1)S(1)}, bf16[512,384]{1,0:T(8,128)(2,1)S(1)}, u32[]{:S(2)}, u32[]{:S(2)}) collective-permute-start(bf16[512,384]{1,0:T(8,128)(2,1)S(1)} %pad_maximum_fusion.refs_0_), channel_id=1, source_target_pairs={{0,1},{1,0},{2,3},{3,2},{4,5},{5,4},{6,7},{7,6},{8,9},{9,8},{10,11... | collective-permute-start | bytes 1179656 | tf_op jit(solution)/shard_map/ppermute | solution.py:60
  47.0 17.0 %collective-permute-start.6 = (bf16[512,384]{1,0:T(8,128)(2,1)S(1)}, bf16[512,384]{1,0:T(8,128)(2,1)S(1)}, u32[]{:S(2)}, u32[]{:S(2)}) collective-permute-start(bf16[512,384]{1,0:T(8,128)(2,1)S(1)} %collective-permute-done.1.refs_1_), channel_id=1, source_target_pairs={{0,1},{1,0},{2,3},{3,2},{4,5},{5,4},{6,7},{7,6},{8,9},{9,8},{10,11... | collective-permute-start | bytes 1179656 | tf_op jit(solution)/shard_map/ppermute | solution.py:60
  47.5 16.5 %collective-permute-start.7 = (bf16[512,384]{1,0:T(8,128)(2,1)S(1)}, bf16[512,384]{1,0:T(8,128)(2,1)S(1)}, u32[]{:S(2)}, u32[]{:S(2)}) collective-permute-start(bf16[512,384]{1,0:T(8,128)(2,1)S(1)} %collective-permute-done.3.refs_2_), channel_id=1, source_target_pairs={{0,1},{1,0},{2,3},{3,2},{4,5},{5,4},{6,7},{7,6},{8,9},{9,8},{10,11... | collective-permute-start | bytes 1179656 | tf_op jit(solution)/shard_map/ppermute | solution.py:60
  58.5 74.1 %collective-permute-start.22 = (bf16[1536,384]{1,0:T(8,128)(2,1)S(1)}, bf16[1536,384]{1,0:T(8,128)(2,1)S(1)}, u32[]{:S(2)}, u32[]{:S(2)}) collective-permute-start(bf16[1536,384]{1,0:T(8,128)(2,1)S(1)} %shard_map.200.refs_2_.refs_1_), channel_id=1, source_target_pairs={{0,16},{4,20},{8,24},{12,28},{16,0},{20,4},{24,8},{28,12},{1,17},{... | collective-permute-start | bytes 3538952 | tf_op jit(solution)/shard_map/ppermute | solution.py:64
  61.1 71.5 %collective-permute-start.21 = (bf16[1536,384]{1,0:T(8,128)(2,1)S(1)}, bf16[1536,384]{1,0:T(8,128)(2,1)S(1)}, u32[]{:S(2)}, u32[]{:S(2)}) collective-permute-start(bf16[1536,384]{1,0:T(8,128)(2,1)S(1)} %shard_map.200.refs_2_.refs_1_), channel_id=1, source_target_pairs={{0,8},{4,12},{8,0},{12,4},{16,24},{20,28},{24,16},{28,20},{1,9},{5... | collective-permute-start | bytes 3538952 | tf_op jit(solution)/shard_map/ppermute | solution.py:64
  69.9 47.1 %collective-permute-start.16 = (bf16[192,512]{1,0:T(8,128)(2,1)S(1)}, bf16[192,512]{1,0:T(8,128)(2,1)S(1)}, u32[]{:S(2)}, u32[]{:S(2)}) collective-permute-start(bf16[192,512]{1,0:T(8,128)(2,1)S(1)} %get-tuple-element.106.refs_1_.refs_10_.refs_13_), channel_id=1, source_target_pairs={{0,8},{4,12},{8,16},{12,20},{1,9},{5,13},{9,17},{13,21},{2,10},{6,... | collective-permute-start | bytes 589832 | tf_op jit(solution)/shard_map/ppermute | solution.py:64
  71.8 49.4 %collective-permute-start.17 = (bf16[192,512]{1,0:T(8,128)(2,1)S(1)}, bf16[192,512]{1,0:T(8,128)(2,1)S(1)}, u32[]{:S(2)}, u32[]{:S(2)}) collective-permute-start(bf16[192,512]{1,0:T(8,128)(2,1)S(1)} %get-tuple-element.106.refs_1_.refs_10_.refs_13_), channel_id=1, source_target_pairs={{0,16},{4,20},{8,24},{12,28},{1,17},{5,21},{9,25},{13,29},{2,18},{... | collective-permute-start | bytes 589832 | tf_op jit(solution)/shard_map/ppermute | solution.py:64
  73.1 51.7 %collective-permute-start.18 = (bf16[192,512]{1,0:T(8,128)(2,1)S(1)}, bf16[192,512]{1,0:T(8,128)(2,1)S(1)}, u32[]{:S(2)}, u32[]{:S(2)}) collective-permute-start(bf16[192,512]{1,0:T(8,128)(2,1)S(1)} %get-tuple-element.106.refs_1_.refs_10_.refs_13_), channel_id=1, source_target_pairs={{0,24},{4,28},{1,25},{5,29},{2,26},{6,30},{3,27},{7,31}} | collective-permute-start | bytes 589832 | tf_op jit(solution)/shard_map/ppermute | solution.py:64
  133.7 21.1 %collective-permute-start.27 = (bf16[1536,384]{1,0:T(8,128)(2,1)S(1)}, bf16[1536,384]{1,0:T(8,128)(2,1)S(1)}, u32[]{:S(2)}, u32[]{:S(2)}) collective-permute-start(bf16[1536,384]{1,0:T(8,128)(2,1)S(1)} %shard_map.200.refs_2_.refs_1_), channel_id=1, source_target_pairs={{8,16},{12,20},{16,8},{20,12},{9,17},{13,21},{17,9},{21,13},{10,18... | collective-permute-start | bytes 3538952 | tf_op jit(solution)/shard_map/ppermute | solution.py:64
  134.5 33.8 %collective-permute-start.28 = (bf16[1536,384]{1,0:T(8,128)(2,1)S(1)}, bf16[1536,384]{1,0:T(8,128)(2,1)S(1)}, u32[]{:S(2)}, u32[]{:S(2)}) collective-permute-start(bf16[1536,384]{1,0:T(8,128)(2,1)S(1)} %collective-permute-done.22.refs_4_.refs_3_), channel_id=1, source_target_pairs={{8,0},{12,4},{16,24},{20,28},{9,1},{13,5},{17,25},{21,29},{10,2},{... | collective-permute-start | bytes 3538952 | tf_op jit(solution)/shard_map/ppermute | solution.py:64
  196.5 29.1 %collective-permute-start.39 = (bf16[1536,384]{1,0:T(8,128)(2,1)}, bf16[1536,384]{1,0:T(8,128)(2,1)}, u32[]{:S(2)}, u32[]{:S(2)}) collective-permute-start(bf16[1536,384]{1,0:T(8,128)(2,1)} %get-tuple-element.141), channel_id=1, source_target_pairs={{0,8},{4,12},{24,16},{28,20},{1,9},{5,13},{25,17},{29,21},{2,10},{... | collective-permute-start | bytes 3538952 | tf_op jit(solution)/shard_map/ppermute | solution.py:64
  200.0 25.7 %collective-permute-start.40 = (bf16[1536,384]{1,0:T(8,128)(2,1)}, bf16[1536,384]{1,0:T(8,128)(2,1)S(1)}, u32[]{:S(2)}, u32[]{:S(2)}) collective-permute-start(bf16[1536,384]{1,0:T(8,128)(2,1)} %get-tuple-element.141), channel_id=1, source_target_pairs={{8,16},{12,20},{16,8},{20,12},{9,17},{13,21},{17,9},{21,13},{10,18... | collective-permute-start | bytes 3538952 | tf_op jit(solution)/shard_map/ppermute | solution.py:64
  202.8 48.1 %collective-permute-start.44 = (bf16[1536,384]{1,0:T(8,128)(2,1)}, bf16[1536,384]{1,0:T(8,128)(2,1)S(1)}, u32[]{:S(2)}, u32[]{:S(2)}) collective-permute-start(bf16[1536,384]{1,0:T(8,128)(2,1)} %copy-done.67), channel_id=1, source_target_pairs={{0,8},{4,12},{8,0},{12,4},{16,24},{20,28},{24,16},{28,20},{1,9},{5... | collective-permute-start | bytes 3538952 | tf_op jit(solution)/shard_map/ppermute | solution.py:64
  214.8 17.0 %collective-permute-start.37 = (bf16[512,384]{1,0:T(8,128)(2,1)S(1)}, bf16[512,384]{1,0:T(8,128)(2,1)S(1)}, u32[]{:S(2)}, u32[]{:S(2)}) collective-permute-start(bf16[512,384]{1,0:T(8,128)(2,1)S(1)} %get-tuple-element.191.refs_0_), channel_id=1, source_target_pairs={{0,1},{1,0},{2,3},{3,2},{4,5},{5,4},{6,7},{7,6},{8,9},{9,8},{10,11... | collective-permute-start | bytes 1179656 | tf_op jit(solution)/shard_map/ppermute | solution.py:60
  227.7 47.3 %collective-permute-start.45 = (bf16[768,384]{1,0:T(8,128)(2,1)S(1)}, bf16[768,384]{1,0:T(8,128)(2,1)S(1)}, u32[]{:S(2)}, u32[]{:S(2)}) collective-permute-start(bf16[768,384]{1,0:T(8,128)(2,1)S(1)} %shard_map.206), channel_id=1, source_target_pairs={{0,16},{4,20},{8,24},{12,28},{16,0},{20,4},{24,8},{28,12},{1,17},{... | collective-permute-start | bytes 1769480 | tf_op jit(solution)/shard_map/ppermute | solution.py:64
  244.4 30.5 %collective-permute-start.42 = (bf16[192,512]{1,0:T(8,128)(2,1)S(1)}, bf16[192,512]{1,0:T(8,128)(2,1)S(1)}, u32[]{:S(2)}, u32[]{:S(2)}) collective-permute-start(bf16[192,512]{1,0:T(8,128)(2,1)S(1)} %get-tuple-element.151), channel_id=1, source_target_pairs={{16,0},{20,4},{24,8},{28,12},{17,1},{21,5},{25,9},{29,13},{18,2},{... | collective-permute-start | bytes 589832 | tf_op jit(solution)/shard_map/ppermute | solution.py:64
  245.7 29.2 %collective-permute-start.43 = (bf16[192,512]{1,0:T(8,128)(2,1)S(1)}, bf16[192,512]{1,0:T(8,128)(2,1)S(1)}, u32[]{:S(2)}, u32[]{:S(2)}) collective-permute-start(bf16[192,512]{1,0:T(8,128)(2,1)S(1)} %get-tuple-element.152), channel_id=1, source_target_pairs={{24,0},{28,4},{25,1},{29,5},{26,2},{30,6},{27,3},{31,7}} | collective-permute-start | bytes 589832 | tf_op jit(solution)/shard_map/ppermute | solution.py:64
  292.8 25.5 %collective-permute-start.65 = (bf16[768,384]{1,0:T(8,128)(2,1)}, bf16[768,384]{1,0:T(8,128)(2,1)}, u32[]{:S(2)}, u32[]{:S(2)}) collective-permute-start(bf16[768,384]{1,0:T(8,128)(2,1)} %shard_map.212), channel_id=1, source_target_pairs={{0,16},{4,20},{8,24},{12,28},{16,0},{20,4},{24,8},{28,12},{1,17},{... | collective-permute-start | bytes 1769480 | tf_op jit(solution)/shard_map/ppermute | solution.py:64
  292.9 18.4 %collective-permute-start.56 = (f32[1,512]{1,0:T(1,128)S(1)}, f32[1,512]{1,0:T(1,128)S(1)}, u32[]{:S(2)}, u32[]{:S(2)}) collective-permute-start(f32[1,512]{1,0:T(1,128)S(1)} %add.168), channel_id=1, source_target_pairs={{0,4},{4,0},{8,12},{12,8},{16,20},{20,16},{24,28},{28,24},{1,5},{5... | collective-permute-start | bytes 6152 | tf_op jit(solution)/shard_map/ppermute | solution.py:51
  295.9 26.0 %collective-permute-start.52 = (bf16[512,384]{1,0:T(8,128)(2,1)}, bf16[512,384]{1,0:T(8,128)(2,1)}, u32[]{:S(2)}, u32[]{:S(2)}) collective-permute-start(bf16[512,384]{1,0:T(8,128)(2,1)} %broadcast_select_fusion), channel_id=1, source_target_pairs={{0,2},{1,3},{2,0},{3,1},{4,6},{5,7},{6,4},{7,5},{8,10},{9,11},{10,... | collective-permute-start | bytes 1179656 | tf_op jit(solution)/shard_map/ppermute | solution.py:57
  297.5 28.6 %collective-permute-start.61 = (bf16[576,384]{1,0:T(8,128)(2,1)}, bf16[576,384]{1,0:T(8,128)(2,1)S(1)}, u32[]{:S(2)}, u32[]{:S(2)}) collective-permute-start(bf16[576,384]{1,0:T(8,128)(2,1)} %get-tuple-element.171), channel_id=1, source_target_pairs={{8,16},{12,20},{16,8},{20,12},{9,17},{13,21},{17,9},{21,13},{10,18... | collective-permute-start | bytes 1327112 | tf_op jit(solution)/shard_map/ppermute | solution.py:64
  298.2 29.5 %collective-permute-start.62 = (bf16[576,384]{1,0:T(8,128)(2,1)}, bf16[576,384]{1,0:T(8,128)(2,1)}, u32[]{:S(2)}, u32[]{:S(2)}) collective-permute-start(bf16[576,384]{1,0:T(8,128)(2,1)} %get-tuple-element.171), channel_id=1, source_target_pairs={{0,8},{4,12},{24,16},{28,20},{1,9},{5,13},{25,17},{29,21},{2,10},{... | collective-permute-start | bytes 1327112 | tf_op jit(solution)/shard_map/ppermute | solution.py:64
  311.4 42.0 %collective-permute-start.60 = (bf16[576,384]{1,0:T(8,128)(2,1)}, bf16[576,384]{1,0:T(8,128)(2,1)}, u32[]{:S(2)}, u32[]{:S(2)}) collective-permute-start(bf16[576,384]{1,0:T(8,128)(2,1)} %get-tuple-element.170), channel_id=1, source_target_pairs={{0,8},{4,12},{8,0},{12,4},{16,24},{20,28},{24,16},{28,20},{1,9},{5... | collective-permute-start | bytes 1327112 | tf_op jit(solution)/shard_map/ppermute | solution.py:64
  323.8 26.9 %collective-permute-start.66 = (bf16[768,384]{1,0:T(8,128)(2,1)S(1)}, bf16[768,384]{1,0:T(8,128)(2,1)S(1)}, u32[]{:S(2)}, u32[]{:S(2)}) collective-permute-start(bf16[768,384]{1,0:T(8,128)(2,1)S(1)} %get-tuple-element.181), channel_id=1, source_target_pairs={{0,4},{4,0},{8,12},{12,8},{16,20},{20,16},{24,28},{28,24},{1,5},{5... | collective-permute-start | bytes 1769480 | tf_op jit(solution)/shard_map/ppermute | solution.py:51
  324.4 19.1 %collective-permute-start.53 = (bf16[256,384]{1,0:T(8,128)(2,1)S(1)}, bf16[256,384]{1,0:T(8,128)(2,1)S(1)}, u32[]{:S(2)}, u32[]{:S(2)}) collective-permute-start(bf16[256,384]{1,0:T(8,128)(2,1)S(1)} %broadcast_select_fusion.3), channel_id=1, source_target_pairs={{0,4},{4,0},{8,12},{12,8},{16,20},{20,16},{24,28},{28,24},{1,5},{5... | collective-permute-start | bytes 589832 | tf_op jit(solution)/shard_map/ppermute | solution.py:51
  326.2 20.2 %collective-permute-start.48 = (bf16[512,384]{1,0:T(8,128)(2,1)S(1)}, bf16[512,384]{1,0:T(8,128)(2,1)S(1)}, u32[]{:S(2)}, u32[]{:S(2)}) collective-permute-start(bf16[512,384]{1,0:T(8,128)(2,1)S(1)} %broadcast_select_fusion.2), channel_id=1, source_target_pairs={{0,2},{1,3},{2,0},{3,1},{4,6},{5,7},{6,4},{7,5},{8,10},{9,11},{10,... | collective-permute-start | bytes 1179656 | tf_op jit(solution)/shard_map/ppermute | solution.py:57
  329.7 23.7 %collective-permute-start.63 = (bf16[576,384]{1,0:T(8,128)(2,1)S(1)}, bf16[576,384]{1,0:T(8,128)(2,1)S(1)}, u32[]{:S(2)}, u32[]{:S(2)}) collective-permute-start(bf16[576,384]{1,0:T(8,128)(2,1)S(1)} %shard_map.209), channel_id=1, source_target_pairs={{0,16},{4,20},{8,24},{12,28},{16,0},{20,4},{24,8},{28,12},{1,17},{... | collective-permute-start | bytes 1327112 | tf_op jit(solution)/shard_map/ppermute | solution.py:64
  (119 other events, 1286.5 us)

commit v3 on v2

--- a/solution.py
+++ b/solution.py
@@ -124,7 +124,7 @@
 
 def second_scatter(place, started, part, count, *earlier):
     if not place.lined:
-        return None
+        return None, None
     rows, cols = started[1].shape
     at = slice(part * (rows // count), (part + 1) * (rows // count))
     (summed,) = call(
@@ -136,7 +136,7 @@
         [pltpu.VMEM((rows // count, cols), bf16)] * 2 + [pltpu.SemaphoreType.DMA((2,))],
         earlier=[started[4]] + list(earlier),
     )
-    return place.send_z(summed, SECOND)
+    return summed, place.send_z(summed, SECOND)
 
 
 def end_scatter(place, started, seconds, *earlier):
@@ -165,10 +165,13 @@
     return own + [place.swap_c(part) for part in own]
 
 
-def own_sum(place, keeps, sends):
+def own_sum(place, keeps, sends, before_x=(), before_y=()):
     first, second = reduce_core(place, keeps, sends)
+    if before_x:
+        first, second = lax.optimization_barrier((first, second) + tuple(before_x))[:2]
     mine, other = jnp.where(place.x == 0, first, second), jnp.where(place.x == 0, second, first)
     mine = add(mine, place.swap_x(other))
+    mine = after(mine, *before_y) if before_y else mine
     mine, other = part_of(place.y, mine, 0)
     return mine.astype(f32) + place.swap_y(other).astype(f32)
 
@@ -440,8 +443,12 @@
     change,
     *refs,
 ):
-    outs, (weights, acc, gate_slope, up_slope, sems) = refs[:4], refs[4:]
-    wait = start_pieces(table, pieces, weights, sems)
+    outs, (down, weights, acc, gate_slope, up_slope, sems, down_sems) = refs[:4], refs[4:]
+    split = weights.shape[1]
+    wait = start_pieces(table, pieces, weights, sems, slice(0, split))
+    down_wait = start_pieces(
+        table, pieces, down, down_sems, slice(split, split + down.shape[1])
+    )
     count, tokens = normed.shape[:2]
     width = acc.shape[1]
     half = width // 2
@@ -467,8 +474,10 @@
 
     lax.fori_loop(0, 4, part, 0)
 
-    def back(b, total):
-        return total + dims(grad[b], weights[b, width:], 1, 1)
+    def back(k, total):
+        b = table[ORDER + k]
+        down_wait(k)
+        return total + dims(grad[b], down[b], 1, 1)
 
     slope = lax.fori_loop(0, count, back, jnp.zeros((tokens, half), f32))
     change[:, :half] = (slope * gate_slope[...]).astype(bf16)
@@ -481,32 +490,32 @@
     )
 
 
-def forward_parts_body(table, active, normed, change, grad, *refs):
-    parts, flipped = refs[:-1], refs[-1]
+def forward_third_body(table, active, normed, change, grad, third, both):
     width = change.shape[1]
-    flipped[:width] = change[...].T
-    flipped[width:] = active[...].T
-    rows = width // 4
+    both[:width] = change[...].T
+    both[width:] = active[...].T
+    b = table[ORDER + 3]
+    third[:width] = dims(both[:width], normed[b], 1, 0).astype(bf16)
+    third[width:] = dims(both[width:], grad[b], 1, 0).astype(bf16)
+
+
+def forward_parts_body(table, both, normed, grad, *parts):
+    rows = both.shape[0] // 6
 
     def fill(first, count, source):
         def one(i, _):
             at = pl.ds(pl.multiple_of((first + i) * rows, rows), rows)
             for k, part in enumerate(parts):
-                part[at] = dims(flipped[at], source[table[ORDER + k]], 1, 0).astype(bf16)
+                part[at] = dims(both[at], source[table[ORDER + k]], 1, 0).astype(bf16)
             return 0
 
         lax.fori_loop(0, count, one, 0)
 
     fill(0, 4, normed)
-    fill(4, flipped.shape[0] // rows - 4, grad)
-
-
-def down_body(table, active, pieces, *refs):
-    outs, (weights, sems) = refs[:4], refs[4:]
-    rows = weights.shape[1]
-    wait = start_pieces(table, pieces, weights, sems, slice(2 * rows, 3 * rows))
-    for k in range(weights.shape[0]):
-        wait(k)
+    fill(4, 2, grad)
+
+
+def down_body(table, active, weights, *outs):
     values = active[...]
     keep_and_send(table, lambda b: dims(values, weights[b], 1, 0), outs)
 
@@ -788,11 +797,11 @@
     mine, other = halves(query_weight, key_matrix, value_matrix, out_weight.T)
     attend_got = place.swap_y(other)
     attend_piece = whole_piece(mine, attend_got)
-    mine, other = halves(gate_weight, up_weight, down_weight.T, earlier=[attend_got])
+    mine, other = halves(gate_weight, up_weight, down_weight.T, earlier=[attend_piece])
     forward_got = place.swap_y(other)
     forward_piece = whole_piece(mine, forward_got)
     rows = jnp.concatenate([layer_in, out_grad], axis=0)
-    input_rows = spread(after(rows, attend_got), forward_got)
+    input_rows = spread(after(rows, attend_piece), forward_got)
     if lined:
         attend_pieces = gather_pieces(place, attend_piece)
         forward_pieces = gather_pieces(place, after(forward_piece, *attend_pieces[1:]), True)
@@ -858,30 +867,49 @@
         summed,
         held=[raw, gain_mid],
     )
-    active, change, *halves_out = call(
+    active, change, *halves_out, down_whole = call(
         forward_body,
-        [((tokens, hidden_dev), bf16), ((tokens, 2 * hidden_dev), bf16)] + wide,
+        [((tokens, hidden_dev), bf16), ((tokens, 2 * hidden_dev), bf16)]
+        + wide
+        + [((ny, hidden_dev, width), bf16)],
         table,
         [normed_mid],
         [forward_pieces],
-        [pltpu.VMEM(forward_shape, bf16), pltpu.VMEM((tokens, 2 * hidden_dev), f32)]
+        [
+            pltpu.VMEM((ny, 2 * hidden_dev, width), bf16),
+            pltpu.VMEM((tokens, 2 * hidden_dev), f32),
+        ]
         + [pltpu.VMEM((tokens, hidden_dev), f32)] * 2
-        + [sems],
+        + [sems, sems],
+        held=[grad],
+    )
+    third, both = call(
+        forward_third_body,
+        [(forward_shape[1:], bf16), (forward_shape[1:2] + (tokens,), bf16)],
+        table,
+        [active, normed_mid, change],
         held=[grad],
     )
     forward_parts = call(
         forward_parts_body,
-        [(forward_shape[1:], bf16)] * ny,
-        table,
-        [active, normed_mid, change],
+        [(forward_shape[1:], bf16)] * 3,
+        table,
+        [both, normed_mid],
         held=[grad],
-        scratch=[pltpu.VMEM(forward_shape[1:2] + (tokens,), bf16)],
-    )
+    )
+    forward_parts = list(forward_parts) + [third]
     forward_started = start_scatter(place, forward_parts)
+    down_halves = call(
+        down_body, wide, table, [active, down_whole], earlier=[forward_parts[0]]
+    )
     summed = all_sum(
-        place, halves_out[:2], halves_out[2:], before_second=forward_parts[:1]
-    )
-    forward_second = second_scatter(place, forward_started, 0, 2, summed[-1])
+        place,
+        halves_out[:2],
+        halves_out[2:],
+        before_second=forward_parts[:1],
+        before_last=list(down_halves[:1]) + forward_started[2:3] + forward_started[4:],
+    )
+    _, forward_second = second_scatter(place, forward_started, 0, 2, summed[-1])
     hidden_own = own_block(place, hidden)
     through, pull, query_low, own_back, *returns, inner_first = call(
         attend_back_body,
@@ -916,6 +944,8 @@
             pltpu.VMEM((query_rows, tokens), bf16),
         ],
     )
+    down_sends = lax.optimization_barrier(tuple(down_halves[2:]) + (through,))[:2]
+    layer_out = (hidden_own + own_sum(place, down_halves[:2], down_sends)).astype(bf16)
     inverse_own, _ = part_of(y, inverse_mid, 0)
     pull_own, _ = part_of(y, pull, 0)
     mid_own = jnp.where(place.x == 0, summed[0], summed[1])
@@ -953,19 +983,27 @@
         earlier=forward_started[3:4] + ([forward_second] if lined else []),
         alias=ny,
     )
-    attend_parts, first_halves, (inner, own_low) = results[:ny], results[ny:-2], results[-2:]
+    attend_parts, first_halves = results[:ny], results[ny:-2]
+    inner, own_low = results[-2:]
     attend_started = start_scatter(place, attend_parts)
     forward_seconds = [
         forward_second,
-        second_scatter(place, forward_started, 1, 2, summed[-1], moved[0]),
+        second_scatter(place, forward_started, 1, 2, summed[-1], moved[0])[1],
     ]
-    attend_second = second_scatter(place, attend_started, 0, 1)
-    forward_grad = end_scatter(place, forward_started, forward_seconds, own_low)
+    attend_sent, attend_second = second_scatter(place, attend_started, 0, 1)
     attend_grad = end_scatter(place, attend_started, [attend_second], own_low)
     inner = inner + place.swap_c(inner)
     inner = inner + place.swap_x(inner)
     inner = inner + place.swap_y(inner)
-    first_own = own_sum(place, first_halves[:2], first_halves[2:])
+    first_own = own_sum(
+        place,
+        first_halves[:2],
+        first_halves[2:],
+        before_y=[attend_sent] if lined else [],
+    )
+    forward_grad = end_scatter(
+        place, forward_started, forward_seconds, *([attend_sent] if lined else [])
+    )
     input_own = layer_in.astype(f32)
     inverse_own, _ = part_of(y, inverse_in, 0)
     scaled = first_own * first_gain[None, :]
@@ -979,18 +1017,6 @@
     while bit < place.nx:
         terms = terms + place.swap_gx(terms, bit)
         bit *= 2
-
-    down_halves = call(
-        down_body,
-        wide,
-        table,
-        [],
-        [forward_pieces],
-        [pltpu.VMEM((ny, hidden_dev, width), bf16), sems],
-        earlier=[own_low],
-        held=[active],
-    )
-    layer_out = (hidden_own + own_sum(place, down_halves[:2], down_halves[2:])).astype(bf16)
 
     def joined(parts, outs):
         rows, cols = parts[0].shape

time: 365 us -> 356 us (0.975)
  local copies, waits for them, and re-layouts: 20.6 us -> 9.37 us
  waiting for transfers between devices: 178 us -> 183 us
  Pallas kernels: 71.1 us -> 66.4 us
    unnamed x169 -> x115, local copies, waits for them, and re-layouts: 19.8 us -> 8.53 us
    pallas_call x21 -> x22, Pallas kernels: 71.1 us -> 66.4 us  [call(): pl.pallas_call(kernel, out_shape=[jax.ShapeDtypeStruct(shape, dtype) for...]
    ppermute x23, starting transfers between devices: 42.9 us -> 46.9 us  [send_z(): return lax.ppermute(value, 'gx', pairs)]
    ppermute x23, waiting for transfers between devices: 117 us -> 121 us  [send_z(): return lax.ppermute(value, 'gx', pairs)]
  transfers between devices with their start and end apart: 67 -> 67, of which waited for: 31 -> 37; matrix products, arithmetic and copies ran while one was open for 4% -> 5% of each run, Pallas kernels for 13% -> 12%
where the time goes in v3:
time: 356 us; the launch traced here: 355 us
  waiting for transfers between devices  183 us (51%)
  starting transfers between devices  77.2 us (22%)
  Pallas kernels  66.4 us (19%)
  other arithmetic  17.2 us (5%)
  local copies, waits for them, and re-layouts  9.37 us (3%)
    ppermute x23, waiting for transfers between devices, send_z(): return lax.ppermute(value, 'gx', pairs)  121 us
    pallas_call x22, Pallas kernels, call(): pl.pallas_call(kernel, out_shape=[jax.ShapeDtypeStruct(shape, dtype) for...  66.4 us
    ppermute x23, starting transfers between devices, send_z(): return lax.ppermute(value, 'gx', pairs)  46.9 us
    ppermute x16, waiting for transfers between devices, swap_gx(): return lax.ppermute(value, 'gx', [(i, i ^ bit) for i in range(self.nx)])  40.2 us
    ppermute x16, starting transfers between devices, swap_gx(): return lax.ppermute(value, 'gx', [(i, i ^ bit) for i in range(self.nx)])  17.3 us
    ppermute x9, waiting for transfers between devices, swap_x(): return lax.ppermute(value, 'gy', [(i, i ^ 2) for i in range(self.ny)])  15.1 us
    ppermute x9, starting transfers between devices, swap_x(): return lax.ppermute(value, 'gy', [(i, i ^ 2) for i in range(self.ny)])  9.05 us
    unnamed x115, local copies, waits for them, and re-layouts  8.53 us
  transfers between devices with their start and end apart: 67, of which 37 were waited for; matrix products, arithmetic and copies ran while one was open for 5% of the time, Pallas kernels for 12%

profile of v3, /device:TPU:0, one launch (start us, length us, event | category | flops | bytes accessed | tf_op | source)
XLA Modules:
  0.0 354.9 jit_solution(16113484801379410741)
XLA Ops:
  6.2 3.0 collective-permute-start
  9.2 5.4 %collective-permute-done.refs_1_ = bf16[288,384]{1,0:T(8,128)(2,1)S(1)} collective-permute-done((bf16[288,384]{1,0:T(8,128)(2,1)S(1)}, bf16[288,384]{1,0:T(8,128)(2,1)S(1)}, u32[]{:S(2)}, u32[]{:S(2)}) %collective-permute-start) | collective-permute-done | bytes 221216 | tf_op jit(solution)/shard_map/ppermute | solution.py:51
  20.7 2.6 collective-permute-start.13
  25.6 3.3 collective-permute-done.1.refs_1_
  34.5 8.2 %collective-permute-done.13.refs_5_ = bf16[576,384]{1,0:T(8,128)(2,1)S(1)} collective-permute-done((bf16[576,384]{1,0:T(8,128)(2,1)S(1)}, bf16[576,384]{1,0:T(8,128)(2,1)S(1)}, u32[]{:S(2)}, u32[]{:S(2)}) %collective-permute-start.13) | collective-permute-done | bytes 442400 | tf_op jit(solution)/shard_map/ppermute | solution.py:64
  44.8 7.0 %collective-permute-done.4.refs_3_ = bf16[512,384]{1,0:T(8,128)(2,1)S(1)} collective-permute-done((bf16[512,384]{1,0:T(8,128)(2,1)S(1)}, bf16[512,384]{1,0:T(8,128)(2,1)S(1)}, u32[]{:S(2)}, u32[]{:S(2)}) %collective-permute-start.4) | collective-permute-done | bytes 393248 | tf_op jit(solution)/shard_map/ppermute | solution.py:51
  51.9 2.6 collective-permute-done.15.refs_7_
  55.6 5.1 %collective-permute-start.22 = (bf16[1536,384]{1,0:T(8,128)(2,1)S(1)}, bf16[1536,384]{1,0:T(8,128)(2,1)S(1)}, u32[]{:S(2)}, u32[]{:S(2)}) collective-permute-start(bf16[1536,384]{1,0:T(8,128)(2,1)S(1)} %shard_map.200.refs_2_), channel_id=1, source_target_pairs={{0,16},{4,20},{8,24},{12,28},{16,0},{20,4},{24,8},{28,12},{1,17},{... | collective-permute-start | bytes 3538952 | tf_op jit(solution)/shard_map/ppermute | solution.py:64
  61.2 2.4 shard_map.197
  63.6 3.3 shard_map.198
  71.5 40.0 %collective-permute-done.16.refs_2_ = bf16[192,512]{1,0:T(8,128)(2,1)S(1)} collective-permute-done((bf16[192,512]{1,0:T(8,128)(2,1)S(1)}, bf16[192,512]{1,0:T(8,128)(2,1)S(1)}, u32[]{:S(2)}, u32[]{:S(2)}) %collective-permute-start.16) | collective-permute-done | bytes 196640 | tf_op jit(solution)/shard_map/ppermute | solution.py:64
  111.5 4.3 %collective-permute-done.17.refs_3_ = bf16[192,512]{1,0:T(8,128)(2,1)S(1)} collective-permute-done((bf16[192,512]{1,0:T(8,128)(2,1)S(1)}, bf16[192,512]{1,0:T(8,128)(2,1)S(1)}, u32[]{:S(2)}, u32[]{:S(2)}) %collective-permute-start.17) | collective-permute-done | bytes 196640 | tf_op jit(solution)/shard_map/ppermute | solution.py:64
  115.8 3.9 %collective-permute-done.18.refs_4_ = bf16[192,512]{1,0:T(8,128)(2,1)S(1)} collective-permute-done((bf16[192,512]{1,0:T(8,128)(2,1)S(1)}, bf16[192,512]{1,0:T(8,128)(2,1)S(1)}, u32[]{:S(2)}, u32[]{:S(2)}) %collective-permute-start.18) | collective-permute-done | bytes 196640 | tf_op jit(solution)/shard_map/ppermute | solution.py:64
  119.7 5.2 %shard_map.199 = (f32[192,512]{1,0:T(8,128)S(1)}, bf16[192,512]{1,0:T(8,128)(2,1)S(1)}, f32[2,1,512]{2,1,0:T(1,128)S(1)}, bf16[192,1024]{1,0:T(8,128)(2,1)S(1)},...) custom-call(s32[11]{0:T(128)S(1)} %concatenate.6.table_ref, ...), custom_call_target="tpu_custom_call" | custom-call | tf_op jit(solution)/shard_map/pallas_call | solution.py:219
  131.3 7.3 %collective-permute-done.23 = bf16[512,384]{1,0:T(8,128)(2,1)S(1)} collective-permute-done((bf16[512,384]{1,0:T(8,128)(2,1)S(1)}, bf16[512,384]{1,0:T(8,128)(2,1)S(1)}, u32[]{:S(2)}, u32[]{:S(2)}) %collective-permute-start.23) | collective-permute-done | bytes 393248 | tf_op jit(solution)/shard_map/ppermute | solution.py:57
  141.0 8.2 %collective-permute-done.25 = bf16[512,384]{1,0:T(8,128)(2,1)S(1)} collective-permute-done((bf16[512,384]{1,0:T(8,128)(2,1)S(1)}, bf16[512,384]{1,0:T(8,128)(2,1)S(1)}, u32[]{:S(2)}, u32[]{:S(2)}) %collective-permute-start.25) | collective-permute-done | bytes 393248 | tf_op jit(solution)/shard_map/ppermute | solution.py:51
  150.2 16.2 %collective-permute-done.28.refs_6_ = bf16[1536,384]{1,0:T(8,128)(2,1)S(1)} collective-permute-done((bf16[1536,384]{1,0:T(8,128)(2,1)S(1)}, bf16[1536,384]{1,0:T(8,128)(2,1)S(1)}, u32[]{:S(2)}, u32[]{:S(2)}) %collective-permute-start.28) | collective-permute-done | bytes 1179680 | tf_op jit(solution)/shard_map/ppermute | solution.py:64
  170.7 10.3 %shard_map.202 = (bf16[512,512]{1,0:T(8,128)(2,1)S(1)}, bf16[512,1024]{1,0:T(8,128)(2,1)S(1)}, bf16[512,384]{1,0:T(8,128)(2,1)S(1)}, bf16[512,384]{1,0:T(8,128)(...) custom-call(s32[11]{0:T(128)S(1)} %concatenate.6.table_ref, ...), custom_call_target="tpu_custom_call" | custom-call | tf_op jit(solution)/shard_map/pallas_call | solution.py:219
  191.4 4.1 %shard_map.204 = (bf16[1536,384]{1,0:T(8,128)(2,1)S(1)}, bf16[1536,384]{1,0:T(8,128)(2,1)S(1)}, bf16[1536,384]{1,0:T(8,128)(2,1)S(1)}) custom-call(s32[11]{0:T(128)S(1)} %concatenate.6.table_ref, bf16[1536,512]{1,0:T(8,128)(2,1)S(1)} %get-tuple-element.134.refs_0_, bf16[4,512,384]{2,1,0:T(8,128)(2,1)S(1)} %get-tuple-element.129.refs_0_.refs_1_, ...), custom_call_target="tpu_custom_call" | custom-call | tf_op jit(solution)/shard_map/pallas_call | solution.py:219
  202.1 4.0 %collective-permute-done.35 = bf16[512,384]{1,0:T(8,128)(2,1)S(1)} collective-permute-done((bf16[512,384]{1,0:T(8,128)(2,1)S(1)}, bf16[512,384]{1,0:T(8,128)(2,1)S(1)}, u32[]{:S(2)}, u32[]{:S(2)}) %collective-permute-start.35) | collective-permute-done | bytes 393248 | tf_op jit(solution)/shard_map/ppermute | solution.py:51
  207.5 9.5 %collective-permute-done.37.refs_16_.refs_1_ = bf16[1536,384]{1,0:T(8,128)(2,1)S(1)} collective-permute-done((bf16[1536,384]{1,0:T(8,128)(2,1)S(1)}, bf16[1536,384]{1,0:T(8,128)(2,1)S(1)}, u32[]{:S(2)}, u32[]{:S(2)}) %collective-permute-start.37) | collective-permute-done | bytes 1179680 | tf_op jit(solution)/shard_map/ppermute | solution.py:64
  219.7 4.2 %collective-permute-start.49 = (bf16[768,384]{1,0:T(8,128)(2,1)S(1)}, bf16[768,384]{1,0:T(8,128)(2,1)S(1)}, u32[]{:S(2)}, u32[]{:S(2)}) collective-permute-start(bf16[768,384]{1,0:T(8,128)(2,1)S(1)} %shard_map.208), channel_id=1, source_target_pairs={{0,16},{4,20},{8,24},{12,28},{16,0},{20,4},{24,8},{28,12},{1,17},{... | collective-permute-start | bytes 1769480 | tf_op jit(solution)/shard_map/ppermute | solution.py:64
  223.9 10.3 %shard_map.206 = (bf16[4,512,384]{2,1,0:T(8,128)(2,1)S(1)}, f32[512,1]{1,0:T(8,128)S(1)}, bf16[192,512]{1,0:T(8,128)(2,1)S(1)}, f32[192,512]{1,0:T(8,128)S(1)}, ...) custom-call(s32[11]{0:T(128)S(1)} %concatenate.6.table_ref, ...), custom_call_target="tpu_custom_call" | custom-call | tf_op jit(solution)/shard_map/pallas_call | solution.py:219
  238.3 2.4 shard_map.207
  242.3 4.7 %collective-permute-done.45.refs_5_.refs_4_ = bf16[192,512]{1,0:T(8,128)(2,1)S(1)} collective-permute-done((bf16[192,512]{1,0:T(8,128)(2,1)S(1)}, bf16[192,512]{1,0:T(8,128)(2,1)S(1)}, u32[]{:S(2)}, u32[]{:S(2)}) %collective-permute-start.45) | collective-permute-done | bytes 196640 | tf_op jit(solution)/shard_map/ppermute | solution.py:64
  247.0 20.0 %collective-permute-done.46.refs_6_ = bf16[192,512]{1,0:T(8,128)(2,1)S(1)} collective-permute-done((bf16[192,512]{1,0:T(8,128)(2,1)S(1)}, bf16[192,512]{1,0:T(8,128)(2,1)S(1)}, u32[]{:S(2)}, u32[]{:S(2)}) %collective-permute-start.46) | collective-permute-done | bytes 196640 | tf_op jit(solution)/shard_map/ppermute | solution.py:64
  267.0 5.6 %shard_map.209 = (bf16[576,384]{1,0:T(8,128)(2,1)S(1)}, bf16[576,384]{1,0:T(8,128)(2,1)}, bf16[576,384]{1,0:T(8,128)(2,1)S(1)}, bf16[576,384]{1,0:T(8,128)(2,1)S...) custom-call(s32[11]{0:T(128)S(1)} %concatenate.6.table_ref, ...), custom_call_target="tpu_custom_call", output_to_operand_aliasing={{0}: (1, {}), {1}: (2, {}), {2}: (3, {}), {3}: (4, {})} | custom-call | tf_op jit(solution)/shard_map/pallas_call | solution.py:219
  301.9 5.1 %collective-permute-done.55 = bf16[256,384]{1,0:T(8,128)(2,1)} collective-permute-done((bf16[256,384]{1,0:T(8,128)(2,1)}, bf16[256,384]{1,0:T(8,128)(2,1)}, u32[]{:S(2)}, u32[]{:S(2)}) %collective-permute-start.55) | collective-permute-done | bytes 196640 | tf_op jit(solution)/shard_map/ppermute | solution.py:51
  312.6 12.1 %collective-permute-start.63 = (bf16[576,384]{1,0:T(8,128)(2,1)S(1)}, bf16[576,384]{1,0:T(8,128)(2,1)S(1)}, u32[]{:S(2)}, u32[]{:S(2)}) collective-permute-start(bf16[576,384]{1,0:T(8,128)(2,1)S(1)} %copy-done.31), channel_id=1, source_target_pairs={{0,16},{4,20},{8,24},{12,28},{16,0},{20,4},{24,8},{28,12},{1,17},{... | collective-permute-start | bytes 1327112 | tf_op jit(solution)/shard_map/ppermute | solution.py:64
  329.5 9.6 %collective-permute-done.63.refs_3_ = bf16[576,384]{1,0:T(8,128)(2,1)S(1)} collective-permute-done((bf16[576,384]{1,0:T(8,128)(2,1)S(1)}, bf16[576,384]{1,0:T(8,128)(2,1)S(1)}, u32[]{:S(2)}, u32[]{:S(2)}) %collective-permute-start.63) | collective-permute-done | bytes 442400 | tf_op jit(solution)/shard_map/ppermute | solution.py:64
  341.3 6.4 %collective-permute-done.44 = bf16[256,384]{1,0:T(8,128)(2,1)S(1)} collective-permute-done((bf16[256,384]{1,0:T(8,128)(2,1)S(1)}, bf16[256,384]{1,0:T(8,128)(2,1)S(1)}, u32[]{:S(2)}, u32[]{:S(2)}) %collective-permute-start.44) | collective-permute-done | bytes 196640 | tf_op jit(solution)/shard_map/ppermute | solution.py:51
  350.1 2.7 shard_map.215
  (287 shorter events, 114.1 us)
Async XLA Ops:
  17.2 14.6 %collective-permute-start.2 = (bf16[768,384]{1,0:T(8,128)(2,1)S(1)}, bf16[768,384]{1,0:T(8,128)(2,1)S(1)}, u32[]{:S(2)}, u32[]{:S(2)}) collective-permute-start(bf16[768,384]{1,0:T(8,128)(2,1)S(1)} %get-tuple-element.106), channel_id=1, source_target_pairs={{0,4},{4,0},{8,12},{12,8},{16,20},{20,16},{24,28},{28,24},{1,5},{5... | collective-permute-start | bytes 1769480 | tf_op jit(solution)/shard_map/ppermute | solution.py:51
  20.7 22.1 %collective-permute-start.13 = (bf16[576,384]{1,0:T(8,128)(2,1)S(1)}, bf16[576,384]{1,0:T(8,128)(2,1)S(1)}, u32[]{:S(2)}, u32[]{:S(2)}) collective-permute-start(bf16[576,384]{1,0:T(8,128)(2,1)S(1)} %shard_map.195.refs_3_), channel_id=1, source_target_pairs={{0,16},{4,20},{8,24},{12,28},{16,0},{20,4},{24,8},{28,12},{1,17},{... | collective-permute-start | bytes 1327112 | tf_op jit(solution)/shard_map/ppermute | solution.py:64
  23.2 20.8 %collective-permute-start.12 = (bf16[576,384]{1,0:T(8,128)(2,1)S(1)}, bf16[576,384]{1,0:T(8,128)(2,1)S(1)}, u32[]{:S(2)}, u32[]{:S(2)}) collective-permute-start(bf16[576,384]{1,0:T(8,128)(2,1)S(1)} %shard_map.195.refs_3_), channel_id=1, source_target_pairs={{0,8},{4,12},{8,0},{12,4},{16,24},{20,28},{24,16},{28,20},{1,9},{5... | collective-permute-start | bytes 1327112 | tf_op jit(solution)/shard_map/ppermute | solution.py:64
  24.8 19.3 %collective-permute-start.14 = (bf16[576,384]{1,0:T(8,128)(2,1)S(1)}, bf16[576,384]{1,0:T(8,128)(2,1)S(1)}, u32[]{:S(2)}, u32[]{:S(2)}) collective-permute-start(bf16[576,384]{1,0:T(8,128)(2,1)S(1)} %shard_map.195.refs_3_), channel_id=1, source_target_pairs={{8,16},{12,20},{16,8},{20,12},{9,17},{13,21},{17,9},{21,13},{10,18... | collective-permute-start | bytes 1327112 | tf_op jit(solution)/shard_map/ppermute | solution.py:64
  32.5 12.2 %collective-permute-start.3 = (bf16[512,384]{1,0:T(8,128)(2,1)S(1)}, bf16[512,384]{1,0:T(8,128)(2,1)S(1)}, u32[]{:S(2)}, u32[]{:S(2)}) collective-permute-start(bf16[512,384]{1,0:T(8,128)(2,1)S(1)} %pad_maximum_fusion.refs_0_), channel_id=1, source_target_pairs={{0,4},{4,0},{8,12},{12,8},{16,20},{20,16},{24,28},{28,24},{1,5},{5... | collective-permute-start | bytes 1179656 | tf_op jit(solution)/shard_map/ppermute | solution.py:51
  33.3 18.5 %collective-permute-start.4 = (bf16[512,384]{1,0:T(8,128)(2,1)S(1)}, bf16[512,384]{1,0:T(8,128)(2,1)S(1)}, u32[]{:S(2)}, u32[]{:S(2)}) collective-permute-start(bf16[512,384]{1,0:T(8,128)(2,1)S(1)} %collective-permute-done.1.refs_1_), channel_id=1, source_target_pairs={{0,4},{4,0},{8,12},{12,8},{16,20},{20,16},{24,28},{28,24},{1,5},{5... | collective-permute-start | bytes 1179656 | tf_op jit(solution)/shard_map/ppermute | solution.py:51
  44.1 17.0 %collective-permute-start.6 = (bf16[512,384]{1,0:T(8,128)(2,1)S(1)}, bf16[512,384]{1,0:T(8,128)(2,1)S(1)}, u32[]{:S(2)}, u32[]{:S(2)}) collective-permute-start(bf16[512,384]{1,0:T(8,128)(2,1)S(1)} %collective-permute-done.1.refs_1_), channel_id=1, source_target_pairs={{0,1},{1,0},{2,3},{3,2},{4,5},{5,4},{6,7},{7,6},{8,9},{9,8},{10,11... | collective-permute-start | bytes 1179656 | tf_op jit(solution)/shard_map/ppermute | solution.py:60
  44.7 16.5 %collective-permute-start.7 = (bf16[512,384]{1,0:T(8,128)(2,1)S(1)}, bf16[512,384]{1,0:T(8,128)(2,1)S(1)}, u32[]{:S(2)}, u32[]{:S(2)}) collective-permute-start(bf16[512,384]{1,0:T(8,128)(2,1)S(1)} %collective-permute-done.3.refs_2_), channel_id=1, source_target_pairs={{0,1},{1,0},{2,3},{3,2},{4,5},{5,4},{6,7},{7,6},{8,9},{9,8},{10,11... | collective-permute-start | bytes 1179656 | tf_op jit(solution)/shard_map/ppermute | solution.py:60
  55.6 71.7 %collective-permute-start.21 = (bf16[1536,384]{1,0:T(8,128)(2,1)S(1)}, bf16[1536,384]{1,0:T(8,128)(2,1)S(1)}, u32[]{:S(2)}, u32[]{:S(2)}) collective-permute-start(bf16[1536,384]{1,0:T(8,128)(2,1)S(1)} %shard_map.200.refs_2_), channel_id=1, source_target_pairs={{0,8},{4,12},{8,0},{12,4},{16,24},{20,28},{24,16},{28,20},{1,9},{5... | collective-permute-start | bytes 3538952 | tf_op jit(solution)/shard_map/ppermute | solution.py:64
  55.6 71.7 %collective-permute-start.22 = (bf16[1536,384]{1,0:T(8,128)(2,1)S(1)}, bf16[1536,384]{1,0:T(8,128)(2,1)S(1)}, u32[]{:S(2)}, u32[]{:S(2)}) collective-permute-start(bf16[1536,384]{1,0:T(8,128)(2,1)S(1)} %shard_map.200.refs_2_), channel_id=1, source_target_pairs={{0,16},{4,20},{8,24},{12,28},{16,0},{20,4},{24,8},{28,12},{1,17},{... | collective-permute-start | bytes 3538952 | tf_op jit(solution)/shard_map/ppermute | solution.py:64
  67.0 44.6 %collective-permute-start.16 = (bf16[192,512]{1,0:T(8,128)(2,1)S(1)}, bf16[192,512]{1,0:T(8,128)(2,1)S(1)}, u32[]{:S(2)}, u32[]{:S(2)}) collective-permute-start(bf16[192,512]{1,0:T(8,128)(2,1)S(1)} %get-tuple-element.111.refs_1_.refs_10_.refs_13_), channel_id=1, source_target_pairs={{0,8},{4,12},{8,16},{12,20},{1,9},{5,13},{9,17},{13,21},{2,10},{6,... | collective-permute-start | bytes 589832 | tf_op jit(solution)/shard_map/ppermute | solution.py:64
  68.9 46.9 %collective-permute-start.17 = (bf16[192,512]{1,0:T(8,128)(2,1)S(1)}, bf16[192,512]{1,0:T(8,128)(2,1)S(1)}, u32[]{:S(2)}, u32[]{:S(2)}) collective-permute-start(bf16[192,512]{1,0:T(8,128)(2,1)S(1)} %get-tuple-element.111.refs_1_.refs_10_.refs_13_), channel_id=1, source_target_pairs={{0,16},{4,20},{8,24},{12,28},{1,17},{5,21},{9,25},{13,29},{2,18},{... | collective-permute-start | bytes 589832 | tf_op jit(solution)/shard_map/ppermute | solution.py:64
  70.2 49.5 %collective-permute-start.18 = (bf16[192,512]{1,0:T(8,128)(2,1)S(1)}, bf16[192,512]{1,0:T(8,128)(2,1)S(1)}, u32[]{:S(2)}, u32[]{:S(2)}) collective-permute-start(bf16[192,512]{1,0:T(8,128)(2,1)S(1)} %get-tuple-element.111.refs_1_.refs_10_.refs_13_), channel_id=1, source_target_pairs={{0,24},{4,28},{1,25},{5,29},{2,26},{6,30},{3,27},{7,31}} | collective-permute-start | bytes 589832 | tf_op jit(solution)/shard_map/ppermute | solution.py:64
  129.3 20.9 %collective-permute-start.27 = (bf16[1536,384]{1,0:T(8,128)(2,1)S(1)}, bf16[1536,384]{1,0:T(8,128)(2,1)S(1)}, u32[]{:S(2)}, u32[]{:S(2)}) collective-permute-start(bf16[1536,384]{1,0:T(8,128)(2,1)S(1)} %shard_map.200.refs_2_), channel_id=1, source_target_pairs={{8,16},{12,20},{16,8},{20,12},{9,17},{13,21},{17,9},{21,13},{10,18... | collective-permute-start | bytes 3538952 | tf_op jit(solution)/shard_map/ppermute | solution.py:64
  130.0 36.4 %collective-permute-start.28 = (bf16[1536,384]{1,0:T(8,128)(2,1)S(1)}, bf16[1536,384]{1,0:T(8,128)(2,1)S(1)}, u32[]{:S(2)}, u32[]{:S(2)}) collective-permute-start(bf16[1536,384]{1,0:T(8,128)(2,1)S(1)} %collective-permute-done.22.refs_4_), channel_id=1, source_target_pairs={{8,0},{12,4},{16,24},{20,28},{9,1},{13,5},{17,25},{21,29},{10,2},{... | collective-permute-start | bytes 3538952 | tf_op jit(solution)/shard_map/ppermute | solution.py:64
  188.3 28.7 %collective-permute-start.37 = (bf16[1536,384]{1,0:T(8,128)(2,1)S(1)}, bf16[1536,384]{1,0:T(8,128)(2,1)S(1)}, u32[]{:S(2)}, u32[]{:S(2)}) collective-permute-start(bf16[1536,384]{1,0:T(8,128)(2,1)S(1)} %get-tuple-element.147), channel_id=1, source_target_pairs={{0,8},{4,12},{24,16},{28,20},{1,9},{5,13},{25,17},{29,21},{2,10},{... | collective-permute-start | bytes 3538952 | tf_op jit(solution)/shard_map/ppermute | solution.py:64
  190.7 26.3 %collective-permute-start.38 = (bf16[1536,384]{1,0:T(8,128)(2,1)S(1)}, bf16[1536,384]{1,0:T(8,128)(2,1)S(1)}, u32[]{:S(2)}, u32[]{:S(2)}) collective-permute-start(bf16[1536,384]{1,0:T(8,128)(2,1)S(1)} %get-tuple-element.147), channel_id=1, source_target_pairs={{8,16},{12,20},{16,8},{20,12},{9,17},{13,21},{17,9},{21,13},{10,18... | collective-permute-start | bytes 3538952 | tf_op jit(solution)/shard_map/ppermute | solution.py:64
  200.7 41.6 %collective-permute-start.48 = (bf16[1536,384]{1,0:T(8,128)(2,1)S(1)}, bf16[1536,384]{1,0:T(8,128)(2,1)S(1)}, u32[]{:S(2)}, u32[]{:S(2)}) collective-permute-start(bf16[1536,384]{1,0:T(8,128)(2,1)S(1)} %get-tuple-element.171), channel_id=1, source_target_pairs={{0,8},{4,12},{8,0},{12,4},{16,24},{20,28},{24,16},{28,20},{1,9},{5... | collective-permute-start | bytes 3538952 | tf_op jit(solution)/shard_map/ppermute | solution.py:64
  219.7 47.3 %collective-permute-start.49 = (bf16[768,384]{1,0:T(8,128)(2,1)S(1)}, bf16[768,384]{1,0:T(8,128)(2,1)S(1)}, u32[]{:S(2)}, u32[]{:S(2)}) collective-permute-start(bf16[768,384]{1,0:T(8,128)(2,1)S(1)} %shard_map.208), channel_id=1, source_target_pairs={{0,16},{4,20},{8,24},{12,28},{16,0},{20,4},{24,8},{28,12},{1,17},{... | collective-permute-start | bytes 1769480 | tf_op jit(solution)/shard_map/ppermute | solution.py:64
  234.2 12.8 %collective-permute-start.45 = (bf16[192,512]{1,0:T(8,128)(2,1)S(1)}, bf16[192,512]{1,0:T(8,128)(2,1)S(1)}, u32[]{:S(2)}, u32[]{:S(2)}) collective-permute-start(bf16[192,512]{1,0:T(8,128)(2,1)S(1)} %get-tuple-element.167), channel_id=1, source_target_pairs={{8,0},{12,4},{16,8},{20,12},{9,1},{13,5},{17,9},{21,13},{10,2},{14... | collective-permute-start | bytes 589832 | tf_op jit(solution)/shard_map/ppermute | solution.py:64
  235.5 31.5 %collective-permute-start.46 = (bf16[192,512]{1,0:T(8,128)(2,1)S(1)}, bf16[192,512]{1,0:T(8,128)(2,1)S(1)}, u32[]{:S(2)}, u32[]{:S(2)}) collective-permute-start(bf16[192,512]{1,0:T(8,128)(2,1)S(1)} %get-tuple-element.168), channel_id=1, source_target_pairs={{16,0},{20,4},{24,8},{28,12},{17,1},{21,5},{25,9},{29,13},{18,2},{... | collective-permute-start | bytes 589832 | tf_op jit(solution)/shard_map/ppermute | solution.py:64
  236.8 30.2 %collective-permute-start.47 = (bf16[192,512]{1,0:T(8,128)(2,1)S(1)}, bf16[192,512]{1,0:T(8,128)(2,1)S(1)}, u32[]{:S(2)}, u32[]{:S(2)}) collective-permute-start(bf16[192,512]{1,0:T(8,128)(2,1)S(1)} %get-tuple-element.169), channel_id=1, source_target_pairs={{24,0},{28,4},{25,1},{29,5},{26,2},{30,6},{27,3},{31,7}} | collective-permute-start | bytes 589832 | tf_op jit(solution)/shard_map/ppermute | solution.py:64
  281.2 14.7 %collective-permute-start.53 = (bf16[576,384]{1,0:T(8,128)(2,1)S(1)}, bf16[576,384]{1,0:T(8,128)(2,1)S(1)}, u32[]{:S(2)}, u32[]{:S(2)}) collective-permute-start(bf16[576,384]{1,0:T(8,128)(2,1)S(1)} %copy-done.33), channel_id=1, source_target_pairs={{0,8},{4,12},{24,16},{28,20},{1,9},{5,13},{25,17},{29,21},{2,10},{... | collective-permute-start | bytes 1327112 | tf_op jit(solution)/shard_map/ppermute | solution.py:64
  282.5 14.8 %collective-permute-start.54 = (bf16[576,384]{1,0:T(8,128)(2,1)S(1)}, bf16[576,384]{1,0:T(8,128)(2,1)S(1)}, u32[]{:S(2)}, u32[]{:S(2)}) collective-permute-start(bf16[576,384]{1,0:T(8,128)(2,1)S(1)} %copy-done.33), channel_id=1, source_target_pairs={{8,16},{12,20},{16,8},{20,12},{9,17},{13,21},{17,9},{21,13},{10,18... | collective-permute-start | bytes 1327112 | tf_op jit(solution)/shard_map/ppermute | solution.py:64
  290.0 35.1 %collective-permute-start.65 = (bf16[768,384]{1,0:T(8,128)(2,1)}, bf16[768,384]{1,0:T(8,128)(2,1)}, u32[]{:S(2)}, u32[]{:S(2)}) collective-permute-start(bf16[768,384]{1,0:T(8,128)(2,1)} %shard_map.213), channel_id=1, source_target_pairs={{0,16},{4,20},{8,24},{12,28},{16,0},{20,4},{24,8},{28,12},{1,17},{... | collective-permute-start | bytes 1769480 | tf_op jit(solution)/shard_map/ppermute | solution.py:64
  294.4 16.9 %collective-permute-start.43 = (bf16[512,384]{1,0:T(8,128)(2,1)}, bf16[512,384]{1,0:T(8,128)(2,1)}, u32[]{:S(2)}, u32[]{:S(2)}) collective-permute-start(bf16[512,384]{1,0:T(8,128)(2,1)} %broadcast_select_fusion.2), channel_id=1, source_target_pairs={{0,2},{1,3},{2,0},{3,1},{4,6},{5,7},{6,4},{7,5},{8,10},{9,11},{10,... | collective-permute-start | bytes 1179656 | tf_op jit(solution)/shard_map/ppermute | solution.py:57
  295.9 33.7 %collective-permute-start.62 = (bf16[576,384]{1,0:T(8,128)(2,1)}, bf16[576,384]{1,0:T(8,128)(2,1)}, u32[]{:S(2)}, u32[]{:S(2)}) collective-permute-start(bf16[576,384]{1,0:T(8,128)(2,1)} %get-tuple-element.182), channel_id=1, source_target_pairs={{0,8},{4,12},{8,0},{12,4},{16,24},{20,28},{24,16},{28,20},{1,9},{5... | collective-permute-start | bytes 1327112 | tf_op jit(solution)/shard_map/ppermute | solution.py:64
  310.6 17.7 %collective-permute-start.59 = (f32[2,384]{1,0:T(2,128)S(1)}, f32[2,384]{1,0:T(2,128)S(1)}, u32[]{:S(2)}, u32[]{:S(2)}) collective-permute-start(f32[2,384]{1,0:T(2,128)S(1)} %pad_maximum_fusion.2), channel_id=1, source_target_pairs={{0,4},{4,0},{8,12},{12,8},{16,20},{20,16},{24,28},{28,24},{1,5},{5... | collective-permute-start | bytes 9224 | tf_op jit(solution)/shard_map/ppermute | solution.py:51
  312.6 26.6 %collective-permute-start.63 = (bf16[576,384]{1,0:T(8,128)(2,1)S(1)}, bf16[576,384]{1,0:T(8,128)(2,1)S(1)}, u32[]{:S(2)}, u32[]{:S(2)}) collective-permute-start(bf16[576,384]{1,0:T(8,128)(2,1)S(1)} %copy-done.31), channel_id=1, source_target_pairs={{0,16},{4,20},{8,24},{12,28},{16,0},{20,4},{24,8},{28,12},{1,17},{... | collective-permute-start | bytes 1327112 | tf_op jit(solution)/shard_map/ppermute | solution.py:64
  327.2 22.9 %collective-permute-start.66 = (bf16[768,384]{1,0:T(8,128)(2,1)S(1)}, bf16[768,384]{1,0:T(8,128)(2,1)S(1)}, u32[]{:S(2)}, u32[]{:S(2)}) collective-permute-start(bf16[768,384]{1,0:T(8,128)(2,1)S(1)} %get-tuple-element.191), channel_id=1, source_target_pairs={{0,4},{4,0},{8,12},{12,8},{16,20},{20,16},{24,28},{28,24},{1,5},{5... | collective-permute-start | bytes 1769480 | tf_op jit(solution)/shard_map/ppermute | solution.py:51
  328.3 12.9 %collective-permute-start.60 = (f32[2,384]{1,0:T(2,128)S(1)}, f32[2,384]{1,0:T(2,128)S(1)}, u32[]{:S(2)}, u32[]{:S(2)}) collective-permute-start(f32[2,384]{1,0:T(2,128)S(1)} %fusion.12), channel_id=1, source_target_pairs={{0,8},{4,12},{8,0},{12,4},{16,24},{20,28},{24,16},{28,20},{1,9},{5... | collective-permute-start | bytes 9224 | tf_op jit(solution)/shard_map/ppermute | solution.py:51
  328.5 19.3 %collective-permute-start.44 = (bf16[256,384]{1,0:T(8,128)(2,1)S(1)}, bf16[256,384]{1,0:T(8,128)(2,1)S(1)}, u32[]{:S(2)}, u32[]{:S(2)}) collective-permute-start(bf16[256,384]{1,0:T(8,128)(2,1)S(1)} %broadcast_select_fusion.5), channel_id=1, source_target_pairs={{0,4},{4,0},{8,12},{12,8},{16,20},{20,16},{24,28},{28,24},{1,5},{5... | collective-permute-start | bytes 589832 | tf_op jit(solution)/shard_map/ppermute | solution.py:51
  (92 other events, 780.9 us)

commit v4 on v3

--- a/solution.py
+++ b/solution.py
@@ -851,6 +851,7 @@
         + wide,
         table,
         [query, own] + moved + [attend_weights],
+        earlier=forward_pieces[1:3],
     )
     summed = all_sum(
         place,

time: 356 us -> 349 us (0.980)
  waiting for transfers between devices: 183 us -> 172 us
  starting transfers between devices: 77.2 us -> 82 us
    ppermute x23, waiting for transfers between devices: 121 us -> 107 us  [send_z(): return lax.ppermute(value, 'gx', pairs)]
    ppermute x16, waiting for transfers between devices: 40.2 us -> 46.1 us  [swap_gx(): return lax.ppermute(value, 'gx', [(i, i ^ bit) for i in range(self.nx)])]
    unnamed x115 -> x119, local copies, waits for them, and re-layouts: 8.53 us -> 7.84 us
  transfers between devices with their start and end apart: 67 -> 67, of which waited for: 37 -> 35; matrix products, arithmetic and copies ran while one was open for 5% -> 5% of each run, Pallas kernels for 12% -> 11%
where the time goes in v4:
time: 349 us; the launch traced here: 348 us
  waiting for transfers between devices  172 us (49%)
  starting transfers between devices  82 us (23%)
  Pallas kernels  65.2 us (19%)
  other arithmetic  18.6 us (5%)
  local copies, waits for them, and re-layouts  8.68 us (2%)
    ppermute x23, waiting for transfers between devices, send_z(): return lax.ppermute(value, 'gx', pairs)  107 us
    pallas_call x22, Pallas kernels, call(): pl.pallas_call(kernel, out_shape=[jax.ShapeDtypeStruct(shape, dtype) for...  65.2 us
    ppermute x23, starting transfers between devices, send_z(): return lax.ppermute(value, 'gx', pairs)  48 us
    ppermute x16, waiting for transfers between devices, swap_gx(): return lax.ppermute(value, 'gx', [(i, i ^ bit) for i in range(self.nx)])  46.1 us
    ppermute x16, starting transfers between devices, swap_gx(): return lax.ppermute(value, 'gx', [(i, i ^ bit) for i in range(self.nx)])  19.5 us
    ppermute x9, waiting for transfers between devices, swap_x(): return lax.ppermute(value, 'gy', [(i, i ^ 2) for i in range(self.ny)])  11.7 us
    ppermute x9, starting transfers between devices, swap_x(): return lax.ppermute(value, 'gy', [(i, i ^ 2) for i in range(self.ny)])  10.6 us
    unnamed x119, local copies, waits for them, and re-layouts  7.84 us
  transfers between devices with their start and end apart: 67, of which 35 were waited for; matrix products, arithmetic and copies ran while one was open for 5% of the time, Pallas kernels for 11%

profile of v4, /device:TPU:0, one launch (start us, length us, event | category | flops | bytes accessed | tf_op | source)
XLA Modules:
  0.0 348.2 jit_solution(17828886807744047626)
XLA Ops:
  6.2 3.0 collective-permute-start
  9.2 5.4 %collective-permute-done.refs_1_ = bf16[288,384]{1,0:T(8,128)(2,1)S(1)} collective-permute-done((bf16[288,384]{1,0:T(8,128)(2,1)S(1)}, bf16[288,384]{1,0:T(8,128)(2,1)S(1)}, u32[]{:S(2)}, u32[]{:S(2)}) %collective-permute-start) | collective-permute-done | bytes 221216 | tf_op jit(solution)/shard_map/ppermute | solution.py:51
  15.4 2.9 collective-permute-start.13
  23.9 14.3 %collective-permute-done.13.refs_5_ = bf16[576,384]{1,0:T(8,128)(2,1)S(1)} collective-permute-done((bf16[576,384]{1,0:T(8,128)(2,1)S(1)}, bf16[576,384]{1,0:T(8,128)(2,1)S(1)}, u32[]{:S(2)}, u32[]{:S(2)}) %collective-permute-start.13) | collective-permute-done | bytes 442400 | tf_op jit(solution)/shard_map/ppermute | solution.py:64
  42.2 8.3 %collective-permute-done.15.refs_7_ = bf16[576,384]{1,0:T(8,128)(2,1)S(1)} collective-permute-done((bf16[576,384]{1,0:T(8,128)(2,1)S(1)}, bf16[576,384]{1,0:T(8,128)(2,1)S(1)}, u32[]{:S(2)}, u32[]{:S(2)}) %collective-permute-start.15) | collective-permute-done | bytes 442400 | tf_op jit(solution)/shard_map/ppermute | solution.py:64
  50.5 4.6 %collective-permute-start.20 = (bf16[1536,384]{1,0:T(8,128)(2,1)S(1)}, bf16[1536,384]{1,0:T(8,128)(2,1)S(1)}, u32[]{:S(2)}, u32[]{:S(2)}) collective-permute-start(bf16[1536,384]{1,0:T(8,128)(2,1)S(1)} %shard_map.199.refs_2_), channel_id=1, source_target_pairs={{0,16},{4,20},{8,24},{12,28},{16,0},{20,4},{24,8},{28,12},{1,17},{... | collective-permute-start | bytes 3538952 | tf_op jit(solution)/shard_map/ppermute | solution.py:64
  61.6 9.7 %collective-permute-done.3.refs_2_ = bf16[512,384]{1,0:T(8,128)(2,1)S(1)} collective-permute-done((bf16[512,384]{1,0:T(8,128)(2,1)S(1)}, bf16[512,384]{1,0:T(8,128)(2,1)S(1)}, u32[]{:S(2)}, u32[]{:S(2)}) %collective-permute-start.3) | collective-permute-done | bytes 393248 | tf_op jit(solution)/shard_map/ppermute | solution.py:51
  71.3 7.5 %collective-permute-done.4.refs_3_ = bf16[512,384]{1,0:T(8,128)(2,1)S(1)} collective-permute-done((bf16[512,384]{1,0:T(8,128)(2,1)S(1)}, bf16[512,384]{1,0:T(8,128)(2,1)S(1)}, u32[]{:S(2)}, u32[]{:S(2)}) %collective-permute-start.4) | collective-permute-done | bytes 393248 | tf_op jit(solution)/shard_map/ppermute | solution.py:51
  83.0 3.3 shard_map.198
  90.9 15.6 %collective-permute-done.16.refs_2_ = bf16[192,512]{1,0:T(8,128)(2,1)S(1)} collective-permute-done((bf16[192,512]{1,0:T(8,128)(2,1)S(1)}, bf16[192,512]{1,0:T(8,128)(2,1)S(1)}, u32[]{:S(2)}, u32[]{:S(2)}) %collective-permute-start.16) | collective-permute-done | bytes 196640 | tf_op jit(solution)/shard_map/ppermute | solution.py:64
  110.9 5.2 %shard_map.200 = (f32[192,512]{1,0:T(8,128)S(1)}, bf16[192,512]{1,0:T(8,128)(2,1)S(1)}, f32[2,1,512]{2,1,0:T(1,128)S(1)}, bf16[192,1024]{1,0:T(8,128)(2,1)S(1)},...) custom-call(s32[11]{0:T(128)S(1)} %concatenate.6.table_ref, ...), custom_call_target="tpu_custom_call" | custom-call | tf_op jit(solution)/shard_map/pallas_call | solution.py:219
  123.4 6.4 %collective-permute-done.23 = bf16[512,384]{1,0:T(8,128)(2,1)S(1)} collective-permute-done((bf16[512,384]{1,0:T(8,128)(2,1)S(1)}, bf16[512,384]{1,0:T(8,128)(2,1)S(1)}, u32[]{:S(2)}, u32[]{:S(2)}) %collective-permute-start.23) | collective-permute-done | bytes 393248 | tf_op jit(solution)/shard_map/ppermute | solution.py:57
  132.9 7.9 %collective-permute-done.25 = bf16[512,384]{1,0:T(8,128)(2,1)S(1)} collective-permute-done((bf16[512,384]{1,0:T(8,128)(2,1)S(1)}, bf16[512,384]{1,0:T(8,128)(2,1)S(1)}, u32[]{:S(2)}, u32[]{:S(2)}) %collective-permute-start.25) | collective-permute-done | bytes 393248 | tf_op jit(solution)/shard_map/ppermute | solution.py:51
  142.2 19.2 %collective-permute-done.28.refs_6_ = bf16[1536,384]{1,0:T(8,128)(2,1)S(1)} collective-permute-done((bf16[1536,384]{1,0:T(8,128)(2,1)S(1)}, bf16[1536,384]{1,0:T(8,128)(2,1)S(1)}, u32[]{:S(2)}, u32[]{:S(2)}) %collective-permute-start.28) | collective-permute-done | bytes 1179680 | tf_op jit(solution)/shard_map/ppermute | solution.py:64
  165.7 10.2 %shard_map.202 = (bf16[512,512]{1,0:T(8,128)(2,1)S(1)}, bf16[512,1024]{1,0:T(8,128)(2,1)S(1)}, bf16[512,384]{1,0:T(8,128)(2,1)S(1)}, bf16[512,384]{1,0:T(8,128)(...) custom-call(s32[11]{0:T(128)S(1)} %concatenate.6.table_ref, ...), custom_call_target="tpu_custom_call" | custom-call | tf_op jit(solution)/shard_map/pallas_call | solution.py:219
  181.2 2.4 collective-permute-start.37
  184.3 4.1 %shard_map.204 = (bf16[1536,384]{1,0:T(8,128)(2,1)S(1)}, bf16[1536,384]{1,0:T(8,128)(2,1)S(1)}, bf16[1536,384]{1,0:T(8,128)(2,1)S(1)}) custom-call(s32[11]{0:T(128)S(1)} %concatenate.6.table_ref, bf16[1536,512]{1,0:T(8,128)(2,1)S(1)} %get-tuple-element.134.refs_0_, bf16[4,512,384]{2,1,0:T(8,128)(2,1)S(1)} %get-tuple-element.129.refs_0_.refs_1_, ...), custom_call_target="tpu_custom_call" | custom-call | tf_op jit(solution)/shard_map/pallas_call | solution.py:219
  193.9 2.5 collective-permute-start.48
  196.3 3.9 %collective-permute-done.35 = bf16[512,384]{1,0:T(8,128)(2,1)S(1)} collective-permute-done((bf16[512,384]{1,0:T(8,128)(2,1)S(1)}, bf16[512,384]{1,0:T(8,128)(2,1)S(1)}, u32[]{:S(2)}, u32[]{:S(2)}) %collective-permute-start.35) | collective-permute-done | bytes 393248 | tf_op jit(solution)/shard_map/ppermute | solution.py:51
  200.6 9.3 %collective-permute-done.37.refs_16_.refs_1_ = bf16[1536,384]{1,0:T(8,128)(2,1)S(1)} collective-permute-done((bf16[1536,384]{1,0:T(8,128)(2,1)S(1)}, bf16[1536,384]{1,0:T(8,128)(2,1)S(1)}, u32[]{:S(2)}, u32[]{:S(2)}) %collective-permute-start.37) | collective-permute-done | bytes 1179680 | tf_op jit(solution)/shard_map/ppermute | solution.py:64
  212.6 4.2 %collective-permute-start.49 = (bf16[768,384]{1,0:T(8,128)(2,1)S(1)}, bf16[768,384]{1,0:T(8,128)(2,1)S(1)}, u32[]{:S(2)}, u32[]{:S(2)}) collective-permute-start(bf16[768,384]{1,0:T(8,128)(2,1)S(1)} %shard_map.208), channel_id=1, source_target_pairs={{0,16},{4,20},{8,24},{12,28},{16,0},{20,4},{24,8},{28,12},{1,17},{... | collective-permute-start | bytes 1769480 | tf_op jit(solution)/shard_map/ppermute | solution.py:64
  216.8 10.3 %shard_map.206 = (bf16[4,512,384]{2,1,0:T(8,128)(2,1)S(1)}, f32[512,1]{1,0:T(8,128)S(1)}, bf16[192,512]{1,0:T(8,128)(2,1)S(1)}, f32[192,512]{1,0:T(8,128)S(1)}, ...) custom-call(s32[11]{0:T(128)S(1)} %concatenate.6.table_ref, ...), custom_call_target="tpu_custom_call" | custom-call | tf_op jit(solution)/shard_map/pallas_call | solution.py:219
  231.2 2.4 shard_map.207
  233.7 4.9 %collective-permute-done.48.refs_15_.refs_1_ = bf16[1536,384]{1,0:T(8,128)(2,1)S(1)} collective-permute-done((bf16[1536,384]{1,0:T(8,128)(2,1)S(1)}, bf16[1536,384]{1,0:T(8,128)(2,1)S(1)}, u32[]{:S(2)}, u32[]{:S(2)}) %collective-permute-start.48) | collective-permute-done | bytes 1179680 | tf_op jit(solution)/shard_map/ppermute | solution.py:64
  240.9 19.0 %collective-permute-done.46.refs_6_ = bf16[192,512]{1,0:T(8,128)(2,1)S(1)} collective-permute-done((bf16[192,512]{1,0:T(8,128)(2,1)S(1)}, bf16[192,512]{1,0:T(8,128)(2,1)S(1)}, u32[]{:S(2)}, u32[]{:S(2)}) %collective-permute-start.46) | collective-permute-done | bytes 196640 | tf_op jit(solution)/shard_map/ppermute | solution.py:64
  259.9 5.6 %shard_map.209 = (bf16[576,384]{1,0:T(8,128)(2,1)S(1)}, bf16[576,384]{1,0:T(8,128)(2,1)}, bf16[576,384]{1,0:T(8,128)(2,1)S(1)}, bf16[576,384]{1,0:T(8,128)(2,1)S...) custom-call(s32[11]{0:T(128)S(1)} %concatenate.6.table_ref, ...), custom_call_target="tpu_custom_call", output_to_operand_aliasing={{0}: (1, {}), {1}: (2, {}), {2}: (3, {}), {3}: (4, {})} | custom-call | tf_op jit(solution)/shard_map/pallas_call | solution.py:219
  296.7 3.2 collective-permute-done.55
  299.9 2.7 fusion.6
  306.6 12.3 %collective-permute-start.63 = (bf16[576,384]{1,0:T(8,128)(2,1)S(1)}, bf16[576,384]{1,0:T(8,128)(2,1)S(1)}, u32[]{:S(2)}, u32[]{:S(2)}) collective-permute-start(bf16[576,384]{1,0:T(8,128)(2,1)S(1)} %copy-done.31), channel_id=1, source_target_pairs={{0,16},{4,20},{8,24},{12,28},{16,0},{20,4},{24,8},{28,12},{1,17},{... | collective-permute-start | bytes 1327112 | tf_op jit(solution)/shard_map/ppermute | solution.py:64
  322.8 9.2 %collective-permute-done.63.refs_3_ = bf16[576,384]{1,0:T(8,128)(2,1)S(1)} collective-permute-done((bf16[576,384]{1,0:T(8,128)(2,1)S(1)}, bf16[576,384]{1,0:T(8,128)(2,1)S(1)}, u32[]{:S(2)}, u32[]{:S(2)}) %collective-permute-start.63) | collective-permute-done | bytes 442400 | tf_op jit(solution)/shard_map/ppermute | solution.py:64
  334.7 6.3 %collective-permute-done.44 = bf16[256,384]{1,0:T(8,128)(2,1)S(1)} collective-permute-done((bf16[256,384]{1,0:T(8,128)(2,1)S(1)}, bf16[256,384]{1,0:T(8,128)(2,1)S(1)}, u32[]{:S(2)}, u32[]{:S(2)}) %collective-permute-start.44) | collective-permute-done | bytes 196640 | tf_op jit(solution)/shard_map/ppermute | solution.py:51
  343.4 2.7 shard_map.215
  (291 shorter events, 118.0 us)
Async XLA Ops:
  15.4 22.9 %collective-permute-start.13 = (bf16[576,384]{1,0:T(8,128)(2,1)S(1)}, bf16[576,384]{1,0:T(8,128)(2,1)S(1)}, u32[]{:S(2)}, u32[]{:S(2)}) collective-permute-start(bf16[576,384]{1,0:T(8,128)(2,1)S(1)} %shard_map.195.refs_3_), channel_id=1, source_target_pairs={{0,16},{4,20},{8,24},{12,28},{16,0},{20,4},{24,8},{28,12},{1,17},{... | collective-permute-start | bytes 1327112 | tf_op jit(solution)/shard_map/ppermute | solution.py:64
  20.1 21.1 %collective-permute-start.2 = (bf16[768,384]{1,0:T(8,128)(2,1)S(1)}, bf16[768,384]{1,0:T(8,128)(2,1)S(1)}, u32[]{:S(2)}, u32[]{:S(2)}) collective-permute-start(bf16[768,384]{1,0:T(8,128)(2,1)S(1)} %get-tuple-element.106), channel_id=1, source_target_pairs={{0,4},{4,0},{8,12},{12,8},{16,20},{20,16},{24,28},{28,24},{1,5},{5... | collective-permute-start | bytes 1769480 | tf_op jit(solution)/shard_map/ppermute | solution.py:51
  21.7 20.5 %collective-permute-start.12 = (bf16[576,384]{1,0:T(8,128)(2,1)S(1)}, bf16[576,384]{1,0:T(8,128)(2,1)S(1)}, u32[]{:S(2)}, u32[]{:S(2)}) collective-permute-start(bf16[576,384]{1,0:T(8,128)(2,1)S(1)} %shard_map.195.refs_3_), channel_id=1, source_target_pairs={{0,8},{4,12},{8,0},{12,4},{16,24},{20,28},{24,16},{28,20},{1,9},{5... | collective-permute-start | bytes 1327112 | tf_op jit(solution)/shard_map/ppermute | solution.py:64
  23.3 18.9 %collective-permute-start.14 = (bf16[576,384]{1,0:T(8,128)(2,1)S(1)}, bf16[576,384]{1,0:T(8,128)(2,1)S(1)}, u32[]{:S(2)}, u32[]{:S(2)}) collective-permute-start(bf16[576,384]{1,0:T(8,128)(2,1)S(1)} %shard_map.195.refs_3_), channel_id=1, source_target_pairs={{8,16},{12,20},{16,8},{20,12},{9,17},{13,21},{17,9},{21,13},{10,18... | collective-permute-start | bytes 1327112 | tf_op jit(solution)/shard_map/ppermute | solution.py:64
  39.6 19.2 %collective-permute-start.1 = (bf16[512,384]{1,0:T(8,128)(2,1)S(1)}, bf16[512,384]{1,0:T(8,128)(2,1)S(1)}, u32[]{:S(2)}, u32[]{:S(2)}) collective-permute-start(bf16[512,384]{1,0:T(8,128)(2,1)S(1)} %pad_maximum_fusion.refs_0_), channel_id=1, source_target_pairs={{0,2},{1,3},{2,0},{3,1},{4,6},{5,7},{6,4},{7,5},{8,10},{9,11},{10,... | collective-permute-start | bytes 1179656 | tf_op jit(solution)/shard_map/ppermute | solution.py:57
  50.5 60.4 %collective-permute-start.19 = (bf16[1536,384]{1,0:T(8,128)(2,1)S(1)}, bf16[1536,384]{1,0:T(8,128)(2,1)S(1)}, u32[]{:S(2)}, u32[]{:S(2)}) collective-permute-start(bf16[1536,384]{1,0:T(8,128)(2,1)S(1)} %shard_map.199.refs_2_), channel_id=1, source_target_pairs={{0,8},{4,12},{8,0},{12,4},{16,24},{20,28},{24,16},{28,20},{1,9},{5... | collective-permute-start | bytes 3538952 | tf_op jit(solution)/shard_map/ppermute | solution.py:64
  50.5 60.4 %collective-permute-start.20 = (bf16[1536,384]{1,0:T(8,128)(2,1)S(1)}, bf16[1536,384]{1,0:T(8,128)(2,1)S(1)}, u32[]{:S(2)}, u32[]{:S(2)}) collective-permute-start(bf16[1536,384]{1,0:T(8,128)(2,1)S(1)} %shard_map.199.refs_2_), channel_id=1, source_target_pairs={{0,16},{4,20},{8,24},{12,28},{16,0},{20,4},{24,8},{28,12},{1,17},{... | collective-permute-start | bytes 3538952 | tf_op jit(solution)/shard_map/ppermute | solution.py:64
  60.8 18.0 %collective-permute-start.4 = (bf16[512,384]{1,0:T(8,128)(2,1)S(1)}, bf16[512,384]{1,0:T(8,128)(2,1)S(1)}, u32[]{:S(2)}, u32[]{:S(2)}) collective-permute-start(bf16[512,384]{1,0:T(8,128)(2,1)S(1)} %collective-permute-done.1.refs_1_), channel_id=1, source_target_pairs={{0,4},{4,0},{8,12},{12,8},{16,20},{20,16},{24,28},{28,24},{1,5},{5... | collective-permute-start | bytes 1179656 | tf_op jit(solution)/shard_map/ppermute | solution.py:51
  61.5 17.9 %collective-permute-start.6 = (bf16[512,384]{1,0:T(8,128)(2,1)S(1)}, bf16[512,384]{1,0:T(8,128)(2,1)S(1)}, u32[]{:S(2)}, u32[]{:S(2)}) collective-permute-start(bf16[512,384]{1,0:T(8,128)(2,1)S(1)} %collective-permute-done.1.refs_1_), channel_id=1, source_target_pairs={{0,1},{1,0},{2,3},{3,2},{4,5},{5,4},{6,7},{7,6},{8,9},{9,8},{10,11... | collective-permute-start | bytes 1179656 | tf_op jit(solution)/shard_map/ppermute | solution.py:60
  86.3 20.1 %collective-permute-start.16 = (bf16[192,512]{1,0:T(8,128)(2,1)S(1)}, bf16[192,512]{1,0:T(8,128)(2,1)S(1)}, u32[]{:S(2)}, u32[]{:S(2)}) collective-permute-start(bf16[192,512]{1,0:T(8,128)(2,1)S(1)} %get-tuple-element.111.refs_1_.refs_10_.refs_13_), channel_id=1, source_target_pairs={{0,8},{4,12},{8,16},{12,20},{1,9},{5,13},{9,17},{13,21},{2,10},{6,... | collective-permute-start | bytes 589832 | tf_op jit(solution)/shard_map/ppermute | solution.py:64
  88.2 20.5 %collective-permute-start.17 = (bf16[192,512]{1,0:T(8,128)(2,1)S(1)}, bf16[192,512]{1,0:T(8,128)(2,1)S(1)}, u32[]{:S(2)}, u32[]{:S(2)}) collective-permute-start(bf16[192,512]{1,0:T(8,128)(2,1)S(1)} %get-tuple-element.111.refs_1_.refs_10_.refs_13_), channel_id=1, source_target_pairs={{0,16},{4,20},{8,24},{12,28},{1,17},{5,21},{9,25},{13,29},{2,18},{... | collective-permute-start | bytes 589832 | tf_op jit(solution)/shard_map/ppermute | solution.py:64
  89.6 21.3 %collective-permute-start.18 = (bf16[192,512]{1,0:T(8,128)(2,1)S(1)}, bf16[192,512]{1,0:T(8,128)(2,1)S(1)}, u32[]{:S(2)}, u32[]{:S(2)}) collective-permute-start(bf16[192,512]{1,0:T(8,128)(2,1)S(1)} %get-tuple-element.111.refs_1_.refs_10_.refs_13_), channel_id=1, source_target_pairs={{0,24},{4,28},{1,25},{5,29},{2,26},{6,30},{3,27},{7,31}} | collective-permute-start | bytes 589832 | tf_op jit(solution)/shard_map/ppermute | solution.py:64
  121.4 20.9 %collective-permute-start.27 = (bf16[1536,384]{1,0:T(8,128)(2,1)S(1)}, bf16[1536,384]{1,0:T(8,128)(2,1)S(1)}, u32[]{:S(2)}, u32[]{:S(2)}) collective-permute-start(bf16[1536,384]{1,0:T(8,128)(2,1)S(1)} %shard_map.199.refs_2_), channel_id=1, source_target_pairs={{8,16},{12,20},{16,8},{20,12},{9,17},{13,21},{17,9},{21,13},{10,18... | collective-permute-start | bytes 3538952 | tf_op jit(solution)/shard_map/ppermute | solution.py:64
  122.1 39.3 %collective-permute-start.28 = (bf16[1536,384]{1,0:T(8,128)(2,1)S(1)}, bf16[1536,384]{1,0:T(8,128)(2,1)S(1)}, u32[]{:S(2)}, u32[]{:S(2)}) collective-permute-start(bf16[1536,384]{1,0:T(8,128)(2,1)S(1)} %collective-permute-done.20.refs_7_.refs_4_), channel_id=1, source_target_pairs={{8,0},{12,4},{16,24},{20,28},{9,1},{13,5},{17,25},{21,29},{10,2},{... | collective-permute-start | bytes 3538952 | tf_op jit(solution)/shard_map/ppermute | solution.py:64
  181.2 28.7 %collective-permute-start.37 = (bf16[1536,384]{1,0:T(8,128)(2,1)S(1)}, bf16[1536,384]{1,0:T(8,128)(2,1)S(1)}, u32[]{:S(2)}, u32[]{:S(2)}) collective-permute-start(bf16[1536,384]{1,0:T(8,128)(2,1)S(1)} %get-tuple-element.147), channel_id=1, source_target_pairs={{0,8},{4,12},{24,16},{28,20},{1,9},{5,13},{25,17},{29,21},{2,10},{... | collective-permute-start | bytes 3538952 | tf_op jit(solution)/shard_map/ppermute | solution.py:64
  183.6 26.3 %collective-permute-start.38 = (bf16[1536,384]{1,0:T(8,128)(2,1)S(1)}, bf16[1536,384]{1,0:T(8,128)(2,1)S(1)}, u32[]{:S(2)}, u32[]{:S(2)}) collective-permute-start(bf16[1536,384]{1,0:T(8,128)(2,1)S(1)} %get-tuple-element.147), channel_id=1, source_target_pairs={{8,16},{12,20},{16,8},{20,12},{9,17},{13,21},{17,9},{21,13},{10,18... | collective-permute-start | bytes 3538952 | tf_op jit(solution)/shard_map/ppermute | solution.py:64
  193.9 44.7 %collective-permute-start.48 = (bf16[1536,384]{1,0:T(8,128)(2,1)S(1)}, bf16[1536,384]{1,0:T(8,128)(2,1)S(1)}, u32[]{:S(2)}, u32[]{:S(2)}) collective-permute-start(bf16[1536,384]{1,0:T(8,128)(2,1)S(1)} %get-tuple-element.171), channel_id=1, source_target_pairs={{0,8},{4,12},{8,0},{12,4},{16,24},{20,28},{24,16},{28,20},{1,9},{5... | collective-permute-start | bytes 3538952 | tf_op jit(solution)/shard_map/ppermute | solution.py:64
  212.6 47.3 %collective-permute-start.49 = (bf16[768,384]{1,0:T(8,128)(2,1)S(1)}, bf16[768,384]{1,0:T(8,128)(2,1)S(1)}, u32[]{:S(2)}, u32[]{:S(2)}) collective-permute-start(bf16[768,384]{1,0:T(8,128)(2,1)S(1)} %shard_map.208), channel_id=1, source_target_pairs={{0,16},{4,20},{8,24},{12,28},{16,0},{20,4},{24,8},{28,12},{1,17},{... | collective-permute-start | bytes 1769480 | tf_op jit(solution)/shard_map/ppermute | solution.py:64
  227.1 13.8 %collective-permute-start.45 = (bf16[192,512]{1,0:T(8,128)(2,1)S(1)}, bf16[192,512]{1,0:T(8,128)(2,1)S(1)}, u32[]{:S(2)}, u32[]{:S(2)}) collective-permute-start(bf16[192,512]{1,0:T(8,128)(2,1)S(1)} %get-tuple-element.167), channel_id=1, source_target_pairs={{8,0},{12,4},{16,8},{20,12},{9,1},{13,5},{17,9},{21,13},{10,2},{14... | collective-permute-start | bytes 589832 | tf_op jit(solution)/shard_map/ppermute | solution.py:64
  228.4 31.5 %collective-permute-start.46 = (bf16[192,512]{1,0:T(8,128)(2,1)S(1)}, bf16[192,512]{1,0:T(8,128)(2,1)S(1)}, u32[]{:S(2)}, u32[]{:S(2)}) collective-permute-start(bf16[192,512]{1,0:T(8,128)(2,1)S(1)} %get-tuple-element.168), channel_id=1, source_target_pairs={{16,0},{20,4},{24,8},{28,12},{17,1},{21,5},{25,9},{29,13},{18,2},{... | collective-permute-start | bytes 589832 | tf_op jit(solution)/shard_map/ppermute | solution.py:64
  229.7 30.2 %collective-permute-start.47 = (bf16[192,512]{1,0:T(8,128)(2,1)S(1)}, bf16[192,512]{1,0:T(8,128)(2,1)S(1)}, u32[]{:S(2)}, u32[]{:S(2)}) collective-permute-start(bf16[192,512]{1,0:T(8,128)(2,1)S(1)} %get-tuple-element.169), channel_id=1, source_target_pairs={{24,0},{28,4},{25,1},{29,5},{26,2},{30,6},{27,3},{31,7}} | collective-permute-start | bytes 589832 | tf_op jit(solution)/shard_map/ppermute | solution.py:64
  274.1 14.6 %collective-permute-start.53 = (bf16[576,384]{1,0:T(8,128)(2,1)S(1)}, bf16[576,384]{1,0:T(8,128)(2,1)S(1)}, u32[]{:S(2)}, u32[]{:S(2)}) collective-permute-start(bf16[576,384]{1,0:T(8,128)(2,1)S(1)} %copy-done.33), channel_id=1, source_target_pairs={{0,8},{4,12},{24,16},{28,20},{1,9},{5,13},{25,17},{29,21},{2,10},{... | collective-permute-start | bytes 1327112 | tf_op jit(solution)/shard_map/ppermute | solution.py:64
  275.4 14.8 %collective-permute-start.54 = (bf16[576,384]{1,0:T(8,128)(2,1)S(1)}, bf16[576,384]{1,0:T(8,128)(2,1)S(1)}, u32[]{:S(2)}, u32[]{:S(2)}) collective-permute-start(bf16[576,384]{1,0:T(8,128)(2,1)S(1)} %copy-done.33), channel_id=1, source_target_pairs={{8,16},{12,20},{16,8},{20,12},{9,17},{13,21},{17,9},{21,13},{10,18... | collective-permute-start | bytes 1327112 | tf_op jit(solution)/shard_map/ppermute | solution.py:64
  283.8 35.1 %collective-permute-start.65 = (bf16[768,384]{1,0:T(8,128)(2,1)}, bf16[768,384]{1,0:T(8,128)(2,1)S(1)}, u32[]{:S(2)}, u32[]{:S(2)}) collective-permute-start(bf16[768,384]{1,0:T(8,128)(2,1)} %shard_map.213), channel_id=1, source_target_pairs={{0,16},{4,20},{8,24},{12,28},{16,0},{20,4},{24,8},{28,12},{1,17},{... | collective-permute-start | bytes 1769480 | tf_op jit(solution)/shard_map/ppermute | solution.py:64
  288.2 17.1 %collective-permute-start.43 = (bf16[512,384]{1,0:T(8,128)(2,1)}, bf16[512,384]{1,0:T(8,128)(2,1)}, u32[]{:S(2)}, u32[]{:S(2)}) collective-permute-start(bf16[512,384]{1,0:T(8,128)(2,1)} %broadcast_select_fusion.2), channel_id=1, source_target_pairs={{0,2},{1,3},{2,0},{3,1},{4,6},{5,7},{6,4},{7,5},{8,10},{9,11},{10,... | collective-permute-start | bytes 1179656 | tf_op jit(solution)/shard_map/ppermute | solution.py:57
  288.8 34.0 %collective-permute-start.62 = (bf16[576,384]{1,0:T(8,128)(2,1)}, bf16[576,384]{1,0:T(8,128)(2,1)S(1)}, u32[]{:S(2)}, u32[]{:S(2)}) collective-permute-start(bf16[576,384]{1,0:T(8,128)(2,1)} %get-tuple-element.182), channel_id=1, source_target_pairs={{0,8},{4,12},{8,0},{12,4},{16,24},{20,28},{24,16},{28,20},{1,9},{5... | collective-permute-start | bytes 1327112 | tf_op jit(solution)/shard_map/ppermute | solution.py:64
  303.7 17.4 %collective-permute-start.59 = (f32[2,384]{1,0:T(2,128)S(1)}, f32[2,384]{1,0:T(2,128)S(1)}, u32[]{:S(2)}, u32[]{:S(2)}) collective-permute-start(f32[2,384]{1,0:T(2,128)S(1)} %pad_maximum_fusion.2), channel_id=1, source_target_pairs={{0,4},{4,0},{8,12},{12,8},{16,20},{20,16},{24,28},{28,24},{1,5},{5... | collective-permute-start | bytes 9224 | tf_op jit(solution)/shard_map/ppermute | solution.py:51
  306.6 25.4 %collective-permute-start.63 = (bf16[576,384]{1,0:T(8,128)(2,1)S(1)}, bf16[576,384]{1,0:T(8,128)(2,1)S(1)}, u32[]{:S(2)}, u32[]{:S(2)}) collective-permute-start(bf16[576,384]{1,0:T(8,128)(2,1)S(1)} %copy-done.31), channel_id=1, source_target_pairs={{0,16},{4,20},{8,24},{12,28},{16,0},{20,4},{24,8},{28,12},{1,17},{... | collective-permute-start | bytes 1327112 | tf_op jit(solution)/shard_map/ppermute | solution.py:64
  320.5 22.9 %collective-permute-start.66 = (bf16[768,384]{1,0:T(8,128)(2,1)S(1)}, bf16[768,384]{1,0:T(8,128)(2,1)S(1)}, u32[]{:S(2)}, u32[]{:S(2)}) collective-permute-start(bf16[768,384]{1,0:T(8,128)(2,1)S(1)} %get-tuple-element.191), channel_id=1, source_target_pairs={{0,4},{4,0},{8,12},{12,8},{16,20},{20,16},{24,28},{28,24},{1,5},{5... | collective-permute-start | bytes 1769480 | tf_op jit(solution)/shard_map/ppermute | solution.py:51
  321.1 13.5 %collective-permute-start.60 = (f32[2,384]{1,0:T(2,128)S(1)}, f32[2,384]{1,0:T(2,128)S(1)}, u32[]{:S(2)}, u32[]{:S(2)}) collective-permute-start(f32[2,384]{1,0:T(2,128)S(1)} %fusion.12), channel_id=1, source_target_pairs={{0,8},{4,12},{8,0},{12,4},{16,24},{20,28},{24,16},{28,20},{1,9},{5... | collective-permute-start | bytes 9224 | tf_op jit(solution)/shard_map/ppermute | solution.py:51
  321.3 19.7 %collective-permute-start.44 = (bf16[256,384]{1,0:T(8,128)(2,1)S(1)}, bf16[256,384]{1,0:T(8,128)(2,1)S(1)}, u32[]{:S(2)}, u32[]{:S(2)}) collective-permute-start(bf16[256,384]{1,0:T(8,128)(2,1)S(1)} %broadcast_select_fusion.5), channel_id=1, source_target_pairs={{0,4},{4,0},{8,12},{12,8},{16,20},{20,16},{24,28},{28,24},{1,5},{5... | collective-permute-start | bytes 589832 | tf_op jit(solution)/shard_map/ppermute | solution.py:51
  333.0 13.1 %collective-permute-start.64 = (bf16[288,384]{1,0:T(8,128)(2,1)S(1)}, bf16[288,384]{1,0:T(8,128)(2,1)S(1)}, u32[]{:S(2)}, u32[]{:S(2)}) collective-permute-start(bf16[288,384]{1,0:T(8,128)(2,1)S(1)} %get-tuple-element.184), channel_id=1, source_target_pairs={{0,4},{4,0},{8,12},{12,8},{16,20},{20,16},{24,28},{28,24},{1,5},{5... | collective-permute-start | bytes 663560 | tf_op jit(solution)/shard_map/ppermute | solution.py:51
  (94 other events, 841.0 us)

commit v5 on v4

--- a/solution.py
+++ b/solution.py
@@ -188,6 +188,8 @@
 
 
 def call(body, outs, table, operands, pieces=(), scratch=(), earlier=(), held=(), alias=0, limit=24):
+    if operands:
+        operands, held = list(operands) + list(held), ()
     lengths = [len(p) for p in pieces]
     flat = [a for p in pieces for a in p] + list(earlier)
     vmem = pl.BlockSpec(memory_space=pltpu.VMEM)
@@ -801,7 +803,7 @@
     forward_got = place.swap_y(other)
     forward_piece = whole_piece(mine, forward_got)
     rows = jnp.concatenate([layer_in, out_grad], axis=0)
-    input_rows = spread(after(rows, attend_piece), forward_got)
+    input_rows = spread(after(rows, attend_got), forward_got)
     if lined:
         attend_pieces = gather_pieces(place, attend_piece)
         forward_pieces = gather_pieces(place, after(forward_piece, *attend_pieces[1:]), True)

time: 349 us -> 348 us (level)
  Pallas kernels: 65.2 us -> 61.2 us
    pallas_call x22, Pallas kernels: 65.2 us -> 61.2 us  [call(): pl.pallas_call(kernel, out_shape=[jax.ShapeDtypeStruct(shape, dtype) for...]
  transfers between devices with their start and end apart: 67 -> 67, of which waited for: 35 -> 35; matrix products, arithmetic and copies ran while one was open for 5% -> 6% of each run, Pallas kernels for 11% -> 10%
where the time goes in v5:
time: 348 us; the launch traced here: 347 us
  waiting for transfers between devices  175 us (50%)
  starting transfers between devices  81.8 us (24%)
  Pallas kernels  61.2 us (18%)
  other arithmetic  18.6 us (5%)
  local copies, waits for them, and re-layouts  8.68 us (2%)
    ppermute x23, waiting for transfers between devices, send_z(): return lax.ppermute(value, 'gx', pairs)  109 us
    pallas_call x22, Pallas kernels, call(): pl.pallas_call(kernel, out_shape=[jax.ShapeDtypeStruct(shape, dtype) for...  61.2 us
    ppermute x23, starting transfers between devices, send_z(): return lax.ppermute(value, 'gx', pairs)  47.8 us
    ppermute x16, waiting for transfers between devices, swap_gx(): return lax.ppermute(value, 'gx', [(i, i ^ bit) for i in range(self.nx)])  46.4 us
    ppermute x16, starting transfers between devices, swap_gx(): return lax.ppermute(value, 'gx', [(i, i ^ bit) for i in range(self.nx)])  19.5 us
    ppermute x9, waiting for transfers between devices, swap_x(): return lax.ppermute(value, 'gy', [(i, i ^ 2) for i in range(self.ny)])  11.9 us
    ppermute x9, starting transfers between devices, swap_x(): return lax.ppermute(value, 'gy', [(i, i ^ 2) for i in range(self.ny)])  10.6 us
    unnamed x119, local copies, waits for them, and re-layouts  7.84 us
  transfers between devices with their start and end apart: 67, of which 35 were waited for; matrix products, arithmetic and copies ran while one was open for 6% of the time, Pallas kernels for 10%

profile of v5, /device:TPU:0, one launch (start us, length us, event | category | flops | bytes accessed | tf_op | source)
XLA Modules:
  0.0 346.8 jit_solution(1083063348341057086)
XLA Ops:
  6.2 3.0 collective-permute-start
  9.2 5.4 %collective-permute-done.refs_1_ = bf16[288,384]{1,0:T(8,128)(2,1)S(1)} collective-permute-done((bf16[288,384]{1,0:T(8,128)(2,1)S(1)}, bf16[288,384]{1,0:T(8,128)(2,1)S(1)}, u32[]{:S(2)}, u32[]{:S(2)}) %collective-permute-start) | collective-permute-done | bytes 221216 | tf_op jit(solution)/shard_map/ppermute | solution.py:51
  15.4 2.9 collective-permute-start.13
  23.9 14.3 %collective-permute-done.13.refs_5_ = bf16[576,384]{1,0:T(8,128)(2,1)S(1)} collective-permute-done((bf16[576,384]{1,0:T(8,128)(2,1)S(1)}, bf16[576,384]{1,0:T(8,128)(2,1)S(1)}, u32[]{:S(2)}, u32[]{:S(2)}) %collective-permute-start.13) | collective-permute-done | bytes 442400 | tf_op jit(solution)/shard_map/ppermute | solution.py:64
  42.2 8.3 %collective-permute-done.15.refs_7_ = bf16[576,384]{1,0:T(8,128)(2,1)S(1)} collective-permute-done((bf16[576,384]{1,0:T(8,128)(2,1)S(1)}, bf16[576,384]{1,0:T(8,128)(2,1)S(1)}, u32[]{:S(2)}, u32[]{:S(2)}) %collective-permute-start.15) | collective-permute-done | bytes 442400 | tf_op jit(solution)/shard_map/ppermute | solution.py:64
  50.5 4.6 %collective-permute-start.20 = (bf16[1536,384]{1,0:T(8,128)(2,1)S(1)}, bf16[1536,384]{1,0:T(8,128)(2,1)S(1)}, u32[]{:S(2)}, u32[]{:S(2)}) collective-permute-start(bf16[1536,384]{1,0:T(8,128)(2,1)S(1)} %shard_map.199.refs_2_), channel_id=1, source_target_pairs={{0,16},{4,20},{8,24},{12,28},{16,0},{20,4},{24,8},{28,12},{1,17},{... | collective-permute-start | bytes 3538952 | tf_op jit(solution)/shard_map/ppermute | solution.py:64
  61.6 9.7 %collective-permute-done.3.refs_2_ = bf16[512,384]{1,0:T(8,128)(2,1)S(1)} collective-permute-done((bf16[512,384]{1,0:T(8,128)(2,1)S(1)}, bf16[512,384]{1,0:T(8,128)(2,1)S(1)}, u32[]{:S(2)}, u32[]{:S(2)}) %collective-permute-start.3) | collective-permute-done | bytes 393248 | tf_op jit(solution)/shard_map/ppermute | solution.py:51
  71.3 7.5 %collective-permute-done.4.refs_3_ = bf16[512,384]{1,0:T(8,128)(2,1)S(1)} collective-permute-done((bf16[512,384]{1,0:T(8,128)(2,1)S(1)}, bf16[512,384]{1,0:T(8,128)(2,1)S(1)}, u32[]{:S(2)}, u32[]{:S(2)}) %collective-permute-start.4) | collective-permute-done | bytes 393248 | tf_op jit(solution)/shard_map/ppermute | solution.py:51
  80.6 2.4 shard_map.197
  83.0 3.3 shard_map.198
  90.9 15.6 %collective-permute-done.16.refs_2_ = bf16[192,512]{1,0:T(8,128)(2,1)S(1)} collective-permute-done((bf16[192,512]{1,0:T(8,128)(2,1)S(1)}, bf16[192,512]{1,0:T(8,128)(2,1)S(1)}, u32[]{:S(2)}, u32[]{:S(2)}) %collective-permute-start.16) | collective-permute-done | bytes 196640 | tf_op jit(solution)/shard_map/ppermute | solution.py:64
  110.9 5.2 %shard_map.200 = (f32[192,512]{1,0:T(8,128)S(1)}, bf16[192,512]{1,0:T(8,128)(2,1)S(1)}, f32[2,1,512]{2,1,0:T(1,128)S(1)}, bf16[192,1024]{1,0:T(8,128)(2,1)S(1)},...) custom-call(s32[11]{0:T(128)S(1)} %concatenate.6.table_ref, ...), custom_call_target="tpu_custom_call" | custom-call | tf_op jit(solution)/shard_map/pallas_call | solution.py:221
  123.4 6.4 %collective-permute-done.23 = bf16[512,384]{1,0:T(8,128)(2,1)S(1)} collective-permute-done((bf16[512,384]{1,0:T(8,128)(2,1)S(1)}, bf16[512,384]{1,0:T(8,128)(2,1)S(1)}, u32[]{:S(2)}, u32[]{:S(2)}) %collective-permute-start.23) | collective-permute-done | bytes 393248 | tf_op jit(solution)/shard_map/ppermute | solution.py:57
  132.9 7.9 %collective-permute-done.25 = bf16[512,384]{1,0:T(8,128)(2,1)S(1)} collective-permute-done((bf16[512,384]{1,0:T(8,128)(2,1)S(1)}, bf16[512,384]{1,0:T(8,128)(2,1)S(1)}, u32[]{:S(2)}, u32[]{:S(2)}) %collective-permute-start.25) | collective-permute-done | bytes 393248 | tf_op jit(solution)/shard_map/ppermute | solution.py:51
  142.2 19.2 %collective-permute-done.28.refs_6_ = bf16[1536,384]{1,0:T(8,128)(2,1)S(1)} collective-permute-done((bf16[1536,384]{1,0:T(8,128)(2,1)S(1)}, bf16[1536,384]{1,0:T(8,128)(2,1)S(1)}, u32[]{:S(2)}, u32[]{:S(2)}) %collective-permute-start.28) | collective-permute-done | bytes 1179680 | tf_op jit(solution)/shard_map/ppermute | solution.py:64
  165.6 10.1 %shard_map.202 = (bf16[512,512]{1,0:T(8,128)(2,1)S(1)}, bf16[512,1024]{1,0:T(8,128)(2,1)S(1)}, bf16[512,384]{1,0:T(8,128)(2,1)S(1)}, bf16[512,384]{1,0:T(8,128)(...) custom-call(s32[11]{0:T(128)S(1)} %concatenate.6.table_ref, ...), custom_call_target="tpu_custom_call" | custom-call | tf_op jit(solution)/shard_map/pallas_call | solution.py:221
  180.8 2.4 collective-permute-start.37
  183.9 4.0 %shard_map.204 = (bf16[1536,384]{1,0:T(8,128)(2,1)S(1)}, bf16[1536,384]{1,0:T(8,128)(2,1)S(1)}, bf16[1536,384]{1,0:T(8,128)(2,1)S(1)}) custom-call(s32[11]{0:T(128)S(1)} %concatenate.6.table_ref, bf16[1536,512]{1,0:T(8,128)(2,1)S(1)} %get-tuple-element.134.refs_0_, bf16[4,512,384]{2,1,0:T(8,128)(2,1)S(1)} %get-tuple-element.129.refs_0_.refs_1_, ...), custom_call_target="tpu_custom_call" | custom-call | tf_op jit(solution)/shard_map/pallas_call | solution.py:221
  195.8 4.1 %collective-permute-done.35 = bf16[512,384]{1,0:T(8,128)(2,1)S(1)} collective-permute-done((bf16[512,384]{1,0:T(8,128)(2,1)S(1)}, bf16[512,384]{1,0:T(8,128)(2,1)S(1)}, u32[]{:S(2)}, u32[]{:S(2)}) %collective-permute-start.35) | collective-permute-done | bytes 393248 | tf_op jit(solution)/shard_map/ppermute | solution.py:51
  200.3 9.2 %collective-permute-done.37.refs_16_.refs_1_ = bf16[1536,384]{1,0:T(8,128)(2,1)S(1)} collective-permute-done((bf16[1536,384]{1,0:T(8,128)(2,1)S(1)}, bf16[1536,384]{1,0:T(8,128)(2,1)S(1)}, u32[]{:S(2)}, u32[]{:S(2)}) %collective-permute-start.37) | collective-permute-done | bytes 1179680 | tf_op jit(solution)/shard_map/ppermute | solution.py:64
  212.2 4.2 %collective-permute-start.49 = (bf16[768,384]{1,0:T(8,128)(2,1)S(1)}, bf16[768,384]{1,0:T(8,128)(2,1)S(1)}, u32[]{:S(2)}, u32[]{:S(2)}) collective-permute-start(bf16[768,384]{1,0:T(8,128)(2,1)S(1)} %shard_map.208), channel_id=1, source_target_pairs={{0,16},{4,20},{8,24},{12,28},{16,0},{20,4},{24,8},{28,12},{1,17},{... | collective-permute-start | bytes 1769480 | tf_op jit(solution)/shard_map/ppermute | solution.py:64
  216.4 8.2 %shard_map.206 = (bf16[4,512,384]{2,1,0:T(8,128)(2,1)S(1)}, f32[512,1]{1,0:T(8,128)S(1)}, bf16[192,512]{1,0:T(8,128)(2,1)S(1)}, f32[192,512]{1,0:T(8,128)S(1)}, ...) custom-call(s32[11]{0:T(128)S(1)} %concatenate.6.table_ref, ...), custom_call_target="tpu_custom_call" | custom-call | tf_op jit(solution)/shard_map/pallas_call | solution.py:221
  230.8 7.1 %collective-permute-done.48.refs_15_.refs_1_ = bf16[1536,384]{1,0:T(8,128)(2,1)S(1)} collective-permute-done((bf16[1536,384]{1,0:T(8,128)(2,1)S(1)}, bf16[1536,384]{1,0:T(8,128)(2,1)S(1)}, u32[]{:S(2)}, u32[]{:S(2)}) %collective-permute-start.48) | collective-permute-done | bytes 1179680 | tf_op jit(solution)/shard_map/ppermute | solution.py:64
  237.9 2.5 collective-permute-done.45.refs_5_.refs_4_
  240.3 19.3 %collective-permute-done.46.refs_6_ = bf16[192,512]{1,0:T(8,128)(2,1)S(1)} collective-permute-done((bf16[192,512]{1,0:T(8,128)(2,1)S(1)}, bf16[192,512]{1,0:T(8,128)(2,1)S(1)}, u32[]{:S(2)}, u32[]{:S(2)}) %collective-permute-start.46) | collective-permute-done | bytes 196640 | tf_op jit(solution)/shard_map/ppermute | solution.py:64
  259.6 4.5 %shard_map.209 = (bf16[576,384]{1,0:T(8,128)(2,1)S(1)}, bf16[576,384]{1,0:T(8,128)(2,1)}, bf16[576,384]{1,0:T(8,128)(2,1)S(1)}, bf16[576,384]{1,0:T(8,128)(2,1)S...) custom-call(s32[11]{0:T(128)S(1)} %concatenate.6.table_ref, ...), custom_call_target="tpu_custom_call", output_to_operand_aliasing={{0}: (1, {}), {1}: (2, {}), {2}: (3, {}), {3}: (4, {})} | custom-call | tf_op jit(solution)/shard_map/pallas_call | solution.py:221
  295.3 3.2 collective-permute-done.55
  298.5 2.7 fusion.6
  305.2 12.3 %collective-permute-start.63 = (bf16[576,384]{1,0:T(8,128)(2,1)S(1)}, bf16[576,384]{1,0:T(8,128)(2,1)S(1)}, u32[]{:S(2)}, u32[]{:S(2)}) collective-permute-start(bf16[576,384]{1,0:T(8,128)(2,1)S(1)} %copy-done.31), channel_id=1, source_target_pairs={{0,16},{4,20},{8,24},{12,28},{16,0},{20,4},{24,8},{28,12},{1,17},{... | collective-permute-start | bytes 1327112 | tf_op jit(solution)/shard_map/ppermute | solution.py:64
  321.4 9.2 %collective-permute-done.63.refs_3_ = bf16[576,384]{1,0:T(8,128)(2,1)S(1)} collective-permute-done((bf16[576,384]{1,0:T(8,128)(2,1)S(1)}, bf16[576,384]{1,0:T(8,128)(2,1)S(1)}, u32[]{:S(2)}, u32[]{:S(2)}) %collective-permute-start.63) | collective-permute-done | bytes 442400 | tf_op jit(solution)/shard_map/ppermute | solution.py:64
  333.3 6.3 %collective-permute-done.44 = bf16[256,384]{1,0:T(8,128)(2,1)S(1)} collective-permute-done((bf16[256,384]{1,0:T(8,128)(2,1)S(1)}, bf16[256,384]{1,0:T(8,128)(2,1)S(1)}, u32[]{:S(2)}, u32[]{:S(2)}) %collective-permute-start.44) | collective-permute-done | bytes 196640 | tf_op jit(solution)/shard_map/ppermute | solution.py:51
  342.0 2.7 shard_map.215
  (291 shorter events, 117.4 us)
Async XLA Ops:
  15.4 22.9 %collective-permute-start.13 = (bf16[576,384]{1,0:T(8,128)(2,1)S(1)}, bf16[576,384]{1,0:T(8,128)(2,1)S(1)}, u32[]{:S(2)}, u32[]{:S(2)}) collective-permute-start(bf16[576,384]{1,0:T(8,128)(2,1)S(1)} %shard_map.195.refs_3_), channel_id=1, source_target_pairs={{0,16},{4,20},{8,24},{12,28},{16,0},{20,4},{24,8},{28,12},{1,17},{... | collective-permute-start | bytes 1327112 | tf_op jit(solution)/shard_map/ppermute | solution.py:64
  20.1 21.1 %collective-permute-start.2 = (bf16[768,384]{1,0:T(8,128)(2,1)S(1)}, bf16[768,384]{1,0:T(8,128)(2,1)S(1)}, u32[]{:S(2)}, u32[]{:S(2)}) collective-permute-start(bf16[768,384]{1,0:T(8,128)(2,1)S(1)} %get-tuple-element.106), channel_id=1, source_target_pairs={{0,4},{4,0},{8,12},{12,8},{16,20},{20,16},{24,28},{28,24},{1,5},{5... | collective-permute-start | bytes 1769480 | tf_op jit(solution)/shard_map/ppermute | solution.py:51
  21.7 20.5 %collective-permute-start.12 = (bf16[576,384]{1,0:T(8,128)(2,1)S(1)}, bf16[576,384]{1,0:T(8,128)(2,1)S(1)}, u32[]{:S(2)}, u32[]{:S(2)}) collective-permute-start(bf16[576,384]{1,0:T(8,128)(2,1)S(1)} %shard_map.195.refs_3_), channel_id=1, source_target_pairs={{0,8},{4,12},{8,0},{12,4},{16,24},{20,28},{24,16},{28,20},{1,9},{5... | collective-permute-start | bytes 1327112 | tf_op jit(solution)/shard_map/ppermute | solution.py:64
  23.3 18.9 %collective-permute-start.14 = (bf16[576,384]{1,0:T(8,128)(2,1)S(1)}, bf16[576,384]{1,0:T(8,128)(2,1)S(1)}, u32[]{:S(2)}, u32[]{:S(2)}) collective-permute-start(bf16[576,384]{1,0:T(8,128)(2,1)S(1)} %shard_map.195.refs_3_), channel_id=1, source_target_pairs={{8,16},{12,20},{16,8},{20,12},{9,17},{13,21},{17,9},{21,13},{10,18... | collective-permute-start | bytes 1327112 | tf_op jit(solution)/shard_map/ppermute | solution.py:64
  39.6 19.2 %collective-permute-start.1 = (bf16[512,384]{1,0:T(8,128)(2,1)S(1)}, bf16[512,384]{1,0:T(8,128)(2,1)S(1)}, u32[]{:S(2)}, u32[]{:S(2)}) collective-permute-start(bf16[512,384]{1,0:T(8,128)(2,1)S(1)} %pad_maximum_fusion.refs_0_), channel_id=1, source_target_pairs={{0,2},{1,3},{2,0},{3,1},{4,6},{5,7},{6,4},{7,5},{8,10},{9,11},{10,... | collective-permute-start | bytes 1179656 | tf_op jit(solution)/shard_map/ppermute | solution.py:57
  50.5 60.4 %collective-permute-start.19 = (bf16[1536,384]{1,0:T(8,128)(2,1)S(1)}, bf16[1536,384]{1,0:T(8,128)(2,1)S(1)}, u32[]{:S(2)}, u32[]{:S(2)}) collective-permute-start(bf16[1536,384]{1,0:T(8,128)(2,1)S(1)} %shard_map.199.refs_2_), channel_id=1, source_target_pairs={{0,8},{4,12},{8,0},{12,4},{16,24},{20,28},{24,16},{28,20},{1,9},{5... | collective-permute-start | bytes 3538952 | tf_op jit(solution)/shard_map/ppermute | solution.py:64
  50.5 60.4 %collective-permute-start.20 = (bf16[1536,384]{1,0:T(8,128)(2,1)S(1)}, bf16[1536,384]{1,0:T(8,128)(2,1)S(1)}, u32[]{:S(2)}, u32[]{:S(2)}) collective-permute-start(bf16[1536,384]{1,0:T(8,128)(2,1)S(1)} %shard_map.199.refs_2_), channel_id=1, source_target_pairs={{0,16},{4,20},{8,24},{12,28},{16,0},{20,4},{24,8},{28,12},{1,17},{... | collective-permute-start | bytes 3538952 | tf_op jit(solution)/shard_map/ppermute | solution.py:64
  60.8 18.0 %collective-permute-start.4 = (bf16[512,384]{1,0:T(8,128)(2,1)S(1)}, bf16[512,384]{1,0:T(8,128)(2,1)S(1)}, u32[]{:S(2)}, u32[]{:S(2)}) collective-permute-start(bf16[512,384]{1,0:T(8,128)(2,1)S(1)} %collective-permute-done.1.refs_1_), channel_id=1, source_target_pairs={{0,4},{4,0},{8,12},{12,8},{16,20},{20,16},{24,28},{28,24},{1,5},{5... | collective-permute-start | bytes 1179656 | tf_op jit(solution)/shard_map/ppermute | solution.py:51
  61.5 17.9 %collective-permute-start.6 = (bf16[512,384]{1,0:T(8,128)(2,1)S(1)}, bf16[512,384]{1,0:T(8,128)(2,1)S(1)}, u32[]{:S(2)}, u32[]{:S(2)}) collective-permute-start(bf16[512,384]{1,0:T(8,128)(2,1)S(1)} %collective-permute-done.1.refs_1_), channel_id=1, source_target_pairs={{0,1},{1,0},{2,3},{3,2},{4,5},{5,4},{6,7},{7,6},{8,9},{9,8},{10,11... | collective-permute-start | bytes 1179656 | tf_op jit(solution)/shard_map/ppermute | solution.py:60
  86.3 20.1 %collective-permute-start.16 = (bf16[192,512]{1,0:T(8,128)(2,1)S(1)}, bf16[192,512]{1,0:T(8,128)(2,1)S(1)}, u32[]{:S(2)}, u32[]{:S(2)}) collective-permute-start(bf16[192,512]{1,0:T(8,128)(2,1)S(1)} %get-tuple-element.111.refs_1_.refs_10_.refs_13_), channel_id=1, source_target_pairs={{0,8},{4,12},{8,16},{12,20},{1,9},{5,13},{9,17},{13,21},{2,10},{6,... | collective-permute-start | bytes 589832 | tf_op jit(solution)/shard_map/ppermute | solution.py:64
  88.2 20.5 %collective-permute-start.17 = (bf16[192,512]{1,0:T(8,128)(2,1)S(1)}, bf16[192,512]{1,0:T(8,128)(2,1)S(1)}, u32[]{:S(2)}, u32[]{:S(2)}) collective-permute-start(bf16[192,512]{1,0:T(8,128)(2,1)S(1)} %get-tuple-element.111.refs_1_.refs_10_.refs_13_), channel_id=1, source_target_pairs={{0,16},{4,20},{8,24},{12,28},{1,17},{5,21},{9,25},{13,29},{2,18},{... | collective-permute-start | bytes 589832 | tf_op jit(solution)/shard_map/ppermute | solution.py:64
  89.6 21.3 %collective-permute-start.18 = (bf16[192,512]{1,0:T(8,128)(2,1)S(1)}, bf16[192,512]{1,0:T(8,128)(2,1)S(1)}, u32[]{:S(2)}, u32[]{:S(2)}) collective-permute-start(bf16[192,512]{1,0:T(8,128)(2,1)S(1)} %get-tuple-element.111.refs_1_.refs_10_.refs_13_), channel_id=1, source_target_pairs={{0,24},{4,28},{1,25},{5,29},{2,26},{6,30},{3,27},{7,31}} | collective-permute-start | bytes 589832 | tf_op jit(solution)/shard_map/ppermute | solution.py:64
  121.4 20.9 %collective-permute-start.27 = (bf16[1536,384]{1,0:T(8,128)(2,1)S(1)}, bf16[1536,384]{1,0:T(8,128)(2,1)S(1)}, u32[]{:S(2)}, u32[]{:S(2)}) collective-permute-start(bf16[1536,384]{1,0:T(8,128)(2,1)S(1)} %shard_map.199.refs_2_), channel_id=1, source_target_pairs={{8,16},{12,20},{16,8},{20,12},{9,17},{13,21},{17,9},{21,13},{10,18... | collective-permute-start | bytes 3538952 | tf_op jit(solution)/shard_map/ppermute | solution.py:64
  122.1 39.3 %collective-permute-start.28 = (bf16[1536,384]{1,0:T(8,128)(2,1)S(1)}, bf16[1536,384]{1,0:T(8,128)(2,1)S(1)}, u32[]{:S(2)}, u32[]{:S(2)}) collective-permute-start(bf16[1536,384]{1,0:T(8,128)(2,1)S(1)} %collective-permute-done.20.refs_7_.refs_4_), channel_id=1, source_target_pairs={{8,0},{12,4},{16,24},{20,28},{9,1},{13,5},{17,25},{21,29},{10,2},{... | collective-permute-start | bytes 3538952 | tf_op jit(solution)/shard_map/ppermute | solution.py:64
  180.8 28.7 %collective-permute-start.37 = (bf16[1536,384]{1,0:T(8,128)(2,1)S(1)}, bf16[1536,384]{1,0:T(8,128)(2,1)S(1)}, u32[]{:S(2)}, u32[]{:S(2)}) collective-permute-start(bf16[1536,384]{1,0:T(8,128)(2,1)S(1)} %get-tuple-element.147), channel_id=1, source_target_pairs={{0,8},{4,12},{24,16},{28,20},{1,9},{5,13},{25,17},{29,21},{2,10},{... | collective-permute-start | bytes 3538952 | tf_op jit(solution)/shard_map/ppermute | solution.py:64
  183.2 26.3 %collective-permute-start.38 = (bf16[1536,384]{1,0:T(8,128)(2,1)S(1)}, bf16[1536,384]{1,0:T(8,128)(2,1)S(1)}, u32[]{:S(2)}, u32[]{:S(2)}) collective-permute-start(bf16[1536,384]{1,0:T(8,128)(2,1)S(1)} %get-tuple-element.147), channel_id=1, source_target_pairs={{8,16},{12,20},{16,8},{20,12},{9,17},{13,21},{17,9},{21,13},{10,18... | collective-permute-start | bytes 3538952 | tf_op jit(solution)/shard_map/ppermute | solution.py:64
  193.6 44.3 %collective-permute-start.48 = (bf16[1536,384]{1,0:T(8,128)(2,1)S(1)}, bf16[1536,384]{1,0:T(8,128)(2,1)S(1)}, u32[]{:S(2)}, u32[]{:S(2)}) collective-permute-start(bf16[1536,384]{1,0:T(8,128)(2,1)S(1)} %get-tuple-element.171), channel_id=1, source_target_pairs={{0,8},{4,12},{8,0},{12,4},{16,24},{20,28},{24,16},{28,20},{1,9},{5... | collective-permute-start | bytes 3538952 | tf_op jit(solution)/shard_map/ppermute | solution.py:64
  212.2 47.4 %collective-permute-start.49 = (bf16[768,384]{1,0:T(8,128)(2,1)S(1)}, bf16[768,384]{1,0:T(8,128)(2,1)S(1)}, u32[]{:S(2)}, u32[]{:S(2)}) collective-permute-start(bf16[768,384]{1,0:T(8,128)(2,1)S(1)} %shard_map.208), channel_id=1, source_target_pairs={{0,16},{4,20},{8,24},{12,28},{16,0},{20,4},{24,8},{28,12},{1,17},{... | collective-permute-start | bytes 1769480 | tf_op jit(solution)/shard_map/ppermute | solution.py:64
  224.7 15.6 %collective-permute-start.45 = (bf16[192,512]{1,0:T(8,128)(2,1)S(1)}, bf16[192,512]{1,0:T(8,128)(2,1)S(1)}, u32[]{:S(2)}, u32[]{:S(2)}) collective-permute-start(bf16[192,512]{1,0:T(8,128)(2,1)S(1)} %get-tuple-element.167), channel_id=1, source_target_pairs={{8,0},{12,4},{16,8},{20,12},{9,1},{13,5},{17,9},{21,13},{10,2},{14... | collective-permute-start | bytes 589832 | tf_op jit(solution)/shard_map/ppermute | solution.py:64
  226.0 33.6 %collective-permute-start.46 = (bf16[192,512]{1,0:T(8,128)(2,1)S(1)}, bf16[192,512]{1,0:T(8,128)(2,1)S(1)}, u32[]{:S(2)}, u32[]{:S(2)}) collective-permute-start(bf16[192,512]{1,0:T(8,128)(2,1)S(1)} %get-tuple-element.168), channel_id=1, source_target_pairs={{16,0},{20,4},{24,8},{28,12},{17,1},{21,5},{25,9},{29,13},{18,2},{... | collective-permute-start | bytes 589832 | tf_op jit(solution)/shard_map/ppermute | solution.py:64
  227.3 32.3 %collective-permute-start.47 = (bf16[192,512]{1,0:T(8,128)(2,1)S(1)}, bf16[192,512]{1,0:T(8,128)(2,1)S(1)}, u32[]{:S(2)}, u32[]{:S(2)}) collective-permute-start(bf16[192,512]{1,0:T(8,128)(2,1)S(1)} %get-tuple-element.169), channel_id=1, source_target_pairs={{24,0},{28,4},{25,1},{29,5},{26,2},{30,6},{27,3},{31,7}} | collective-permute-start | bytes 589832 | tf_op jit(solution)/shard_map/ppermute | solution.py:64
  272.7 14.7 %collective-permute-start.53 = (bf16[576,384]{1,0:T(8,128)(2,1)S(1)}, bf16[576,384]{1,0:T(8,128)(2,1)S(1)}, u32[]{:S(2)}, u32[]{:S(2)}) collective-permute-start(bf16[576,384]{1,0:T(8,128)(2,1)S(1)} %copy-done.33), channel_id=1, source_target_pairs={{0,8},{4,12},{24,16},{28,20},{1,9},{5,13},{25,17},{29,21},{2,10},{... | collective-permute-start | bytes 1327112 | tf_op jit(solution)/shard_map/ppermute | solution.py:64
  274.0 14.8 %collective-permute-start.54 = (bf16[576,384]{1,0:T(8,128)(2,1)S(1)}, bf16[576,384]{1,0:T(8,128)(2,1)S(1)}, u32[]{:S(2)}, u32[]{:S(2)}) collective-permute-start(bf16[576,384]{1,0:T(8,128)(2,1)S(1)} %copy-done.33), channel_id=1, source_target_pairs={{8,16},{12,20},{16,8},{20,12},{9,17},{13,21},{17,9},{21,13},{10,18... | collective-permute-start | bytes 1327112 | tf_op jit(solution)/shard_map/ppermute | solution.py:64
  282.4 35.1 %collective-permute-start.65 = (bf16[768,384]{1,0:T(8,128)(2,1)}, bf16[768,384]{1,0:T(8,128)(2,1)S(1)}, u32[]{:S(2)}, u32[]{:S(2)}) collective-permute-start(bf16[768,384]{1,0:T(8,128)(2,1)} %shard_map.213), channel_id=1, source_target_pairs={{0,16},{4,20},{8,24},{12,28},{16,0},{20,4},{24,8},{28,12},{1,17},{... | collective-permute-start | bytes 1769480 | tf_op jit(solution)/shard_map/ppermute | solution.py:64
  286.8 17.1 %collective-permute-start.43 = (bf16[512,384]{1,0:T(8,128)(2,1)}, bf16[512,384]{1,0:T(8,128)(2,1)}, u32[]{:S(2)}, u32[]{:S(2)}) collective-permute-start(bf16[512,384]{1,0:T(8,128)(2,1)} %broadcast_select_fusion.2), channel_id=1, source_target_pairs={{0,2},{1,3},{2,0},{3,1},{4,6},{5,7},{6,4},{7,5},{8,10},{9,11},{10,... | collective-permute-start | bytes 1179656 | tf_op jit(solution)/shard_map/ppermute | solution.py:57
  287.3 34.0 %collective-permute-start.62 = (bf16[576,384]{1,0:T(8,128)(2,1)}, bf16[576,384]{1,0:T(8,128)(2,1)S(1)}, u32[]{:S(2)}, u32[]{:S(2)}) collective-permute-start(bf16[576,384]{1,0:T(8,128)(2,1)} %get-tuple-element.182), channel_id=1, source_target_pairs={{0,8},{4,12},{8,0},{12,4},{16,24},{20,28},{24,16},{28,20},{1,9},{5... | collective-permute-start | bytes 1327112 | tf_op jit(solution)/shard_map/ppermute | solution.py:64
  302.3 17.4 %collective-permute-start.59 = (f32[2,384]{1,0:T(2,128)S(1)}, f32[2,384]{1,0:T(2,128)S(1)}, u32[]{:S(2)}, u32[]{:S(2)}) collective-permute-start(f32[2,384]{1,0:T(2,128)S(1)} %pad_maximum_fusion.2), channel_id=1, source_target_pairs={{0,4},{4,0},{8,12},{12,8},{16,20},{20,16},{24,28},{28,24},{1,5},{5... | collective-permute-start | bytes 9224 | tf_op jit(solution)/shard_map/ppermute | solution.py:51
  305.2 25.4 %collective-permute-start.63 = (bf16[576,384]{1,0:T(8,128)(2,1)S(1)}, bf16[576,384]{1,0:T(8,128)(2,1)S(1)}, u32[]{:S(2)}, u32[]{:S(2)}) collective-permute-start(bf16[576,384]{1,0:T(8,128)(2,1)S(1)} %copy-done.31), channel_id=1, source_target_pairs={{0,16},{4,20},{8,24},{12,28},{16,0},{20,4},{24,8},{28,12},{1,17},{... | collective-permute-start | bytes 1327112 | tf_op jit(solution)/shard_map/ppermute | solution.py:64
  319.1 22.9 %collective-permute-start.66 = (bf16[768,384]{1,0:T(8,128)(2,1)S(1)}, bf16[768,384]{1,0:T(8,128)(2,1)S(1)}, u32[]{:S(2)}, u32[]{:S(2)}) collective-permute-start(bf16[768,384]{1,0:T(8,128)(2,1)S(1)} %get-tuple-element.191), channel_id=1, source_target_pairs={{0,4},{4,0},{8,12},{12,8},{16,20},{20,16},{24,28},{28,24},{1,5},{5... | collective-permute-start | bytes 1769480 | tf_op jit(solution)/shard_map/ppermute | solution.py:51
  319.7 13.5 %collective-permute-start.60 = (f32[2,384]{1,0:T(2,128)S(1)}, f32[2,384]{1,0:T(2,128)S(1)}, u32[]{:S(2)}, u32[]{:S(2)}) collective-permute-start(f32[2,384]{1,0:T(2,128)S(1)} %fusion.12), channel_id=1, source_target_pairs={{0,8},{4,12},{8,0},{12,4},{16,24},{20,28},{24,16},{28,20},{1,9},{5... | collective-permute-start | bytes 9224 | tf_op jit(solution)/shard_map/ppermute | solution.py:51
  319.9 19.7 %collective-permute-start.44 = (bf16[256,384]{1,0:T(8,128)(2,1)S(1)}, bf16[256,384]{1,0:T(8,128)(2,1)S(1)}, u32[]{:S(2)}, u32[]{:S(2)}) collective-permute-start(bf16[256,384]{1,0:T(8,128)(2,1)S(1)} %broadcast_select_fusion.5), channel_id=1, source_target_pairs={{0,4},{4,0},{8,12},{12,8},{16,20},{20,16},{24,28},{28,24},{1,5},{5... | collective-permute-start | bytes 589832 | tf_op jit(solution)/shard_map/ppermute | solution.py:51
  331.6 13.1 %collective-permute-start.64 = (bf16[288,384]{1,0:T(8,128)(2,1)S(1)}, bf16[288,384]{1,0:T(8,128)(2,1)S(1)}, u32[]{:S(2)}, u32[]{:S(2)}) collective-permute-start(bf16[288,384]{1,0:T(8,128)(2,1)S(1)} %get-tuple-element.184), channel_id=1, source_target_pairs={{0,4},{4,0},{8,12},{12,8},{16,20},{20,16},{24,28},{28,24},{1,5},{5... | collective-permute-start | bytes 663560 | tf_op jit(solution)/shard_map/ppermute | solution.py:51
  (94 other events, 838.4 us)

commit v6 on v5

--- a/solution.py
+++ b/solution.py
@@ -126,14 +126,16 @@
     if not place.lined:
         return None, None
     rows, cols = started[1].shape
-    at = slice(part * (rows // count), (part + 1) * (rows // count))
+    cut = rows if count == 1 else rows * 2 // 3
+    at = slice(0, cut) if part == 0 else slice(cut, rows)
+    size = at.stop - at.start
     (summed,) = call(
         partial(add_body, rows=at),
-        [((rows // count, cols), bf16)],
+        [((size, cols), bf16)],
         place.table,
         [],
         [started[1:3]],
-        [pltpu.VMEM((rows // count, cols), bf16)] * 2 + [pltpu.SemaphoreType.DMA((2,))],
+        [pltpu.VMEM((size, cols), bf16)] * 2 + [pltpu.SemaphoreType.DMA((2,))],
         earlier=[started[4]] + list(earlier),
     )
     return summed, place.send_z(summed, SECOND)

time: 348 us -> 346 us (level)
  starting transfers between devices: 81.8 us -> 76.1 us
    ppermute x23, starting transfers between devices: 47.8 us -> 43.5 us  [send_z(): return lax.ppermute(value, 'gx', pairs)]
    ppermute x16, waiting for transfers between devices: 46.4 us -> 42.7 us  [swap_gx(): return lax.ppermute(value, 'gx', [(i, i ^ bit) for i in range(self.nx)])]
    ppermute x23, waiting for transfers between devices: 109 us -> 113 us  [send_z(): return lax.ppermute(value, 'gx', pairs)]
    unnamed x119 -> x117, local copies, waits for them, and re-layouts: 7.84 us -> 8.51 us
  transfers between devices with their start and end apart: 67 -> 67, of which waited for: 35 -> 36; matrix products, arithmetic and copies ran while one was open for 6% -> 6% of each run, Pallas kernels for 10% -> 10%
where the time goes in v6:
time: 346 us; the launch traced here: 345 us
  waiting for transfers between devices  177 us (51%)
  starting transfers between devices  76.1 us (22%)
  Pallas kernels  61.6 us (18%)
  other arithmetic  18.4 us (5%)
  local copies, waits for them, and re-layouts  10 us (3%)
    ppermute x23, waiting for transfers between devices, send_z(): return lax.ppermute(value, 'gx', pairs)  113 us
    pallas_call x22, Pallas kernels, call(): pl.pallas_call(kernel, out_shape=[jax.ShapeDtypeStruct(shape, dtype) for...  61.6 us
    ppermute x23, starting transfers between devices, send_z(): return lax.ppermute(value, 'gx', pairs)  43.5 us
    ppermute x16, waiting for transfers between devices, swap_gx(): return lax.ppermute(value, 'gx', [(i, i ^ bit) for i in range(self.nx)])  42.7 us
    ppermute x16, starting transfers between devices, swap_gx(): return lax.ppermute(value, 'gx', [(i, i ^ bit) for i in range(self.nx)])  18.6 us
    ppermute x9, waiting for transfers between devices, swap_x(): return lax.ppermute(value, 'gy', [(i, i ^ 2) for i in range(self.ny)])  11.9 us
    ppermute x9, starting transfers between devices, swap_x(): return lax.ppermute(value, 'gy', [(i, i ^ 2) for i in range(self.ny)])  10.6 us
    ppermute x19, waiting for transfers between devices, swap_c(): return lax.ppermute(value, 'gy', [(i, i ^ 1) for i in range(self.ny)])  9.76 us
  transfers between devices with their start and end apart: 67, of which 36 were waited for; matrix products, arithmetic and copies ran while one was open for 6% of the time, Pallas kernels for 10%

profile of v6, /device:TPU:0, one launch (start us, length us, event | category | flops | bytes accessed | tf_op | source)
XLA Modules:
  0.0 344.8 jit_solution(9186502685907295879)
XLA Ops:
  6.2 3.0 collective-permute-start
  9.2 5.4 %collective-permute-done.refs_1_ = bf16[288,384]{1,0:T(8,128)(2,1)S(1)} collective-permute-done((bf16[288,384]{1,0:T(8,128)(2,1)S(1)}, bf16[288,384]{1,0:T(8,128)(2,1)S(1)}, u32[]{:S(2)}, u32[]{:S(2)}) %collective-permute-start) | collective-permute-done | bytes 221216 | tf_op jit(solution)/shard_map/ppermute | solution.py:51
  15.4 2.9 collective-permute-start.13
  23.9 14.3 %collective-permute-done.13.refs_5_ = bf16[576,384]{1,0:T(8,128)(2,1)S(1)} collective-permute-done((bf16[576,384]{1,0:T(8,128)(2,1)S(1)}, bf16[576,384]{1,0:T(8,128)(2,1)S(1)}, u32[]{:S(2)}, u32[]{:S(2)}) %collective-permute-start.13) | collective-permute-done | bytes 442400 | tf_op jit(solution)/shard_map/ppermute | solution.py:64
  42.2 8.3 %collective-permute-done.15.refs_7_ = bf16[576,384]{1,0:T(8,128)(2,1)S(1)} collective-permute-done((bf16[576,384]{1,0:T(8,128)(2,1)S(1)}, bf16[576,384]{1,0:T(8,128)(2,1)S(1)}, u32[]{:S(2)}, u32[]{:S(2)}) %collective-permute-start.15) | collective-permute-done | bytes 442400 | tf_op jit(solution)/shard_map/ppermute | solution.py:64
  50.5 4.6 %collective-permute-start.20 = (bf16[1536,384]{1,0:T(8,128)(2,1)S(1)}, bf16[1536,384]{1,0:T(8,128)(2,1)S(1)}, u32[]{:S(2)}, u32[]{:S(2)}) collective-permute-start(bf16[1536,384]{1,0:T(8,128)(2,1)S(1)} %shard_map.199.refs_2_), channel_id=1, source_target_pairs={{0,16},{4,20},{8,24},{12,28},{16,0},{20,4},{24,8},{28,12},{1,17},{... | collective-permute-start | bytes 3538952 | tf_op jit(solution)/shard_map/ppermute | solution.py:64
  61.6 9.7 %collective-permute-done.3.refs_2_ = bf16[512,384]{1,0:T(8,128)(2,1)S(1)} collective-permute-done((bf16[512,384]{1,0:T(8,128)(2,1)S(1)}, bf16[512,384]{1,0:T(8,128)(2,1)S(1)}, u32[]{:S(2)}, u32[]{:S(2)}) %collective-permute-start.3) | collective-permute-done | bytes 393248 | tf_op jit(solution)/shard_map/ppermute | solution.py:51
  71.3 7.5 %collective-permute-done.4.refs_3_ = bf16[512,384]{1,0:T(8,128)(2,1)S(1)} collective-permute-done((bf16[512,384]{1,0:T(8,128)(2,1)S(1)}, bf16[512,384]{1,0:T(8,128)(2,1)S(1)}, u32[]{:S(2)}, u32[]{:S(2)}) %collective-permute-start.4) | collective-permute-done | bytes 393248 | tf_op jit(solution)/shard_map/ppermute | solution.py:51
  80.6 2.4 shard_map.197
  83.0 3.3 shard_map.198
  90.9 15.6 %collective-permute-done.16.refs_2_ = bf16[192,512]{1,0:T(8,128)(2,1)S(1)} collective-permute-done((bf16[192,512]{1,0:T(8,128)(2,1)S(1)}, bf16[192,512]{1,0:T(8,128)(2,1)S(1)}, u32[]{:S(2)}, u32[]{:S(2)}) %collective-permute-start.16) | collective-permute-done | bytes 196640 | tf_op jit(solution)/shard_map/ppermute | solution.py:64
  106.5 2.3 collective-permute-done.17.refs_3_
  110.9 5.2 %shard_map.200 = (f32[192,512]{1,0:T(8,128)S(1)}, bf16[192,512]{1,0:T(8,128)(2,1)S(1)}, f32[2,1,512]{2,1,0:T(1,128)S(1)}, bf16[192,1024]{1,0:T(8,128)(2,1)S(1)},...) custom-call(s32[11]{0:T(128)S(1)} %concatenate.6.table_ref, ...), custom_call_target="tpu_custom_call" | custom-call | tf_op jit(solution)/shard_map/pallas_call | solution.py:223
  123.4 6.4 %collective-permute-done.23 = bf16[512,384]{1,0:T(8,128)(2,1)S(1)} collective-permute-done((bf16[512,384]{1,0:T(8,128)(2,1)S(1)}, bf16[512,384]{1,0:T(8,128)(2,1)S(1)}, u32[]{:S(2)}, u32[]{:S(2)}) %collective-permute-start.23) | collective-permute-done | bytes 393248 | tf_op jit(solution)/shard_map/ppermute | solution.py:57
  132.9 7.9 %collective-permute-done.25 = bf16[512,384]{1,0:T(8,128)(2,1)S(1)} collective-permute-done((bf16[512,384]{1,0:T(8,128)(2,1)S(1)}, bf16[512,384]{1,0:T(8,128)(2,1)S(1)}, u32[]{:S(2)}, u32[]{:S(2)}) %collective-permute-start.25) | collective-permute-done | bytes 393248 | tf_op jit(solution)/shard_map/ppermute | solution.py:51
  142.2 19.2 %collective-permute-done.28.refs_6_ = bf16[1536,384]{1,0:T(8,128)(2,1)S(1)} collective-permute-done((bf16[1536,384]{1,0:T(8,128)(2,1)S(1)}, bf16[1536,384]{1,0:T(8,128)(2,1)S(1)}, u32[]{:S(2)}, u32[]{:S(2)}) %collective-permute-start.28) | collective-permute-done | bytes 1179680 | tf_op jit(solution)/shard_map/ppermute | solution.py:64
  165.6 10.1 %shard_map.202 = (bf16[512,512]{1,0:T(8,128)(2,1)S(1)}, bf16[512,1024]{1,0:T(8,128)(2,1)S(1)}, bf16[512,384]{1,0:T(8,128)(2,1)S(1)}, bf16[512,384]{1,0:T(8,128)(...) custom-call(s32[11]{0:T(128)S(1)} %concatenate.6.table_ref, ...), custom_call_target="tpu_custom_call" | custom-call | tf_op jit(solution)/shard_map/pallas_call | solution.py:223
  180.8 2.4 collective-permute-start.37
  183.9 4.0 %shard_map.204 = (bf16[1536,384]{1,0:T(8,128)(2,1)S(1)}, bf16[1536,384]{1,0:T(8,128)(2,1)S(1)}, bf16[1536,384]{1,0:T(8,128)(2,1)S(1)}) custom-call(s32[11]{0:T(128)S(1)} %concatenate.6.table_ref, bf16[1536,512]{1,0:T(8,128)(2,1)S(1)} %get-tuple-element.134.refs_0_, bf16[4,512,384]{2,1,0:T(8,128)(2,1)S(1)} %get-tuple-element.129.refs_0_.refs_1_, ...), custom_call_target="tpu_custom_call" | custom-call | tf_op jit(solution)/shard_map/pallas_call | solution.py:223
  195.8 4.1 %collective-permute-done.35 = bf16[512,384]{1,0:T(8,128)(2,1)S(1)} collective-permute-done((bf16[512,384]{1,0:T(8,128)(2,1)S(1)}, bf16[512,384]{1,0:T(8,128)(2,1)S(1)}, u32[]{:S(2)}, u32[]{:S(2)}) %collective-permute-start.35) | collective-permute-done | bytes 393248 | tf_op jit(solution)/shard_map/ppermute | solution.py:51
  200.3 9.2 %collective-permute-done.37.refs_16_.refs_1_ = bf16[1536,384]{1,0:T(8,128)(2,1)S(1)} collective-permute-done((bf16[1536,384]{1,0:T(8,128)(2,1)S(1)}, bf16[1536,384]{1,0:T(8,128)(2,1)S(1)}, u32[]{:S(2)}, u32[]{:S(2)}) %collective-permute-start.37) | collective-permute-done | bytes 1179680 | tf_op jit(solution)/shard_map/ppermute | solution.py:64
  212.1 4.2 %collective-permute-start.49 = (bf16[1024,384]{1,0:T(8,128)(2,1)S(1)}, bf16[1024,384]{1,0:T(8,128)(2,1)S(1)}, u32[]{:S(2)}, u32[]{:S(2)}) collective-permute-start(bf16[1024,384]{1,0:T(8,128)(2,1)S(1)} %shard_map.208), channel_id=1, source_target_pairs={{0,16},{4,20},{8,24},{12,28},{16,0},{20,4},{24,8},{28,12},{1,17},{... | collective-permute-start | bytes 2359304 | tf_op jit(solution)/shard_map/ppermute | solution.py:64
  218.0 8.2 %shard_map.206 = (bf16[4,512,384]{2,1,0:T(8,128)(2,1)S(1)}, f32[512,1]{1,0:T(8,128)S(1)}, bf16[192,512]{1,0:T(8,128)(2,1)S(1)}, f32[192,512]{1,0:T(8,128)S(1)}, ...) custom-call(s32[11]{0:T(128)S(1)} %concatenate.6.table_ref, ...), custom_call_target="tpu_custom_call" | custom-call | tf_op jit(solution)/shard_map/pallas_call | solution.py:223
  233.1 6.5 %collective-permute-done.48.refs_15_.refs_1_ = bf16[1536,384]{1,0:T(8,128)(2,1)S(1)} collective-permute-done((bf16[1536,384]{1,0:T(8,128)(2,1)S(1)}, bf16[1536,384]{1,0:T(8,128)(2,1)S(1)}, u32[]{:S(2)}, u32[]{:S(2)}) %collective-permute-start.48) | collective-permute-done | bytes 1179680 | tf_op jit(solution)/shard_map/ppermute | solution.py:64
  241.8 26.1 %collective-permute-done.46.refs_6_ = bf16[192,512]{1,0:T(8,128)(2,1)S(1)} collective-permute-done((bf16[192,512]{1,0:T(8,128)(2,1)S(1)}, bf16[192,512]{1,0:T(8,128)(2,1)S(1)}, u32[]{:S(2)}, u32[]{:S(2)}) %collective-permute-start.46) | collective-permute-done | bytes 196640 | tf_op jit(solution)/shard_map/ppermute | solution.py:64
  267.9 4.5 %shard_map.209 = (bf16[576,384]{1,0:T(8,128)(2,1)S(1)}, bf16[576,384]{1,0:T(8,128)(2,1)}, bf16[576,384]{1,0:T(8,128)(2,1)S(1)}, bf16[576,384]{1,0:T(8,128)(2,1)S...) custom-call(s32[11]{0:T(128)S(1)} %concatenate.6.table_ref, ...), custom_call_target="tpu_custom_call", output_to_operand_aliasing={{0}: (1, {}), {1}: (2, {}), {2}: (3, {}), {3}: (4, {})} | custom-call | tf_op jit(solution)/shard_map/pallas_call | solution.py:223
  304.1 2.6 collective-permute-done.55
  306.7 2.7 fusion.6
  313.4 8.0 %collective-permute-start.63 = (bf16[576,384]{1,0:T(8,128)(2,1)S(1)}, bf16[576,384]{1,0:T(8,128)(2,1)S(1)}, u32[]{:S(2)}, u32[]{:S(2)}) collective-permute-start(bf16[576,384]{1,0:T(8,128)(2,1)S(1)} %shard_map.210), channel_id=1, source_target_pairs={{0,16},{4,20},{8,24},{12,28},{16,0},{20,4},{24,8},{28,12},{1,17},{... | collective-permute-start | bytes 1327112 | tf_op jit(solution)/shard_map/ppermute | solution.py:64
  325.7 6.8 %collective-permute-done.63.refs_3_ = bf16[576,384]{1,0:T(8,128)(2,1)S(1)} collective-permute-done((bf16[576,384]{1,0:T(8,128)(2,1)S(1)}, bf16[576,384]{1,0:T(8,128)(2,1)S(1)}, u32[]{:S(2)}, u32[]{:S(2)}) %collective-permute-start.63) | collective-permute-done | bytes 442400 | tf_op jit(solution)/shard_map/ppermute | solution.py:64
  334.4 3.2 collective-permute-done.44
  340.0 2.7 shard_map.215
  (289 shorter events, 119.7 us)
Async XLA Ops:
  15.4 22.9 %collective-permute-start.13 = (bf16[576,384]{1,0:T(8,128)(2,1)S(1)}, bf16[576,384]{1,0:T(8,128)(2,1)S(1)}, u32[]{:S(2)}, u32[]{:S(2)}) collective-permute-start(bf16[576,384]{1,0:T(8,128)(2,1)S(1)} %shard_map.195.refs_3_), channel_id=1, source_target_pairs={{0,16},{4,20},{8,24},{12,28},{16,0},{20,4},{24,8},{28,12},{1,17},{... | collective-permute-start | bytes 1327112 | tf_op jit(solution)/shard_map/ppermute | solution.py:64
  20.1 21.1 %collective-permute-start.2 = (bf16[768,384]{1,0:T(8,128)(2,1)S(1)}, bf16[768,384]{1,0:T(8,128)(2,1)S(1)}, u32[]{:S(2)}, u32[]{:S(2)}) collective-permute-start(bf16[768,384]{1,0:T(8,128)(2,1)S(1)} %get-tuple-element.106), channel_id=1, source_target_pairs={{0,4},{4,0},{8,12},{12,8},{16,20},{20,16},{24,28},{28,24},{1,5},{5... | collective-permute-start | bytes 1769480 | tf_op jit(solution)/shard_map/ppermute | solution.py:51
  21.7 20.5 %collective-permute-start.12 = (bf16[576,384]{1,0:T(8,128)(2,1)S(1)}, bf16[576,384]{1,0:T(8,128)(2,1)S(1)}, u32[]{:S(2)}, u32[]{:S(2)}) collective-permute-start(bf16[576,384]{1,0:T(8,128)(2,1)S(1)} %shard_map.195.refs_3_), channel_id=1, source_target_pairs={{0,8},{4,12},{8,0},{12,4},{16,24},{20,28},{24,16},{28,20},{1,9},{5... | collective-permute-start | bytes 1327112 | tf_op jit(solution)/shard_map/ppermute | solution.py:64
  23.3 18.9 %collective-permute-start.14 = (bf16[576,384]{1,0:T(8,128)(2,1)S(1)}, bf16[576,384]{1,0:T(8,128)(2,1)S(1)}, u32[]{:S(2)}, u32[]{:S(2)}) collective-permute-start(bf16[576,384]{1,0:T(8,128)(2,1)S(1)} %shard_map.195.refs_3_), channel_id=1, source_target_pairs={{8,16},{12,20},{16,8},{20,12},{9,17},{13,21},{17,9},{21,13},{10,18... | collective-permute-start | bytes 1327112 | tf_op jit(solution)/shard_map/ppermute | solution.py:64
  38.3 12.2 %collective-permute-start.15 = (bf16[576,384]{1,0:T(8,128)(2,1)S(1)}, bf16[576,384]{1,0:T(8,128)(2,1)S(1)}, u32[]{:S(2)}, u32[]{:S(2)}) collective-permute-start(bf16[576,384]{1,0:T(8,128)(2,1)S(1)} %collective-permute-done.13.refs_5_), channel_id=1, source_target_pairs={{8,0},{12,4},{16,24},{20,28},{9,1},{13,5},{17,25},{21,29},{10,2},{... | collective-permute-start | bytes 1327112 | tf_op jit(solution)/shard_map/ppermute | solution.py:64
  39.6 19.2 %collective-permute-start.1 = (bf16[512,384]{1,0:T(8,128)(2,1)S(1)}, bf16[512,384]{1,0:T(8,128)(2,1)S(1)}, u32[]{:S(2)}, u32[]{:S(2)}) collective-permute-start(bf16[512,384]{1,0:T(8,128)(2,1)S(1)} %pad_maximum_fusion.refs_0_), channel_id=1, source_target_pairs={{0,2},{1,3},{2,0},{3,1},{4,6},{5,7},{6,4},{7,5},{8,10},{9,11},{10,... | collective-permute-start | bytes 1179656 | tf_op jit(solution)/shard_map/ppermute | solution.py:57
  50.5 60.4 %collective-permute-start.19 = (bf16[1536,384]{1,0:T(8,128)(2,1)S(1)}, bf16[1536,384]{1,0:T(8,128)(2,1)S(1)}, u32[]{:S(2)}, u32[]{:S(2)}) collective-permute-start(bf16[1536,384]{1,0:T(8,128)(2,1)S(1)} %shard_map.199.refs_2_), channel_id=1, source_target_pairs={{0,8},{4,12},{8,0},{12,4},{16,24},{20,28},{24,16},{28,20},{1,9},{5... | collective-permute-start | bytes 3538952 | tf_op jit(solution)/shard_map/ppermute | solution.py:64
  50.5 60.4 %collective-permute-start.20 = (bf16[1536,384]{1,0:T(8,128)(2,1)S(1)}, bf16[1536,384]{1,0:T(8,128)(2,1)S(1)}, u32[]{:S(2)}, u32[]{:S(2)}) collective-permute-start(bf16[1536,384]{1,0:T(8,128)(2,1)S(1)} %shard_map.199.refs_2_), channel_id=1, source_target_pairs={{0,16},{4,20},{8,24},{12,28},{16,0},{20,4},{24,8},{28,12},{1,17},{... | collective-permute-start | bytes 3538952 | tf_op jit(solution)/shard_map/ppermute | solution.py:64
  59.3 12.0 %collective-permute-start.3 = (bf16[512,384]{1,0:T(8,128)(2,1)S(1)}, bf16[512,384]{1,0:T(8,128)(2,1)S(1)}, u32[]{:S(2)}, u32[]{:S(2)}) collective-permute-start(bf16[512,384]{1,0:T(8,128)(2,1)S(1)} %pad_maximum_fusion.refs_0_), channel_id=1, source_target_pairs={{0,4},{4,0},{8,12},{12,8},{16,20},{20,16},{24,28},{28,24},{1,5},{5... | collective-permute-start | bytes 1179656 | tf_op jit(solution)/shard_map/ppermute | solution.py:51
  60.8 18.0 %collective-permute-start.4 = (bf16[512,384]{1,0:T(8,128)(2,1)S(1)}, bf16[512,384]{1,0:T(8,128)(2,1)S(1)}, u32[]{:S(2)}, u32[]{:S(2)}) collective-permute-start(bf16[512,384]{1,0:T(8,128)(2,1)S(1)} %collective-permute-done.1.refs_1_), channel_id=1, source_target_pairs={{0,4},{4,0},{8,12},{12,8},{16,20},{20,16},{24,28},{28,24},{1,5},{5... | collective-permute-start | bytes 1179656 | tf_op jit(solution)/shard_map/ppermute | solution.py:51
  61.5 17.9 %collective-permute-start.6 = (bf16[512,384]{1,0:T(8,128)(2,1)S(1)}, bf16[512,384]{1,0:T(8,128)(2,1)S(1)}, u32[]{:S(2)}, u32[]{:S(2)}) collective-permute-start(bf16[512,384]{1,0:T(8,128)(2,1)S(1)} %collective-permute-done.1.refs_1_), channel_id=1, source_target_pairs={{0,1},{1,0},{2,3},{3,2},{4,5},{5,4},{6,7},{7,6},{8,9},{9,8},{10,11... | collective-permute-start | bytes 1179656 | tf_op jit(solution)/shard_map/ppermute | solution.py:60
  86.3 20.1 %collective-permute-start.16 = (bf16[192,512]{1,0:T(8,128)(2,1)S(1)}, bf16[192,512]{1,0:T(8,128)(2,1)S(1)}, u32[]{:S(2)}, u32[]{:S(2)}) collective-permute-start(bf16[192,512]{1,0:T(8,128)(2,1)S(1)} %get-tuple-element.111.refs_1_.refs_10_.refs_13_), channel_id=1, source_target_pairs={{0,8},{4,12},{8,16},{12,20},{1,9},{5,13},{9,17},{13,21},{2,10},{6,... | collective-permute-start | bytes 589832 | tf_op jit(solution)/shard_map/ppermute | solution.py:64
  88.2 20.5 %collective-permute-start.17 = (bf16[192,512]{1,0:T(8,128)(2,1)S(1)}, bf16[192,512]{1,0:T(8,128)(2,1)S(1)}, u32[]{:S(2)}, u32[]{:S(2)}) collective-permute-start(bf16[192,512]{1,0:T(8,128)(2,1)S(1)} %get-tuple-element.111.refs_1_.refs_10_.refs_13_), channel_id=1, source_target_pairs={{0,16},{4,20},{8,24},{12,28},{1,17},{5,21},{9,25},{13,29},{2,18},{... | collective-permute-start | bytes 589832 | tf_op jit(solution)/shard_map/ppermute | solution.py:64
  89.6 21.3 %collective-permute-start.18 = (bf16[192,512]{1,0:T(8,128)(2,1)S(1)}, bf16[192,512]{1,0:T(8,128)(2,1)S(1)}, u32[]{:S(2)}, u32[]{:S(2)}) collective-permute-start(bf16[192,512]{1,0:T(8,128)(2,1)S(1)} %get-tuple-element.111.refs_1_.refs_10_.refs_13_), channel_id=1, source_target_pairs={{0,24},{4,28},{1,25},{5,29},{2,26},{6,30},{3,27},{7,31}} | collective-permute-start | bytes 589832 | tf_op jit(solution)/shard_map/ppermute | solution.py:64
  121.4 20.9 %collective-permute-start.27 = (bf16[1536,384]{1,0:T(8,128)(2,1)S(1)}, bf16[1536,384]{1,0:T(8,128)(2,1)S(1)}, u32[]{:S(2)}, u32[]{:S(2)}) collective-permute-start(bf16[1536,384]{1,0:T(8,128)(2,1)S(1)} %shard_map.199.refs_2_), channel_id=1, source_target_pairs={{8,16},{12,20},{16,8},{20,12},{9,17},{13,21},{17,9},{21,13},{10,18... | collective-permute-start | bytes 3538952 | tf_op jit(solution)/shard_map/ppermute | solution.py:64
  122.1 39.3 %collective-permute-start.28 = (bf16[1536,384]{1,0:T(8,128)(2,1)S(1)}, bf16[1536,384]{1,0:T(8,128)(2,1)S(1)}, u32[]{:S(2)}, u32[]{:S(2)}) collective-permute-start(bf16[1536,384]{1,0:T(8,128)(2,1)S(1)} %collective-permute-done.20.refs_7_.refs_4_), channel_id=1, source_target_pairs={{8,0},{12,4},{16,24},{20,28},{9,1},{13,5},{17,25},{21,29},{10,2},{... | collective-permute-start | bytes 3538952 | tf_op jit(solution)/shard_map/ppermute | solution.py:64
  180.8 28.7 %collective-permute-start.37 = (bf16[1536,384]{1,0:T(8,128)(2,1)S(1)}, bf16[1536,384]{1,0:T(8,128)(2,1)S(1)}, u32[]{:S(2)}, u32[]{:S(2)}) collective-permute-start(bf16[1536,384]{1,0:T(8,128)(2,1)S(1)} %get-tuple-element.147), channel_id=1, source_target_pairs={{0,8},{4,12},{24,16},{28,20},{1,9},{5,13},{25,17},{29,21},{2,10},{... | collective-permute-start | bytes 3538952 | tf_op jit(solution)/shard_map/ppermute | solution.py:64
  183.2 26.3 %collective-permute-start.38 = (bf16[1536,384]{1,0:T(8,128)(2,1)S(1)}, bf16[1536,384]{1,0:T(8,128)(2,1)S(1)}, u32[]{:S(2)}, u32[]{:S(2)}) collective-permute-start(bf16[1536,384]{1,0:T(8,128)(2,1)S(1)} %get-tuple-element.147), channel_id=1, source_target_pairs={{8,16},{12,20},{16,8},{20,12},{9,17},{13,21},{17,9},{21,13},{10,18... | collective-permute-start | bytes 3538952 | tf_op jit(solution)/shard_map/ppermute | solution.py:64
  193.6 46.0 %collective-permute-start.48 = (bf16[1536,384]{1,0:T(8,128)(2,1)S(1)}, bf16[1536,384]{1,0:T(8,128)(2,1)S(1)}, u32[]{:S(2)}, u32[]{:S(2)}) collective-permute-start(bf16[1536,384]{1,0:T(8,128)(2,1)S(1)} %get-tuple-element.171), channel_id=1, source_target_pairs={{0,8},{4,12},{8,0},{12,4},{16,24},{20,28},{24,16},{28,20},{1,9},{5... | collective-permute-start | bytes 3538952 | tf_op jit(solution)/shard_map/ppermute | solution.py:64
  212.1 55.8 %collective-permute-start.49 = (bf16[1024,384]{1,0:T(8,128)(2,1)S(1)}, bf16[1024,384]{1,0:T(8,128)(2,1)S(1)}, u32[]{:S(2)}, u32[]{:S(2)}) collective-permute-start(bf16[1024,384]{1,0:T(8,128)(2,1)S(1)} %shard_map.208), channel_id=1, source_target_pairs={{0,16},{4,20},{8,24},{12,28},{16,0},{20,4},{24,8},{28,12},{1,17},{... | collective-permute-start | bytes 2359304 | tf_op jit(solution)/shard_map/ppermute | solution.py:64
  227.0 14.8 %collective-permute-start.45 = (bf16[192,512]{1,0:T(8,128)(2,1)S(1)}, bf16[192,512]{1,0:T(8,128)(2,1)S(1)}, u32[]{:S(2)}, u32[]{:S(2)}) collective-permute-start(bf16[192,512]{1,0:T(8,128)(2,1)S(1)} %get-tuple-element.167), channel_id=1, source_target_pairs={{8,0},{12,4},{16,8},{20,12},{9,1},{13,5},{17,9},{21,13},{10,2},{14... | collective-permute-start | bytes 589832 | tf_op jit(solution)/shard_map/ppermute | solution.py:64
  228.3 39.6 %collective-permute-start.46 = (bf16[192,512]{1,0:T(8,128)(2,1)S(1)}, bf16[192,512]{1,0:T(8,128)(2,1)S(1)}, u32[]{:S(2)}, u32[]{:S(2)}) collective-permute-start(bf16[192,512]{1,0:T(8,128)(2,1)S(1)} %get-tuple-element.168), channel_id=1, source_target_pairs={{16,0},{20,4},{24,8},{28,12},{17,1},{21,5},{25,9},{29,13},{18,2},{... | collective-permute-start | bytes 589832 | tf_op jit(solution)/shard_map/ppermute | solution.py:64
  229.6 38.3 %collective-permute-start.47 = (bf16[192,512]{1,0:T(8,128)(2,1)S(1)}, bf16[192,512]{1,0:T(8,128)(2,1)S(1)}, u32[]{:S(2)}, u32[]{:S(2)}) collective-permute-start(bf16[192,512]{1,0:T(8,128)(2,1)S(1)} %get-tuple-element.169), channel_id=1, source_target_pairs={{24,0},{28,4},{25,1},{29,5},{26,2},{30,6},{27,3},{31,7}} | collective-permute-start | bytes 589832 | tf_op jit(solution)/shard_map/ppermute | solution.py:64
  281.0 14.7 %collective-permute-start.53 = (bf16[576,384]{1,0:T(8,128)(2,1)S(1)}, bf16[576,384]{1,0:T(8,128)(2,1)S(1)}, u32[]{:S(2)}, u32[]{:S(2)}) collective-permute-start(bf16[576,384]{1,0:T(8,128)(2,1)S(1)} %copy-done.31), channel_id=1, source_target_pairs={{0,8},{4,12},{24,16},{28,20},{1,9},{5,13},{25,17},{29,21},{2,10},{... | collective-permute-start | bytes 1327112 | tf_op jit(solution)/shard_map/ppermute | solution.py:64
  282.3 14.8 %collective-permute-start.54 = (bf16[576,384]{1,0:T(8,128)(2,1)S(1)}, bf16[576,384]{1,0:T(8,128)(2,1)S(1)}, u32[]{:S(2)}, u32[]{:S(2)}) collective-permute-start(bf16[576,384]{1,0:T(8,128)(2,1)S(1)} %copy-done.31), channel_id=1, source_target_pairs={{8,16},{12,20},{16,8},{20,12},{9,17},{13,21},{17,9},{21,13},{10,18... | collective-permute-start | bytes 1327112 | tf_op jit(solution)/shard_map/ppermute | solution.py:64
  290.7 30.7 %collective-permute-start.65 = (bf16[512,384]{1,0:T(8,128)(2,1)}, bf16[512,384]{1,0:T(8,128)(2,1)}, u32[]{:S(2)}, u32[]{:S(2)}) collective-permute-start(bf16[512,384]{1,0:T(8,128)(2,1)} %shard_map.213), channel_id=1, source_target_pairs={{0,16},{4,20},{8,24},{12,28},{16,0},{20,4},{24,8},{28,12},{1,17},{... | collective-permute-start | bytes 1179656 | tf_op jit(solution)/shard_map/ppermute | solution.py:64
  295.1 17.0 %collective-permute-start.43 = (bf16[512,384]{1,0:T(8,128)(2,1)}, bf16[512,384]{1,0:T(8,128)(2,1)}, u32[]{:S(2)}, u32[]{:S(2)}) collective-permute-start(bf16[512,384]{1,0:T(8,128)(2,1)} %broadcast_select_fusion.2), channel_id=1, source_target_pairs={{0,2},{1,3},{2,0},{3,1},{4,6},{5,7},{6,4},{7,5},{8,10},{9,11},{10,... | collective-permute-start | bytes 1179656 | tf_op jit(solution)/shard_map/ppermute | solution.py:57
  295.7 30.1 %collective-permute-start.62 = (bf16[576,384]{1,0:T(8,128)(2,1)}, bf16[576,384]{1,0:T(8,128)(2,1)S(1)}, u32[]{:S(2)}, u32[]{:S(2)}) collective-permute-start(bf16[576,384]{1,0:T(8,128)(2,1)} %get-tuple-element.182), channel_id=1, source_target_pairs={{0,8},{4,12},{8,0},{12,4},{16,24},{20,28},{24,16},{28,20},{1,9},{5... | collective-permute-start | bytes 1327112 | tf_op jit(solution)/shard_map/ppermute | solution.py:64
  310.5 13.5 %collective-permute-start.59 = (f32[2,384]{1,0:T(2,128)S(1)}, f32[2,384]{1,0:T(2,128)S(1)}, u32[]{:S(2)}, u32[]{:S(2)}) collective-permute-start(f32[2,384]{1,0:T(2,128)S(1)} %pad_maximum_fusion.2), channel_id=1, source_target_pairs={{0,4},{4,0},{8,12},{12,8},{16,20},{20,16},{24,28},{28,24},{1,5},{5... | collective-permute-start | bytes 9224 | tf_op jit(solution)/shard_map/ppermute | solution.py:51
  313.4 19.1 %collective-permute-start.63 = (bf16[576,384]{1,0:T(8,128)(2,1)S(1)}, bf16[576,384]{1,0:T(8,128)(2,1)S(1)}, u32[]{:S(2)}, u32[]{:S(2)}) collective-permute-start(bf16[576,384]{1,0:T(8,128)(2,1)S(1)} %shard_map.210), channel_id=1, source_target_pairs={{0,16},{4,20},{8,24},{12,28},{16,0},{20,4},{24,8},{28,12},{1,17},{... | collective-permute-start | bytes 1327112 | tf_op jit(solution)/shard_map/ppermute | solution.py:64
  323.5 16.5 %collective-permute-start.66 = (bf16[768,384]{1,0:T(8,128)(2,1)S(1)}, bf16[768,384]{1,0:T(8,128)(2,1)S(1)}, u32[]{:S(2)}, u32[]{:S(2)}) collective-permute-start(bf16[768,384]{1,0:T(8,128)(2,1)S(1)} %get-tuple-element.191), channel_id=1, source_target_pairs={{0,4},{4,0},{8,12},{12,8},{16,20},{20,16},{24,28},{28,24},{1,5},{5... | collective-permute-start | bytes 1769480 | tf_op jit(solution)/shard_map/ppermute | solution.py:51
  324.2 13.4 %collective-permute-start.44 = (bf16[256,384]{1,0:T(8,128)(2,1)S(1)}, bf16[256,384]{1,0:T(8,128)(2,1)S(1)}, u32[]{:S(2)}, u32[]{:S(2)}) collective-permute-start(bf16[256,384]{1,0:T(8,128)(2,1)S(1)} %broadcast_select_fusion.5), channel_id=1, source_target_pairs={{0,4},{4,0},{8,12},{12,8},{16,20},{20,16},{24,28},{28,24},{1,5},{5... | collective-permute-start | bytes 589832 | tf_op jit(solution)/shard_map/ppermute | solution.py:51
  (93 other events, 812.6 us)

commit v7 on v6

--- a/solution.py
+++ b/solution.py
@@ -126,7 +126,7 @@
     if not place.lined:
         return None, None
     rows, cols = started[1].shape
-    cut = rows if count == 1 else rows * 2 // 3
+    cut = rows if count == 1 else rows * 5 // 8
     at = slice(0, cut) if part == 0 else slice(cut, rows)
     size = at.stop - at.start
     (summed,) = call(

time: 346 us -> 344 us (level)
    unnamed x117 -> x121, local copies, waits for them, and re-layouts: 8.51 us -> 7.86 us
  transfers between devices with their start and end apart: 67 -> 67, of which waited for: 36 -> 37; matrix products, arithmetic and copies ran while one was open for 6% -> 6% of each run, Pallas kernels for 10% -> 10%
where the time goes in v7:
time: 344 us
  waiting for transfers between devices  175 us (51%)
  starting transfers between devices  77 us (22%)
  Pallas kernels  61.7 us (18%)
  other arithmetic  18.5 us (5%)
  local copies, waits for them, and re-layouts  9.36 us (3%)
    ppermute x23, waiting for transfers between devices, send_z(): return lax.ppermute(value, 'gx', pairs)  112 us
    pallas_call x22, Pallas kernels, call(): pl.pallas_call(kernel, out_shape=[jax.ShapeDtypeStruct(shape, dtype) for...  61.7 us
    ppermute x23, starting transfers between devices, send_z(): return lax.ppermute(value, 'gx', pairs)  44.4 us
    ppermute x16, waiting for transfers between devices, swap_gx(): return lax.ppermute(value, 'gx', [(i, i ^ bit) for i in range(self.nx)])  42.2 us
    ppermute x16, starting transfers between devices, swap_gx(): return lax.ppermute(value, 'gx', [(i, i ^ bit) for i in range(self.nx)])  18.6 us
    ppermute x9, waiting for transfers between devices, swap_x(): return lax.ppermute(value, 'gy', [(i, i ^ 2) for i in range(self.ny)])  11.9 us
    ppermute x9, starting transfers between devices, swap_x(): return lax.ppermute(value, 'gy', [(i, i ^ 2) for i in range(self.ny)])  10.6 us
    ppermute x19, waiting for transfers between devices, swap_c(): return lax.ppermute(value, 'gy', [(i, i ^ 1) for i in range(self.ny)])  9.76 us
  transfers between devices with their start and end apart: 67, of which 37 were waited for; matrix products, arithmetic and copies ran while one was open for 6% of the time, Pallas kernels for 10%

profile of v7, /device:TPU:0, one launch (start us, length us, event | category | flops | bytes accessed | tf_op | source)
XLA Modules:
  0.0 343.8 jit_solution(4757612715193302577)
XLA Ops:
  6.2 3.0 collective-permute-start
  9.2 5.4 %collective-permute-done.refs_1_ = bf16[288,384]{1,0:T(8,128)(2,1)S(1)} collective-permute-done((bf16[288,384]{1,0:T(8,128)(2,1)S(1)}, bf16[288,384]{1,0:T(8,128)(2,1)S(1)}, u32[]{:S(2)}, u32[]{:S(2)}) %collective-permute-start) | collective-permute-done | bytes 221216 | tf_op jit(solution)/shard_map/ppermute | solution.py:51
  15.4 2.9 collective-permute-start.13
  23.9 14.3 %collective-permute-done.13.refs_5_ = bf16[576,384]{1,0:T(8,128)(2,1)S(1)} collective-permute-done((bf16[576,384]{1,0:T(8,128)(2,1)S(1)}, bf16[576,384]{1,0:T(8,128)(2,1)S(1)}, u32[]{:S(2)}, u32[]{:S(2)}) %collective-permute-start.13) | collective-permute-done | bytes 442400 | tf_op jit(solution)/shard_map/ppermute | solution.py:64
  42.2 8.3 %collective-permute-done.15.refs_7_ = bf16[576,384]{1,0:T(8,128)(2,1)S(1)} collective-permute-done((bf16[576,384]{1,0:T(8,128)(2,1)S(1)}, bf16[576,384]{1,0:T(8,128)(2,1)S(1)}, u32[]{:S(2)}, u32[]{:S(2)}) %collective-permute-start.15) | collective-permute-done | bytes 442400 | tf_op jit(solution)/shard_map/ppermute | solution.py:64
  50.5 4.6 %collective-permute-start.20 = (bf16[1536,384]{1,0:T(8,128)(2,1)S(1)}, bf16[1536,384]{1,0:T(8,128)(2,1)S(1)}, u32[]{:S(2)}, u32[]{:S(2)}) collective-permute-start(bf16[1536,384]{1,0:T(8,128)(2,1)S(1)} %shard_map.199.refs_2_), channel_id=1, source_target_pairs={{0,16},{4,20},{8,24},{12,28},{16,0},{20,4},{24,8},{28,12},{1,17},{... | collective-permute-start | bytes 3538952 | tf_op jit(solution)/shard_map/ppermute | solution.py:64
  61.6 9.7 %collective-permute-done.3.refs_2_ = bf16[512,384]{1,0:T(8,128)(2,1)S(1)} collective-permute-done((bf16[512,384]{1,0:T(8,128)(2,1)S(1)}, bf16[512,384]{1,0:T(8,128)(2,1)S(1)}, u32[]{:S(2)}, u32[]{:S(2)}) %collective-permute-start.3) | collective-permute-done | bytes 393248 | tf_op jit(solution)/shard_map/ppermute | solution.py:51
  71.3 7.5 %collective-permute-done.4.refs_3_ = bf16[512,384]{1,0:T(8,128)(2,1)S(1)} collective-permute-done((bf16[512,384]{1,0:T(8,128)(2,1)S(1)}, bf16[512,384]{1,0:T(8,128)(2,1)S(1)}, u32[]{:S(2)}, u32[]{:S(2)}) %collective-permute-start.4) | collective-permute-done | bytes 393248 | tf_op jit(solution)/shard_map/ppermute | solution.py:51
  80.6 2.4 shard_map.197
  83.0 3.3 shard_map.198
  90.9 15.6 %collective-permute-done.16.refs_2_ = bf16[192,512]{1,0:T(8,128)(2,1)S(1)} collective-permute-done((bf16[192,512]{1,0:T(8,128)(2,1)S(1)}, bf16[192,512]{1,0:T(8,128)(2,1)S(1)}, u32[]{:S(2)}, u32[]{:S(2)}) %collective-permute-start.16) | collective-permute-done | bytes 196640 | tf_op jit(solution)/shard_map/ppermute | solution.py:64
  106.5 2.3 collective-permute-done.17.refs_3_
  110.9 5.2 %shard_map.200 = (f32[192,512]{1,0:T(8,128)S(1)}, bf16[192,512]{1,0:T(8,128)(2,1)S(1)}, f32[2,1,512]{2,1,0:T(1,128)S(1)}, bf16[192,1024]{1,0:T(8,128)(2,1)S(1)},...) custom-call(s32[11]{0:T(128)S(1)} %concatenate.6.table_ref, ...), custom_call_target="tpu_custom_call" | custom-call | tf_op jit(solution)/shard_map/pallas_call | solution.py:223
  123.4 6.4 %collective-permute-done.23 = bf16[512,384]{1,0:T(8,128)(2,1)S(1)} collective-permute-done((bf16[512,384]{1,0:T(8,128)(2,1)S(1)}, bf16[512,384]{1,0:T(8,128)(2,1)S(1)}, u32[]{:S(2)}, u32[]{:S(2)}) %collective-permute-start.23) | collective-permute-done | bytes 393248 | tf_op jit(solution)/shard_map/ppermute | solution.py:57
  132.9 7.9 %collective-permute-done.25 = bf16[512,384]{1,0:T(8,128)(2,1)S(1)} collective-permute-done((bf16[512,384]{1,0:T(8,128)(2,1)S(1)}, bf16[512,384]{1,0:T(8,128)(2,1)S(1)}, u32[]{:S(2)}, u32[]{:S(2)}) %collective-permute-start.25) | collective-permute-done | bytes 393248 | tf_op jit(solution)/shard_map/ppermute | solution.py:51
  142.2 19.2 %collective-permute-done.28.refs_6_ = bf16[1536,384]{1,0:T(8,128)(2,1)S(1)} collective-permute-done((bf16[1536,384]{1,0:T(8,128)(2,1)S(1)}, bf16[1536,384]{1,0:T(8,128)(2,1)S(1)}, u32[]{:S(2)}, u32[]{:S(2)}) %collective-permute-start.28) | collective-permute-done | bytes 1179680 | tf_op jit(solution)/shard_map/ppermute | solution.py:64
  165.6 10.1 %shard_map.202 = (bf16[512,512]{1,0:T(8,128)(2,1)S(1)}, bf16[512,1024]{1,0:T(8,128)(2,1)S(1)}, bf16[512,384]{1,0:T(8,128)(2,1)S(1)}, bf16[512,384]{1,0:T(8,128)(...) custom-call(s32[11]{0:T(128)S(1)} %concatenate.6.table_ref, ...), custom_call_target="tpu_custom_call" | custom-call | tf_op jit(solution)/shard_map/pallas_call | solution.py:223
  180.8 2.4 collective-permute-start.37
  183.9 4.0 %shard_map.204 = (bf16[1536,384]{1,0:T(8,128)(2,1)S(1)}, bf16[1536,384]{1,0:T(8,128)(2,1)S(1)}, bf16[1536,384]{1,0:T(8,128)(2,1)S(1)}) custom-call(s32[11]{0:T(128)S(1)} %concatenate.6.table_ref, bf16[1536,512]{1,0:T(8,128)(2,1)S(1)} %get-tuple-element.134.refs_0_, bf16[4,512,384]{2,1,0:T(8,128)(2,1)S(1)} %get-tuple-element.129.refs_0_.refs_1_, ...), custom_call_target="tpu_custom_call" | custom-call | tf_op jit(solution)/shard_map/pallas_call | solution.py:223
  193.6 2.2 collective-permute-start.48
  195.8 4.1 %collective-permute-done.35 = bf16[512,384]{1,0:T(8,128)(2,1)S(1)} collective-permute-done((bf16[512,384]{1,0:T(8,128)(2,1)S(1)}, bf16[512,384]{1,0:T(8,128)(2,1)S(1)}, u32[]{:S(2)}, u32[]{:S(2)}) %collective-permute-start.35) | collective-permute-done | bytes 393248 | tf_op jit(solution)/shard_map/ppermute | solution.py:51
  200.3 9.2 %collective-permute-done.37.refs_16_.refs_1_ = bf16[1536,384]{1,0:T(8,128)(2,1)S(1)} collective-permute-done((bf16[1536,384]{1,0:T(8,128)(2,1)S(1)}, bf16[1536,384]{1,0:T(8,128)(2,1)S(1)}, u32[]{:S(2)}, u32[]{:S(2)}) %collective-permute-start.37) | collective-permute-done | bytes 1179680 | tf_op jit(solution)/shard_map/ppermute | solution.py:64
  212.6 4.2 %collective-permute-start.49 = (bf16[960,384]{1,0:T(8,128)(2,1)S(1)}, bf16[960,384]{1,0:T(8,128)(2,1)S(1)}, u32[]{:S(2)}, u32[]{:S(2)}) collective-permute-start(bf16[960,384]{1,0:T(8,128)(2,1)S(1)} %shard_map.208), channel_id=1, source_target_pairs={{0,16},{4,20},{8,24},{12,28},{16,0},{20,4},{24,8},{28,12},{1,17},{... | collective-permute-start | bytes 2211848 | tf_op jit(solution)/shard_map/ppermute | solution.py:64
  218.5 8.2 %shard_map.206 = (bf16[4,512,384]{2,1,0:T(8,128)(2,1)S(1)}, f32[512,1]{1,0:T(8,128)S(1)}, bf16[192,512]{1,0:T(8,128)(2,1)S(1)}, f32[192,512]{1,0:T(8,128)S(1)}, ...) custom-call(s32[11]{0:T(128)S(1)} %concatenate.6.table_ref, ...), custom_call_target="tpu_custom_call" | custom-call | tf_op jit(solution)/shard_map/pallas_call | solution.py:223
  232.9 5.6 %collective-permute-done.48.refs_15_.refs_1_ = bf16[1536,384]{1,0:T(8,128)(2,1)S(1)} collective-permute-done((bf16[1536,384]{1,0:T(8,128)(2,1)S(1)}, bf16[1536,384]{1,0:T(8,128)(2,1)S(1)}, u32[]{:S(2)}, u32[]{:S(2)}) %collective-permute-start.48) | collective-permute-done | bytes 1179680 | tf_op jit(solution)/shard_map/ppermute | solution.py:64
  240.7 25.6 %collective-permute-done.46.refs_6_ = bf16[192,512]{1,0:T(8,128)(2,1)S(1)} collective-permute-done((bf16[192,512]{1,0:T(8,128)(2,1)S(1)}, bf16[192,512]{1,0:T(8,128)(2,1)S(1)}, u32[]{:S(2)}, u32[]{:S(2)}) %collective-permute-start.46) | collective-permute-done | bytes 196640 | tf_op jit(solution)/shard_map/ppermute | solution.py:64
  266.3 4.5 %shard_map.209 = (bf16[576,384]{1,0:T(8,128)(2,1)S(1)}, bf16[576,384]{1,0:T(8,128)(2,1)}, bf16[576,384]{1,0:T(8,128)(2,1)S(1)}, bf16[576,384]{1,0:T(8,128)(2,1)S...) custom-call(s32[11]{0:T(128)S(1)} %concatenate.6.table_ref, ...), custom_call_target="tpu_custom_call", output_to_operand_aliasing={{0}: (1, {}), {1}: (2, {}), {2}: (3, {}), {3}: (4, {})} | custom-call | tf_op jit(solution)/shard_map/pallas_call | solution.py:223
  302.8 2.6 collective-permute-done.55
  305.4 2.7 fusion.6
  312.1 8.9 %collective-permute-start.63 = (bf16[576,384]{1,0:T(8,128)(2,1)S(1)}, bf16[576,384]{1,0:T(8,128)(2,1)S(1)}, u32[]{:S(2)}, u32[]{:S(2)}) collective-permute-start(bf16[576,384]{1,0:T(8,128)(2,1)S(1)} %copy-done.31), channel_id=1, source_target_pairs={{0,16},{4,20},{8,24},{12,28},{16,0},{20,4},{24,8},{28,12},{1,17},{... | collective-permute-start | bytes 1327112 | tf_op jit(solution)/shard_map/ppermute | solution.py:64
  324.9 7.2 %collective-permute-done.63.refs_3_ = bf16[576,384]{1,0:T(8,128)(2,1)S(1)} collective-permute-done((bf16[576,384]{1,0:T(8,128)(2,1)S(1)}, bf16[576,384]{1,0:T(8,128)(2,1)S(1)}, u32[]{:S(2)}, u32[]{:S(2)}) %collective-permute-start.63) | collective-permute-done | bytes 442400 | tf_op jit(solution)/shard_map/ppermute | solution.py:64
  339.0 2.7 shard_map.215
  (293 shorter events, 119.7 us)
Async XLA Ops:
  15.4 22.9 %collective-permute-start.13 = (bf16[576,384]{1,0:T(8,128)(2,1)S(1)}, bf16[576,384]{1,0:T(8,128)(2,1)S(1)}, u32[]{:S(2)}, u32[]{:S(2)}) collective-permute-start(bf16[576,384]{1,0:T(8,128)(2,1)S(1)} %shard_map.195.refs_3_), channel_id=1, source_target_pairs={{0,16},{4,20},{8,24},{12,28},{16,0},{20,4},{24,8},{28,12},{1,17},{... | collective-permute-start | bytes 1327112 | tf_op jit(solution)/shard_map/ppermute | solution.py:64
  20.1 21.1 %collective-permute-start.2 = (bf16[768,384]{1,0:T(8,128)(2,1)S(1)}, bf16[768,384]{1,0:T(8,128)(2,1)S(1)}, u32[]{:S(2)}, u32[]{:S(2)}) collective-permute-start(bf16[768,384]{1,0:T(8,128)(2,1)S(1)} %get-tuple-element.106), channel_id=1, source_target_pairs={{0,4},{4,0},{8,12},{12,8},{16,20},{20,16},{24,28},{28,24},{1,5},{5... | collective-permute-start | bytes 1769480 | tf_op jit(solution)/shard_map/ppermute | solution.py:51
  21.7 20.5 %collective-permute-start.12 = (bf16[576,384]{1,0:T(8,128)(2,1)S(1)}, bf16[576,384]{1,0:T(8,128)(2,1)S(1)}, u32[]{:S(2)}, u32[]{:S(2)}) collective-permute-start(bf16[576,384]{1,0:T(8,128)(2,1)S(1)} %shard_map.195.refs_3_), channel_id=1, source_target_pairs={{0,8},{4,12},{8,0},{12,4},{16,24},{20,28},{24,16},{28,20},{1,9},{5... | collective-permute-start | bytes 1327112 | tf_op jit(solution)/shard_map/ppermute | solution.py:64
  23.3 18.9 %collective-permute-start.14 = (bf16[576,384]{1,0:T(8,128)(2,1)S(1)}, bf16[576,384]{1,0:T(8,128)(2,1)S(1)}, u32[]{:S(2)}, u32[]{:S(2)}) collective-permute-start(bf16[576,384]{1,0:T(8,128)(2,1)S(1)} %shard_map.195.refs_3_), channel_id=1, source_target_pairs={{8,16},{12,20},{16,8},{20,12},{9,17},{13,21},{17,9},{21,13},{10,18... | collective-permute-start | bytes 1327112 | tf_op jit(solution)/shard_map/ppermute | solution.py:64
  38.3 12.2 %collective-permute-start.15 = (bf16[576,384]{1,0:T(8,128)(2,1)S(1)}, bf16[576,384]{1,0:T(8,128)(2,1)S(1)}, u32[]{:S(2)}, u32[]{:S(2)}) collective-permute-start(bf16[576,384]{1,0:T(8,128)(2,1)S(1)} %collective-permute-done.13.refs_5_), channel_id=1, source_target_pairs={{8,0},{12,4},{16,24},{20,28},{9,1},{13,5},{17,25},{21,29},{10,2},{... | collective-permute-start | bytes 1327112 | tf_op jit(solution)/shard_map/ppermute | solution.py:64
  39.6 19.2 %collective-permute-start.1 = (bf16[512,384]{1,0:T(8,128)(2,1)S(1)}, bf16[512,384]{1,0:T(8,128)(2,1)S(1)}, u32[]{:S(2)}, u32[]{:S(2)}) collective-permute-start(bf16[512,384]{1,0:T(8,128)(2,1)S(1)} %pad_maximum_fusion.refs_0_), channel_id=1, source_target_pairs={{0,2},{1,3},{2,0},{3,1},{4,6},{5,7},{6,4},{7,5},{8,10},{9,11},{10,... | collective-permute-start | bytes 1179656 | tf_op jit(solution)/shard_map/ppermute | solution.py:57
  50.5 60.4 %collective-permute-start.19 = (bf16[1536,384]{1,0:T(8,128)(2,1)S(1)}, bf16[1536,384]{1,0:T(8,128)(2,1)S(1)}, u32[]{:S(2)}, u32[]{:S(2)}) collective-permute-start(bf16[1536,384]{1,0:T(8,128)(2,1)S(1)} %shard_map.199.refs_2_), channel_id=1, source_target_pairs={{0,8},{4,12},{8,0},{12,4},{16,24},{20,28},{24,16},{28,20},{1,9},{5... | collective-permute-start | bytes 3538952 | tf_op jit(solution)/shard_map/ppermute | solution.py:64
  50.5 60.4 %collective-permute-start.20 = (bf16[1536,384]{1,0:T(8,128)(2,1)S(1)}, bf16[1536,384]{1,0:T(8,128)(2,1)S(1)}, u32[]{:S(2)}, u32[]{:S(2)}) collective-permute-start(bf16[1536,384]{1,0:T(8,128)(2,1)S(1)} %shard_map.199.refs_2_), channel_id=1, source_target_pairs={{0,16},{4,20},{8,24},{12,28},{16,0},{20,4},{24,8},{28,12},{1,17},{... | collective-permute-start | bytes 3538952 | tf_op jit(solution)/shard_map/ppermute | solution.py:64
  59.3 12.0 %collective-permute-start.3 = (bf16[512,384]{1,0:T(8,128)(2,1)S(1)}, bf16[512,384]{1,0:T(8,128)(2,1)S(1)}, u32[]{:S(2)}, u32[]{:S(2)}) collective-permute-start(bf16[512,384]{1,0:T(8,128)(2,1)S(1)} %pad_maximum_fusion.refs_0_), channel_id=1, source_target_pairs={{0,4},{4,0},{8,12},{12,8},{16,20},{20,16},{24,28},{28,24},{1,5},{5... | collective-permute-start | bytes 1179656 | tf_op jit(solution)/shard_map/ppermute | solution.py:51
  60.8 18.0 %collective-permute-start.4 = (bf16[512,384]{1,0:T(8,128)(2,1)S(1)}, bf16[512,384]{1,0:T(8,128)(2,1)S(1)}, u32[]{:S(2)}, u32[]{:S(2)}) collective-permute-start(bf16[512,384]{1,0:T(8,128)(2,1)S(1)} %collective-permute-done.1.refs_1_), channel_id=1, source_target_pairs={{0,4},{4,0},{8,12},{12,8},{16,20},{20,16},{24,28},{28,24},{1,5},{5... | collective-permute-start | bytes 1179656 | tf_op jit(solution)/shard_map/ppermute | solution.py:51
  61.5 17.9 %collective-permute-start.6 = (bf16[512,384]{1,0:T(8,128)(2,1)S(1)}, bf16[512,384]{1,0:T(8,128)(2,1)S(1)}, u32[]{:S(2)}, u32[]{:S(2)}) collective-permute-start(bf16[512,384]{1,0:T(8,128)(2,1)S(1)} %collective-permute-done.1.refs_1_), channel_id=1, source_target_pairs={{0,1},{1,0},{2,3},{3,2},{4,5},{5,4},{6,7},{7,6},{8,9},{9,8},{10,11... | collective-permute-start | bytes 1179656 | tf_op jit(solution)/shard_map/ppermute | solution.py:60
  86.3 20.1 %collective-permute-start.16 = (bf16[192,512]{1,0:T(8,128)(2,1)S(1)}, bf16[192,512]{1,0:T(8,128)(2,1)S(1)}, u32[]{:S(2)}, u32[]{:S(2)}) collective-permute-start(bf16[192,512]{1,0:T(8,128)(2,1)S(1)} %get-tuple-element.111.refs_1_.refs_10_.refs_13_), channel_id=1, source_target_pairs={{0,8},{4,12},{8,16},{12,20},{1,9},{5,13},{9,17},{13,21},{2,10},{6,... | collective-permute-start | bytes 589832 | tf_op jit(solution)/shard_map/ppermute | solution.py:64
  88.2 20.5 %collective-permute-start.17 = (bf16[192,512]{1,0:T(8,128)(2,1)S(1)}, bf16[192,512]{1,0:T(8,128)(2,1)S(1)}, u32[]{:S(2)}, u32[]{:S(2)}) collective-permute-start(bf16[192,512]{1,0:T(8,128)(2,1)S(1)} %get-tuple-element.111.refs_1_.refs_10_.refs_13_), channel_id=1, source_target_pairs={{0,16},{4,20},{8,24},{12,28},{1,17},{5,21},{9,25},{13,29},{2,18},{... | collective-permute-start | bytes 589832 | tf_op jit(solution)/shard_map/ppermute | solution.py:64
  89.6 21.3 %collective-permute-start.18 = (bf16[192,512]{1,0:T(8,128)(2,1)S(1)}, bf16[192,512]{1,0:T(8,128)(2,1)S(1)}, u32[]{:S(2)}, u32[]{:S(2)}) collective-permute-start(bf16[192,512]{1,0:T(8,128)(2,1)S(1)} %get-tuple-element.111.refs_1_.refs_10_.refs_13_), channel_id=1, source_target_pairs={{0,24},{4,28},{1,25},{5,29},{2,26},{6,30},{3,27},{7,31}} | collective-permute-start | bytes 589832 | tf_op jit(solution)/shard_map/ppermute | solution.py:64
  121.4 20.9 %collective-permute-start.27 = (bf16[1536,384]{1,0:T(8,128)(2,1)S(1)}, bf16[1536,384]{1,0:T(8,128)(2,1)S(1)}, u32[]{:S(2)}, u32[]{:S(2)}) collective-permute-start(bf16[1536,384]{1,0:T(8,128)(2,1)S(1)} %shard_map.199.refs_2_), channel_id=1, source_target_pairs={{8,16},{12,20},{16,8},{20,12},{9,17},{13,21},{17,9},{21,13},{10,18... | collective-permute-start | bytes 3538952 | tf_op jit(solution)/shard_map/ppermute | solution.py:64
  122.1 39.3 %collective-permute-start.28 = (bf16[1536,384]{1,0:T(8,128)(2,1)S(1)}, bf16[1536,384]{1,0:T(8,128)(2,1)S(1)}, u32[]{:S(2)}, u32[]{:S(2)}) collective-permute-start(bf16[1536,384]{1,0:T(8,128)(2,1)S(1)} %collective-permute-done.20.refs_7_.refs_4_), channel_id=1, source_target_pairs={{8,0},{12,4},{16,24},{20,28},{9,1},{13,5},{17,25},{21,29},{10,2},{... | collective-permute-start | bytes 3538952 | tf_op jit(solution)/shard_map/ppermute | solution.py:64
  180.8 28.7 %collective-permute-start.37 = (bf16[1536,384]{1,0:T(8,128)(2,1)S(1)}, bf16[1536,384]{1,0:T(8,128)(2,1)S(1)}, u32[]{:S(2)}, u32[]{:S(2)}) collective-permute-start(bf16[1536,384]{1,0:T(8,128)(2,1)S(1)} %get-tuple-element.147), channel_id=1, source_target_pairs={{0,8},{4,12},{24,16},{28,20},{1,9},{5,13},{25,17},{29,21},{2,10},{... | collective-permute-start | bytes 3538952 | tf_op jit(solution)/shard_map/ppermute | solution.py:64
  183.2 26.3 %collective-permute-start.38 = (bf16[1536,384]{1,0:T(8,128)(2,1)S(1)}, bf16[1536,384]{1,0:T(8,128)(2,1)S(1)}, u32[]{:S(2)}, u32[]{:S(2)}) collective-permute-start(bf16[1536,384]{1,0:T(8,128)(2,1)S(1)} %get-tuple-element.147), channel_id=1, source_target_pairs={{8,16},{12,20},{16,8},{20,12},{9,17},{13,21},{17,9},{21,13},{10,18... | collective-permute-start | bytes 3538952 | tf_op jit(solution)/shard_map/ppermute | solution.py:64
  193.6 44.9 %collective-permute-start.48 = (bf16[1536,384]{1,0:T(8,128)(2,1)S(1)}, bf16[1536,384]{1,0:T(8,128)(2,1)S(1)}, u32[]{:S(2)}, u32[]{:S(2)}) collective-permute-start(bf16[1536,384]{1,0:T(8,128)(2,1)S(1)} %get-tuple-element.171), channel_id=1, source_target_pairs={{0,8},{4,12},{8,0},{12,4},{16,24},{20,28},{24,16},{28,20},{1,9},{5... | collective-permute-start | bytes 3538952 | tf_op jit(solution)/shard_map/ppermute | solution.py:64
  212.6 53.7 %collective-permute-start.49 = (bf16[960,384]{1,0:T(8,128)(2,1)S(1)}, bf16[960,384]{1,0:T(8,128)(2,1)S(1)}, u32[]{:S(2)}, u32[]{:S(2)}) collective-permute-start(bf16[960,384]{1,0:T(8,128)(2,1)S(1)} %shard_map.208), channel_id=1, source_target_pairs={{0,16},{4,20},{8,24},{12,28},{16,0},{20,4},{24,8},{28,12},{1,17},{... | collective-permute-start | bytes 2211848 | tf_op jit(solution)/shard_map/ppermute | solution.py:64
  226.8 13.9 %collective-permute-start.45 = (bf16[192,512]{1,0:T(8,128)(2,1)S(1)}, bf16[192,512]{1,0:T(8,128)(2,1)S(1)}, u32[]{:S(2)}, u32[]{:S(2)}) collective-permute-start(bf16[192,512]{1,0:T(8,128)(2,1)S(1)} %get-tuple-element.167), channel_id=1, source_target_pairs={{8,0},{12,4},{16,8},{20,12},{9,1},{13,5},{17,9},{21,13},{10,2},{14... | collective-permute-start | bytes 589832 | tf_op jit(solution)/shard_map/ppermute | solution.py:64
  228.1 38.2 %collective-permute-start.46 = (bf16[192,512]{1,0:T(8,128)(2,1)S(1)}, bf16[192,512]{1,0:T(8,128)(2,1)S(1)}, u32[]{:S(2)}, u32[]{:S(2)}) collective-permute-start(bf16[192,512]{1,0:T(8,128)(2,1)S(1)} %get-tuple-element.168), channel_id=1, source_target_pairs={{16,0},{20,4},{24,8},{28,12},{17,1},{21,5},{25,9},{29,13},{18,2},{... | collective-permute-start | bytes 589832 | tf_op jit(solution)/shard_map/ppermute | solution.py:64
  229.4 36.9 %collective-permute-start.47 = (bf16[192,512]{1,0:T(8,128)(2,1)S(1)}, bf16[192,512]{1,0:T(8,128)(2,1)S(1)}, u32[]{:S(2)}, u32[]{:S(2)}) collective-permute-start(bf16[192,512]{1,0:T(8,128)(2,1)S(1)} %get-tuple-element.169), channel_id=1, source_target_pairs={{24,0},{28,4},{25,1},{29,5},{26,2},{30,6},{27,3},{31,7}} | collective-permute-start | bytes 589832 | tf_op jit(solution)/shard_map/ppermute | solution.py:64
  279.4 14.8 %collective-permute-start.53 = (bf16[576,384]{1,0:T(8,128)(2,1)S(1)}, bf16[576,384]{1,0:T(8,128)(2,1)S(1)}, u32[]{:S(2)}, u32[]{:S(2)}) collective-permute-start(bf16[576,384]{1,0:T(8,128)(2,1)S(1)} %copy-done.33), channel_id=1, source_target_pairs={{0,8},{4,12},{24,16},{28,20},{1,9},{5,13},{25,17},{29,21},{2,10},{... | collective-permute-start | bytes 1327112 | tf_op jit(solution)/shard_map/ppermute | solution.py:64
  280.7 15.0 %collective-permute-start.54 = (bf16[576,384]{1,0:T(8,128)(2,1)S(1)}, bf16[576,384]{1,0:T(8,128)(2,1)S(1)}, u32[]{:S(2)}, u32[]{:S(2)}) collective-permute-start(bf16[576,384]{1,0:T(8,128)(2,1)S(1)} %copy-done.33), channel_id=1, source_target_pairs={{8,16},{12,20},{16,8},{20,12},{9,17},{13,21},{17,9},{21,13},{10,18... | collective-permute-start | bytes 1327112 | tf_op jit(solution)/shard_map/ppermute | solution.py:64
  289.3 31.8 %collective-permute-start.65 = (bf16[576,384]{1,0:T(8,128)(2,1)}, bf16[576,384]{1,0:T(8,128)(2,1)S(1)}, u32[]{:S(2)}, u32[]{:S(2)}) collective-permute-start(bf16[576,384]{1,0:T(8,128)(2,1)} %shard_map.213), channel_id=1, source_target_pairs={{0,16},{4,20},{8,24},{12,28},{16,0},{20,4},{24,8},{28,12},{1,17},{... | collective-permute-start | bytes 1327112 | tf_op jit(solution)/shard_map/ppermute | solution.py:64
  293.7 17.2 %collective-permute-start.43 = (bf16[512,384]{1,0:T(8,128)(2,1)}, bf16[512,384]{1,0:T(8,128)(2,1)}, u32[]{:S(2)}, u32[]{:S(2)}) collective-permute-start(bf16[512,384]{1,0:T(8,128)(2,1)} %broadcast_select_fusion.2), channel_id=1, source_target_pairs={{0,2},{1,3},{2,0},{3,1},{4,6},{5,7},{6,4},{7,5},{8,10},{9,11},{10,... | collective-permute-start | bytes 1179656 | tf_op jit(solution)/shard_map/ppermute | solution.py:57
  294.2 30.7 %collective-permute-start.62 = (bf16[576,384]{1,0:T(8,128)(2,1)}, bf16[576,384]{1,0:T(8,128)(2,1)S(1)}, u32[]{:S(2)}, u32[]{:S(2)}) collective-permute-start(bf16[576,384]{1,0:T(8,128)(2,1)} %get-tuple-element.182), channel_id=1, source_target_pairs={{0,8},{4,12},{8,0},{12,4},{16,24},{20,28},{24,16},{28,20},{1,9},{5... | collective-permute-start | bytes 1327112 | tf_op jit(solution)/shard_map/ppermute | solution.py:64
  309.2 14.0 %collective-permute-start.59 = (f32[2,384]{1,0:T(2,128)S(1)}, f32[2,384]{1,0:T(2,128)S(1)}, u32[]{:S(2)}, u32[]{:S(2)}) collective-permute-start(f32[2,384]{1,0:T(2,128)S(1)} %pad_maximum_fusion.2), channel_id=1, source_target_pairs={{0,4},{4,0},{8,12},{12,8},{16,20},{20,16},{24,28},{28,24},{1,5},{5... | collective-permute-start | bytes 9224 | tf_op jit(solution)/shard_map/ppermute | solution.py:51
  312.1 20.0 %collective-permute-start.63 = (bf16[576,384]{1,0:T(8,128)(2,1)S(1)}, bf16[576,384]{1,0:T(8,128)(2,1)S(1)}, u32[]{:S(2)}, u32[]{:S(2)}) collective-permute-start(bf16[576,384]{1,0:T(8,128)(2,1)S(1)} %copy-done.31), channel_id=1, source_target_pairs={{0,16},{4,20},{8,24},{12,28},{16,0},{20,4},{24,8},{28,12},{1,17},{... | collective-permute-start | bytes 1327112 | tf_op jit(solution)/shard_map/ppermute | solution.py:64
  322.6 16.3 %collective-permute-start.66 = (bf16[768,384]{1,0:T(8,128)(2,1)S(1)}, bf16[768,384]{1,0:T(8,128)(2,1)S(1)}, u32[]{:S(2)}, u32[]{:S(2)}) collective-permute-start(bf16[768,384]{1,0:T(8,128)(2,1)S(1)} %get-tuple-element.191), channel_id=1, source_target_pairs={{0,4},{4,0},{8,12},{12,8},{16,20},{20,16},{24,28},{28,24},{1,5},{5... | collective-permute-start | bytes 1769480 | tf_op jit(solution)/shard_map/ppermute | solution.py:51
  323.4 12.5 %collective-permute-start.44 = (bf16[256,384]{1,0:T(8,128)(2,1)S(1)}, bf16[256,384]{1,0:T(8,128)(2,1)S(1)}, u32[]{:S(2)}, u32[]{:S(2)}) collective-permute-start(bf16[256,384]{1,0:T(8,128)(2,1)S(1)} %broadcast_select_fusion.5), channel_id=1, source_target_pairs={{0,4},{4,0},{8,12},{12,8},{16,20},{20,16},{24,28},{28,24},{1,5},{5... | collective-permute-start | bytes 589832 | tf_op jit(solution)/shard_map/ppermute | solution.py:51
  (95 other events, 828.5 us)
